TPU v7x, 128 devices: a whole 4x4x4 slice. The times are simulated.
128 devices in a mesh: pb: 8 (over z, core), pa: 16 (over y, x).
Axes of the slice: x: 4, y: 4, z: 4, core: 2. Of those that a mesh axis runs over, the one named last changes fastest.
Arguments:
- queries: bfloat16 [16384, 3584], P(('pb', 'pa')), may hold values from -16 to 16
- passages: bfloat16 [65536, 3584], P(('pb', 'pa')), may hold values from -16 to 16
- hard_block_offsets: int32 [4096, 4], P(('pb', 'pa')), may hold values from 0 to 126, all different within a row; in each aligned block of 32 rows (0 to 31, 32 to 63, ...) at most 2 rows name the same one
- positive: int32 [16384], P(('pb', 'pa')), may hold values from 0 to 511
- context: bfloat16 [65536, 3584], P(('pb', 'pa')), may hold values from -24 to 24
- residual: bfloat16 [65536, 3584], P(('pb', 'pa')), may hold values from -6 to 6
- output_weight: bfloat16 [3584, 3584], P(('pb', 'pa')), may hold values from -0.09375 to 0.09375
- adapter_down_weight: bfloat16 [3584, 16], replicated, may hold values from -0.09375 to 0.09375
- adapter_up_weight: bfloat16 [16, 3584], replicated, may hold values from -1.5 to 1.5
- final_norm_weight: bfloat16 [3584], replicated, may hold values from 0.099609375 to 1.8984375
Outputs:
- query_gradient: float32 [16384, 3584], P(('pb', 'pa'))
- grad_passages: float32 [65536, 3584], P(('pb', 'pa'))
- grad_lora_down: float32 [3584, 16], P(('pb', 'pa'))
- grad_lora_up: float32 [16, 3584], P(None, ('pb', 'pa'))
Inputs may be any that keep to these rules, and one draw needn't show every extreme that they name: `hard_block_offsets`: each row lists 4 different offsets. Query block k is paired with passage block (k // 32 + 1 + offset) modulo the number of devices. In each aligned block of 32 rows no offset appears more than 2 times, and some offset appears exactly 2 times.
All inputs are finite; a program needn't handle non-finite values.
Results may differ from a plain program's by a relative error of at most 0.0045.
Values may be sent and summed in bfloat16 or wider, within the bound.
A program may use at most 192 MiB of HBM per device.

v0:
```python
import math

import jax
import jax.numpy as jnp
from jax import lax
from jax.sharding import Mesh
from jax.sharding import PartitionSpec as P

MODEL_WIDTH = 3584
RERUN_QUERIES = 16
TQ = 32
PB_PA = ("pb_0", "pb_1", "pa_0", "pa_1")
CHIPS = ("pb_0", "pa_0", "pa_1")

inverse_temp = 2.0
loss_scale = 32.0
adapter_scale = 2.0
epsilon = 1e-06
absent_mass = 1e30
f32 = jnp.float32
bf16 = jnp.bfloat16


def dot(a, b, **kw):
    return jnp.dot(a, b, preferred_element_type=f32, **kw)


def two_parts(x):
    high = x.astype(bf16)
    return high, (x - high.astype(f32)).astype(bf16)


def device_of(chip, core, per_plane):
    return (chip // per_plane) * 2 * per_plane + core * per_plane + chip % per_plane


def gathered_weight_input(rows):
    count = lax.axis_size(PB_PA)
    per_plane = lax.axis_size("pa_0") * lax.axis_size("pa_1")
    half = rows.shape[1] // 2
    left, right = rows[:, :half], rows[:, half:]
    odd = lax.axis_index("pa_1") % 2 == 1
    core = lax.axis_index("pb_1")
    same = [(f, device_of(f // 2, f % 2, per_plane)) for f in range(count)]
    other = [(f, device_of(f // 2, 1 - f % 2, per_plane)) for f in range(count)]
    first = lax.ppermute(jnp.where(odd, right, left), PB_PA, same)
    second = lax.ppermute(jnp.where(odd, left, right), PB_PA, other)
    low = jnp.where(core == 0, first, second)
    high = jnp.where(core == 0, second, first)
    return jnp.concatenate([low, high], axis=0)


def exchange(array):
    return lax.all_to_all(array, PB_PA, split_axis=0, concat_axis=0, tiled=True)


def local(
    queries,
    passages,
    hard_block_offsets,
    positive,
    context,
    residual,
    output_weight,
    adapter_down_weight,
    adapter_up_weight,
    final_norm_weight,
):
    device_count = lax.axis_size(PB_PA)
    block_count, hard_count = hard_block_offsets.shape
    query_count = queries.shape[0]
    block_rows = query_count // block_count
    capacity = 2 * block_count * hard_count // device_count
    slot_rows = capacity * block_rows
    all_rows = device_count * slot_rows
    passage_count = passages.shape[0]
    score_scale = inverse_temp / math.sqrt(MODEL_WIDTH)

    weight_rows = gathered_weight_input(output_weight)

    source = lax.axis_index(PB_PA)
    target = ((source + 1 + hard_block_offsets) % device_count).reshape(-1)
    order = jnp.arange(target.shape[0], dtype=jnp.int32)
    earlier = (target[:, None] == target[None, :]) & (order[:, None] > order[None, :])
    slot = target * capacity + jnp.sum(earlier.astype(jnp.int32), axis=1)
    slot_of = slot.reshape(block_count, hard_count).T
    key = jnp.repeat(slot_of, block_rows, axis=1) * block_rows + (
        jnp.arange(query_count, dtype=jnp.int32) % block_rows
    )
    row_ids = jnp.arange(all_rows, dtype=jnp.int32)
    picks = row_ids[:, None] == key[0][None, :]
    for t in range(1, hard_count):
        picks = picks | (row_ids[:, None] == key[t][None, :])
    outgoing = jnp.dot(picks.astype(bf16), queries, preferred_element_type=bf16)
    arrived = exchange(outgoing.reshape(device_count, slot_rows, MODEL_WIDTH))
    arrived = arrived.reshape(-1, MODEL_WIDTH)

    half_weight = lax.all_gather(weight_rows, CHIPS, axis=0, tiled=True)
    near_scores = dot(queries, passages.T) * score_scale
    near_peak = jnp.max(near_scores, axis=1)
    near_exp = jnp.exp(near_scores - near_peak[:, None])
    near_sum = jnp.sum(near_exp, axis=1)
    near_mass = near_peak + jnp.log(near_sum)
    positive_hot = positive[:, None] == jnp.arange(passage_count, dtype=jnp.int32)[None, :]
    stacked = dot(
        jnp.concatenate([near_exp.astype(bf16), positive_hot.astype(bf16)], axis=0), passages
    )

    far_scores = dot(arrived, passages.T) * score_scale
    far_peak = jnp.max(far_scores, axis=1)
    far_exp = jnp.exp(far_scores - far_peak[:, None])
    far_sum = jnp.sum(far_exp, axis=1)
    far_mass = far_peak + jnp.log(far_sum)
    far_mean = (dot(far_exp.astype(bf16), passages) / far_sum[:, None]).astype(bf16)
    returned = exchange(far_mean.reshape(device_count, slot_rows, MODEL_WIDTH))
    returned = returned.reshape(-1, MODEL_WIDTH)
    far_mass, _ = lax.optimization_barrier((far_mass, far_mean))
    returned_mass = exchange(far_mass.reshape(device_count, slot_rows)).reshape(-1)
    half_weight, returned_mass = lax.optimization_barrier((half_weight, returned_mass))
    both_halves = lax.all_gather(half_weight, "pb_1", axis=0, tiled=False)

    hits = [key[t][:, None] == row_ids[None, :] for t in range(hard_count)]
    masses = [near_mass] + [
        jnp.sum(jnp.where(hit, returned_mass[None, :], 0.0), axis=1) for hit in hits
    ]
    peak = masses[0]
    for mass in masses[1:]:
        peak = jnp.maximum(peak, mass)
    total = jnp.exp(masses[0] - peak)
    for mass in masses[1:]:
        total = total + jnp.exp(mass - peak)
    log_total = peak + jnp.log(total)

    filled = jnp.any(picks, axis=1)
    log_outgoing = jnp.where(
        filled, jnp.sum(jnp.where(picks, log_total[None, :], 0.0), axis=1), absent_mass
    )
    log_arrived = exchange(log_outgoing.reshape(device_count, slot_rows)).reshape(-1)

    mix = jnp.zeros((query_count, all_rows), f32)
    for t in range(hard_count):
        mix = jnp.where(hits[t], jnp.exp(masses[1 + t] - log_total)[:, None], mix)
    mix_parts = jnp.concatenate(two_parts(mix), axis=0)
    near_share = jnp.exp(near_mass - log_total)
    near_part = (near_share / near_sum)[:, None] * stacked[:query_count] - stacked[query_count:]

    product_dims = (((0,), (0,)), ((), ()))
    far_weight = jnp.exp(far_scores - log_arrived[:, None]).astype(bf16)
    near_weight = (
        jnp.exp(near_scores - log_total[:, None]) - positive_hot.astype(f32)
    ).astype(bf16)
    far_grad = lax.dot_general(far_weight, arrived, product_dims, preferred_element_type=f32)
    near_grad = lax.dot_general(near_weight, queries, product_dims, preferred_element_type=f32)
    grad_passages = loss_scale * score_scale * (far_grad + near_grad)

    narrow = dot(context, adapter_down_weight).astype(bf16)
    frozen = jnp.concatenate([dot(context, both_halves[0]), dot(context, both_halves[1])], axis=1)
    hidden = residual.astype(f32) + frozen + adapter_scale * dot(narrow, adapter_up_weight)
    inverse_rms = lax.rsqrt(jnp.mean(hidden * hidden, axis=1, keepdims=True) + epsilon)
    hidden_low = hidden.astype(bf16)
    hidden_up = dot(hidden_low, adapter_up_weight.T)
    token_query = jnp.arange(context.shape[0], dtype=jnp.int32) // TQ
    of_query = token_query[:, None] == jnp.arange(RERUN_QUERIES, dtype=jnp.int32)[None, :]
    narrow_sums = jnp.sum(
        (inverse_rms * narrow.astype(f32)).reshape(RERUN_QUERIES, TQ, -1), axis=1
    )

    returned, hidden_low, hidden_up, inverse_rms, narrow_sums = lax.optimization_barrier(
        (returned, hidden_low, hidden_up, inverse_rms, narrow_sums)
    )
    far_part = dot(mix_parts, returned)
    query_gradient = (loss_scale * score_scale) * (
        far_part[:query_count] + far_part[query_count:] + near_part
    )

    scaled = final_norm_weight.astype(f32)[None, :] * (query_gradient[:RERUN_QUERIES] / TQ)
    products = dot(hidden_low, scaled.astype(bf16).T)
    mean = jnp.sum(jnp.where(of_query, products, 0.0), axis=1, keepdims=True) / MODEL_WIDTH
    slope = inverse_rms**3 * mean
    scaled_up = dot(scaled, adapter_up_weight.astype(f32).T, precision=lax.Precision.HIGHEST)
    spread_up = jnp.broadcast_to(
        scaled_up[:, None, :], (RERUN_QUERIES, TQ, scaled_up.shape[1])
    ).reshape(context.shape[0], -1)
    grad_narrow = (adapter_scale * (inverse_rms * spread_up - slope * hidden_up)).astype(bf16)
    down_term = lax.dot_general(grad_narrow, context, product_dims, preferred_element_type=f32)
    weighted = (slope * narrow.astype(f32)).astype(bf16)
    up_term = adapter_scale * (
        lax.dot_general(
            narrow_sums,
            scaled,
            product_dims,
            precision=lax.Precision.HIGHEST,
            preferred_element_type=f32,
        )
        - lax.dot_general(weighted, hidden_low, product_dims, preferred_element_type=f32)
    )
    terms = jnp.concatenate([down_term, up_term], axis=0) / RERUN_QUERIES
    rank = narrow.shape[1]
    columns = MODEL_WIDTH // device_count
    pieces = jnp.transpose(terms.reshape(2 * rank, device_count, columns), (1, 0, 2))
    sums = jnp.sum(exchange(pieces.reshape(device_count, -1)), axis=0).reshape(2 * rank, columns)
    return (query_gradient, grad_passages, sums[:rank].T, sums[rank:])


def solution(mesh):
    torus = Mesh(mesh.devices.reshape(4, 2, 4, 4), PB_PA)
    in_specs = (
        P(PB_PA, None),
        P(PB_PA, None),
        P(PB_PA, None),
        P(PB_PA),
        P(PB_PA, None),
        P(PB_PA, None),
        P(PB_PA, None),
        P(),
        P(),
        P(),
    )
    out_specs = (P(PB_PA, None), P(PB_PA, None), P(PB_PA, None), P(None, PB_PA))
    return jax.shard_map(local, mesh=torus, in_specs=in_specs, out_specs=out_specs, check_vma=False)
```

profile of v0, /device:TPU:1, one launch (start us, length us, event | category | flops | bytes accessed | tf_op | source)
XLA Modules:
  0.0 347.3 jit_solution(11407724801208197337)
XLA Ops:
  8.3 6.2 %collective-permute-start = (bf16[28,1792]{1,0:T(8,128)(2,1)S(1)}, bf16[28,1792]{1,0:T(8,128)(2,1)S(1)}, u32[]{:S(2)}, u32[]{:S(2)}) collective-permute-start(bf16[28,1792]{1,0:T(8,128)(2,1)S(1)} %get-tuple-element.32), channel_id=1, source_target_pairs={{0,0},{1,16},{2,1},{3,17},{4,2},{5,18},{6,3},{7,19},{8,4},{9,20},{... | collective-permute-start | bytes 301064 | tf_op jit(solution)/shard_map/ppermute | solution.py:46
  15.6 3.1 collective-permute-done
  18.7 1.2 collective-permute-done.1
  22.3 2.1 convolution_bitcast_fusion
  24.3 109.4 %all_to_all.34 = bf16[128,8,3584]{2,1,0:T(8,128)(2,1)S(1)} all-to-all(bf16[128,8,3584]{2,1,0:T(8,128)(2,1)S(1)} %convolution_bitcast_fusion), channel_id=1, replica_groups=mesh['pb_0'=4,'pb_1'=2,'pa_0'=4,'pa_1'=4] {'pb_0','pb_1','pa_0','pa_1'}, dimensions={0} | all-to-all | bytes 14680064 | tf_op jit(solution)/shard_map/all_to_all | solution.py:54
  133.8 4.0 %multiply_reduce_fusion.1 = (f32[1024]{0:T(1024)S(1)}, f32[1024,512]{0,1:T(8,128)S(1)}) fusion(bf16[512,3584]{1,0:T(8,128)(2,1)S(1)} %copy-done.2, bf16[128,8,3584]{2,1,0:T(8,128)(2,1)S(1)} %all_to_all.34), kind=kOutput, calls=%fused_computation.27 | convolution fusion | flops 3759143936 | bytes 13111296 | tf_op jit(solution)/shard_map/dot_general | solution.py:25
  139.1 6.1 %divide_convert_fusion = bf16[1024,3584]{1,0:T(8,128)(2,1)} fusion(f32[1024]{0:T(1024)S(1)} %fusion.17, bf16[512,3584]{1,0:T(8,128)(2,1)S(1)} %copy-done.2, f32[1024,512]{0,1:T(8,128)S(1)} %get-tuple-element.47, f32[1024]{0:T(1024)S(1)} %get-tuple-element.46), kind=kOutput, calls=%fused_computation | convolution fusion | flops 3767009280 | bytes 13115392 | tf_op jit(solution)/shard_map/dot_general | solution.py:25
  145.3 17.4 %all_to_all.35 = f32[128,1,8]{2,1,0:T(1,128)S(1)} all-to-all(f32[128,1,8]{2,1,0:T(1,128)S(1)} %bitcast.62), channel_id=1, replica_groups=mesh['pb_0'=4,'pb_1'=2,'pa_0'=4,'pa_1'=4] {'pb_0','pb_1','pa_0','pa_1'}, dimensions={0} | all-to-all | bytes 8192 | tf_op jit(solution)/shard_map/all_to_all | solution.py:54
  164.1 16.1 %all-gather.4.cloned.1.call-done = bf16[3584,1792]{1,0:T(8,128)(2,1)} async-done(((bf16[56,1792]{1,0:T(8,128)(2,1)}), bf16[3584,1792]{1,0:T(8,128)(2,1)}) %all-gather.4.cloned.1.call-update) | async-done | bytes 12845072 | tf_op jit(solution)/shard_map/all_gather | solution.py:98
  180.6 3.4 fusion.72
  185.0 17.2 %all_to_all.36 = f32[128,1,8]{2,1,0:T(1,128)S(1)} all-to-all(f32[128,1,8]{2,1,0:T(1,128)S(1)} %bitcast.63), channel_id=1, replica_groups=mesh['pb_0'=4,'pb_1'=2,'pa_0'=4,'pa_1'=4] {'pb_0','pb_1','pa_0','pa_1'}, dimensions={0} | all-to-all | bytes 8192 | tf_op jit(solution)/shard_map/all_to_all | solution.py:54
  202.3 5.9 %all-to-all-start.2 = ((bf16[128,8,3584]{2,1,0:T(8,128)(2,1)}), bf16[128,8,3584]{2,1,0:T(8,128)(2,1)}, u32[]{:S(2)}, u32[]{:S(2)}) async-start(bf16[128,8,3584]{2,1,0:T(8,128)(2,1)} %bitcast.61), calls=%async_computation.2 | async-start | bytes 14680064 | tf_op jit(solution)/shard_map/all_to_all | solution.py:54
  208.2 6.3 %copy.39 = bf16[512,3584]{0,1:T(8,128)(2,1)} copy(bf16[512,3584]{1,0:T(8,128)(2,1)} %param.15) | data formatting | bytes 7340032 | tf_op args[5]
  214.6 3.2 convolution_convert_fusion
  217.8 3.1 fusion.35
  222.5 10.6 %fusion.5 = f32[512,3584]{1,0:T(8,128)} fusion(bf16[128,8,3584]{2,1,0:T(8,128)(2,1)} %copy-done.6, f32[1024,512]{0,1:T(8,128)} %copy-done.9, f32[1024]{0:T(1024)S(1)} %sub.236), kind=kOutput, calls=%fused_computation.7 | convolution fusion | flops 3759669248 | bytes 16781312 | tf_op jit(solution)/shard_map/dot_general | solution.py:152
  233.1 12.7 %fusion.10 = f32[512,1792]{0,1:T(8,128)S(1)} fusion(bf16[512,3584]{1,0:T(8,128)(2,1)} %param.14, bf16[7168,1792]{1,0:T(8,128)(2,1)} %all-gather.6.cloned.1.call-done), kind=kOutput, calls=%fused_computation.16 | convolution fusion | flops 6576668672 | bytes 20185088 | tf_op jit(solution)/shard_map/dot_general | solution.py:25
  245.8 10.3 %fusion.13 = f32[512,1792]{0,1:T(8,128)S(1)} fusion(bf16[512,3584]{1,0:T(8,128)(2,1)S(1)} %copy-done.4, bf16[7168,1792]{1,0:T(8,128)(2,1)} %all-gather.6.cloned.1.call-done), kind=kOutput, calls=%fused_computation.17 | convolution fusion | flops 6576668672 | bytes 20185088 | tf_op jit(solution)/shard_map/dot_general | solution.py:25
  256.2 3.6 %multiply_reduce_fusion = (f32[512]{0:T(512)S(1)}, bf16[512,3584]{0,1:T(8,128)(2,1)}) fusion(bf16[512,16]{0,1:T(8,128)(2,1)S(1)} %convolution_convert_fusion, bf16[16,3584]{1,0:T(8,128)(2,1)S(1)} %copy-done.10, f32[512,1792]{0,1:T(8,128)S(1)} %fusion.13, f32[512,1792]{0,1:T(8,128)S(1)} %fusion.10, bf16[512,3584]{0,1:T(8,128)(2,1)S(1)} %copy-done.7), kind=kOutput, calls=%fused_computation.12 | convolution fusion | flops 73399808 | bytes 14813184 | tf_op jit(solution)/shard_map/dot_general | solution.py:25
  260.0 2.6 fusion.73
  262.6 32.0 %all-to-all-done.2 = bf16[128,8,3584]{2,1,0:T(8,128)(2,1)} async-done(((bf16[128,8,3584]{2,1,0:T(8,128)(2,1)}), bf16[128,8,3584]{2,1,0:T(8,128)(2,1)}, u32[]{:S(2)}, u32[]{:S(2)}) %all-to-all-start.2) | async-done | bytes 7340064 | tf_op jit(solution)/shard_map/all_to_all | solution.py:54
  294.6 5.3 %fusion.26 = f32[256,3584]{1,0:T(8,128)S(1)} fusion(bf16[1024,3584]{1,0:T(8,128)(2,1)} %bitcast.9, bf16[128,1024]{1,0:T(8,128)(2,1)S(1)} %subtract_convert_fusion, bf16[128,1024]{1,0:T(8,128)(2,1)S(1)} %fusion.30), kind=kOutput, calls=%fused_computation.36 | convolution fusion | flops 1880096768 | bytes 11534336 | tf_op jit(solution)/shard_map/dot_general | solution.py:25
  300.7 1.8 copy-done.1
  303.4 2.6 fusion.54
  306.0 1.3 concatenate.24
  307.7 1.3 fusion.42
  309.0 3.1 fusion.9
  312.1 1.3 concatenate.25
  314.1 1.3 copy.46
  315.4 10.0 %all-to-all-start.4 = ((f32[128,1,896]{2,1,0:T(1,128)}), f32[128,1,896]{2,1,0:T(1,128)S(1)}, u32[]{:S(2)}, u32[]{:S(2)}) async-start(f32[128,1,896]{2,1,0:T(1,128)} %copy.46), calls=%async_computation.4 | async-start | bytes 917504 | tf_op jit(solution)/shard_map/all_to_all | solution.py:54
  325.4 7.4 %add_multiply_fusion = f32[512,3584]{1,0:T(8,128)} fusion(f32[512,3584]{1,0:T(8,128)} %fusion.5, bf16[128,3584]{1,0:T(8,128)(2,1)S(1)} %copy-done, f32[128,512]{1,0:T(8,128)S(1)} %get-tuple-element.45, f32[128]{0:T(128)S(1)} %get-tuple-element.25, s32[128]{0:T(128)S(1)} %copy-done.13), kind=kOutput, calls=%fused_computation.11 | convolution fusion | flops 473759744 | bytes 15860736 | tf_op jit(solution)/shard_map/dot_general | solution.py:153
  332.8 5.9 %all-to-all-done.4 = f32[128,1,896]{2,1,0:T(1,128)S(1)} async-done(((f32[128,1,896]{2,1,0:T(1,128)}), f32[128,1,896]{2,1,0:T(1,128)S(1)}, u32[]{:S(2)}, u32[]{:S(2)}) %all-to-all-start.4) | async-done | bytes 458784 | tf_op jit(solution)/shard_map/all_to_all | solution.py:54
  (89 shorter events, 14.9 us)
Async XLA Ops:
  7.2 15.1 %copy-start = (bf16[128,3584]{1,0:T(8,128)(2,1)S(1)}, bf16[128,3584]{1,0:T(8,128)(2,1)}, u32[]{:S(2)}) copy-start(bf16[128,3584]{1,0:T(8,128)(2,1)} %param.10) | copy-start | bytes 2752516
  7.2 173.1 %all-gather.4.cloned.1.call-start = ((), (), s32[]{:S(2)}) async-start(), calls=%async_computation.5 | async-start | bytes 13045760 | tf_op jit(solution)/shard_map/all_gather | solution.py:98
  8.3 10.4 %collective-permute-start = (bf16[28,1792]{1,0:T(8,128)(2,1)S(1)}, bf16[28,1792]{1,0:T(8,128)(2,1)S(1)}, u32[]{:S(2)}, u32[]{:S(2)}) collective-permute-start(bf16[28,1792]{1,0:T(8,128)(2,1)S(1)} %get-tuple-element.32), channel_id=1, source_target_pairs={{0,0},{1,16},{2,1},{3,17},{4,2},{5,18},{6,3},{7,19},{8,4},{9,20},{... | collective-permute-start | bytes 301064 | tf_op jit(solution)/shard_map/ppermute | solution.py:46
  14.5 5.4 %collective-permute-start.1 = (bf16[28,1792]{1,0:T(8,128)(2,1)S(1)}, bf16[28,1792]{1,0:T(8,128)(2,1)S(1)}, u32[]{:S(2)}, u32[]{:S(2)}) collective-permute-start(bf16[28,1792]{1,0:T(8,128)(2,1)S(1)} %get-tuple-element.33), channel_id=1, source_target_pairs={{0,16},{1,0},{2,17},{3,1},{4,18},{5,2},{6,19},{7,3},{8,20},{9,4},{... | collective-permute-start | bytes 301064 | tf_op jit(solution)/shard_map/ppermute | solution.py:47
  20.7 212.4 %all-gather.6.cloned.1.call-start = ((), (), s32[]{:S(2)}) async-start(), calls=%async_computation.6 | async-start | bytes 38535168 | tf_op jit(solution)/shard_map/all_gather | solution.py:120
  24.3 109.4 %copy-start.2 = (bf16[512,3584]{1,0:T(8,128)(2,1)S(1)}, bf16[512,3584]{1,0:T(8,128)(2,1)}, u32[]{:S(2)}) copy-start(bf16[512,3584]{1,0:T(8,128)(2,1)} %param.11) | copy-start | bytes 11010052
  133.8 4.0 %copy-start.6 = (bf16[128,8,3584]{2,1,0:T(8,128)(2,1)}, bf16[128,8,3584]{2,1,0:T(8,128)(2,1)S(1)}, u32[]{:S(2)}) copy-start(bf16[128,8,3584]{2,1,0:T(8,128)(2,1)S(1)} %all_to_all.34) | copy-start | bytes 22020100
  137.8 1.4 copy-start.9
  202.3 5.9 %copy-start.12 = (bf16[3584]{0:T(1024)(128)(2,1)S(1)}, bf16[3584]{0:T(1024)(128)(2,1)}, u32[]{:S(2)}) copy-start(bf16[3584]{0:T(1024)(128)(2,1)} %param.19) | copy-start | bytes 21508
  202.3 92.3 %all-to-all-start.2 = ((bf16[128,8,3584]{2,1,0:T(8,128)(2,1)}), bf16[128,8,3584]{2,1,0:T(8,128)(2,1)}, u32[]{:S(2)}, u32[]{:S(2)}) async-start(bf16[128,8,3584]{2,1,0:T(8,128)(2,1)} %bitcast.61), calls=%async_computation.2 | async-start | bytes 14680064 | tf_op jit(solution)/shard_map/all_to_all | solution.py:54
  208.1 6.4 %copy-start.13 = (s32[128]{0:T(128)S(1)}, s32[128]{0:T(128)}, u32[]{:S(2)}) copy-start(s32[128]{0:T(128)} %param.13) | copy-start | bytes 1540
  208.2 6.4 %copy-start.11 = (bf16[3584,16]{0,1:T(8,128)(2,1)S(1)}, bf16[3584,16]{0,1:T(8,128)(2,1)}, u32[]{:S(2)}) copy-start(bf16[3584,16]{0,1:T(8,128)(2,1)} %param.17) | copy-start | bytes 344068
  214.5 3.3 copy-start.3
  233.1 12.7 %copy-start.4 = (bf16[512,3584]{1,0:T(8,128)(2,1)S(1)}, bf16[512,3584]{1,0:T(8,128)(2,1)}, u32[]{:S(2)}) copy-start(bf16[512,3584]{1,0:T(8,128)(2,1)} %param.14) | copy-start | bytes 11010052
  245.8 10.4 %copy-start.7 = (bf16[512,3584]{0,1:T(8,128)(2,1)S(1)}, bf16[512,3584]{0,1:T(8,128)(2,1)}, u32[]{:S(2)}) copy-start(bf16[512,3584]{0,1:T(8,128)(2,1)} %copy.39) | copy-start | bytes 11010052
  245.8 10.4 %copy-start.10 = (bf16[16,3584]{1,0:T(8,128)(2,1)S(1)}, bf16[16,3584]{1,0:T(8,128)(2,1)}, u32[]{:S(2)}) copy-start(bf16[16,3584]{1,0:T(8,128)(2,1)} %param.18) | copy-start | bytes 344068
  294.6 5.3 %copy-start.5 = (f32[256,3584]{1,0:T(8,128)S(1)}, f32[256,3584]{1,0:T(8,128)}, u32[]{:S(2)}) copy-start(f32[256,3584]{1,0:T(8,128)} %fusion.35) | copy-start | bytes 11010052
  299.9 2.7 copy-start.1
  300.5 2.7 copy-start.8
  315.4 23.3 %all-to-all-start.4 = ((f32[128,1,896]{2,1,0:T(1,128)}), f32[128,1,896]{2,1,0:T(1,128)S(1)}, u32[]{:S(2)}, u32[]{:S(2)}) async-start(f32[128,1,896]{2,1,0:T(1,128)} %copy.46), calls=%async_computation.4 | async-start | bytes 917504 | tf_op jit(solution)/shard_map/all_to_all | solution.py:54
Sparse Core Ops, SparseCore 0:
  20.8 159.4 all-gather.3
  181.9 45.9 all-gather.5
where the time goes:
time: 348 us; the launch traced here: 347 us
  blocking collectives  144 us (41%)
  matrix products  82.2 us (24%)
  waiting for transfers between devices  58.3 us (17%)
  starting transfers between devices  23.3 us (7%)
  local copies, waits for them, and re-layouts  18 us (5%)
  between operations  14.5 us (4%)
  other arithmetic  6.98 us (2%)
    all_to_all x3, blocking collectives, exchange(): return lax.all_to_all(array, PB_PA, split_axis=0, concat_axis=0, tiled=True)  144 us
    dot_general x12, matrix products, dot(): return jnp.dot(a, b, preferred_element_type=f32, **kw)  55.1 us
    all_to_all x2, waiting for transfers between devices, exchange(): return lax.all_to_all(array, PB_PA, split_axis=0, concat_axis=0, tiled=True)  37.9 us
    all_gather x1, waiting for transfers between devices, local(): half_weight = lax.all_gather(weight_rows, CHIPS, axis=0, tiled=True)  16.1 us
    all_to_all x2, starting transfers between devices, exchange(): return lax.all_to_all(array, PB_PA, split_axis=0, concat_axis=0, tiled=True)  15.9 us
    dot_general x1, matrix products, local(): lax.dot_general(far_weight, arrived, product_dims, preferred_element_type...  10.6 us
    unnamed x30, local copies, waits for them, and re-layouts  9.97 us
    dot_general x1, matrix products, local(): lax.dot_general(near_weight, queries, product_dims, preferred_element_typ...  7.38 us
  transfers between devices with their start and end apart: 6, of which 5 were waited for; matrix products, arithmetic and copies ran while one was open for 24% of the time, Pallas kernels for 0%

commit v1 on v0

--- a/solution.py
+++ b/solution.py
@@ -3,6 +3,8 @@
 import jax
 import jax.numpy as jnp
 from jax import lax
+from jax.experimental import pallas as pl
+from jax.experimental.pallas import tpu as pltpu
 from jax.sharding import Mesh
 from jax.sharding import PartitionSpec as P
 
@@ -19,6 +21,7 @@
 absent_mass = 1e30
 f32 = jnp.float32
 bf16 = jnp.bfloat16
+MESH = pl.DeviceIdType.MESH
 
 
 def dot(a, b, **kw):
@@ -52,6 +55,122 @@
 
 def exchange(array):
     return lax.all_to_all(array, PB_PA, split_axis=0, concat_axis=0, tiled=True)
+
+
+def layer_forward_kernel(
+    context, half_weight, residual, down, up, hidden, narrow, hidden_up, inverse,
+    own, other, own_sem, send_sem, recv_sem, squares,
+):
+    core = lax.axis_index("pb_1")
+    twin = (lax.axis_index("pb_0"), 1 - core, lax.axis_index("pa_0"), lax.axis_index("pa_1"))
+    tile = own.shape[2]
+    half = half_weight.shape[1]
+    tiles = half // tile
+    barrier = pltpu.get_barrier_semaphore()
+    pl.semaphore_signal(barrier, inc=1, device_id=twin, device_id_type=MESH)
+    pl.semaphore_wait(barrier, 1)
+
+    def columns(j):
+        return pl.ds(pl.multiple_of(j * tile, tile), tile)
+
+    def sent(j):
+        return pltpu.make_async_remote_copy(
+            half_weight.at[:, columns(j)], other.at[j], send_sem.at[j], recv_sem.at[j],
+            device_id=twin, device_id_type=MESH,
+        )
+
+    def fetched(j):
+        return pltpu.make_async_copy(
+            half_weight.at[:, columns(j)], own.at[lax.rem(j, 2)], own_sem.at[lax.rem(j, 2)]
+        )
+
+    fetched(0).start()
+
+    def send(j, carry):
+        sent(j).start()
+        return carry
+
+    lax.fori_loop(0, tiles, send, 0)
+    low = lax.dot_general(
+        context[...], down[...], (((1,), (1,)), ((), ())), preferred_element_type=f32
+    ).astype(bf16)
+    narrow[...] = low.astype(f32)
+    squares[...] = jnp.zeros_like(squares)
+    hidden_up[...] = jnp.zeros_like(hidden_up)
+
+    def step(weight, start):
+        at = pl.ds(pl.multiple_of(start, tile), tile)
+        up_tile = up[:, at]
+        value = (
+            residual[:, at].astype(f32)
+            + jnp.dot(context[...], weight, preferred_element_type=f32)
+            + adapter_scale * jnp.dot(low, up_tile, preferred_element_type=f32)
+        )
+        squares[...] += jnp.sum(value * value, axis=1, keepdims=True)
+        value = value.astype(bf16)
+        hidden[:, at] = value
+        hidden_up[...] += lax.dot_general(
+            value, up_tile, (((1,), (1,)), ((), ())), preferred_element_type=f32
+        )
+
+    def own_step(j, carry):
+        fetched(j).wait()
+
+        @pl.when(j + 1 < tiles)
+        def _():
+            fetched(j + 1).start()
+
+        step(own[lax.rem(j, 2)], core * half + j * tile)
+        return carry
+
+    lax.fori_loop(0, tiles, own_step, 0)
+
+    def other_step(j, carry):
+        sent(j).wait_recv()
+        step(other[j], (1 - core) * half + j * tile)
+        return carry
+
+    lax.fori_loop(0, tiles, other_step, 0)
+    inverse[...] = lax.rsqrt(squares[...] / MODEL_WIDTH + epsilon)
+
+    def done(j, carry):
+        sent(j).wait_send()
+        return carry
+
+    lax.fori_loop(0, tiles, done, 0)
+
+
+def layer_forward(context, half_weight, residual, down, up):
+    tokens, width = context.shape
+    half = half_weight.shape[1]
+    tile = 256
+    tiles = half // tile
+    rank = up.shape[0]
+    vmem = pl.BlockSpec(memory_space=pltpu.VMEM)
+    return pl.pallas_call(
+        layer_forward_kernel,
+        out_shape=(
+            jax.ShapeDtypeStruct((tokens, width), bf16),
+            jax.ShapeDtypeStruct((tokens, rank), f32),
+            jax.ShapeDtypeStruct((tokens, rank), f32),
+            jax.ShapeDtypeStruct((tokens, 1), f32),
+        ),
+        in_specs=[vmem, pl.BlockSpec(memory_space=pl.ANY), vmem, vmem, vmem],
+        out_specs=(vmem, vmem, vmem, vmem),
+        scratch_shapes=[
+            pltpu.VMEM((2, width, tile), bf16),
+            pltpu.VMEM((tiles, width, tile), bf16),
+            pltpu.SemaphoreType.DMA((2,)),
+            pltpu.SemaphoreType.DMA((tiles,)),
+            pltpu.SemaphoreType.DMA((tiles,)),
+            pltpu.VMEM((tokens, 1), f32),
+        ],
+        compiler_params=pltpu.CompilerParams(
+            collective_id=1, has_side_effects=True, vmem_limit_bytes=44 * 1024 * 1024
+        ),
+        cost_estimate=pl.CostEstimate(flops=1000, bytes_accessed=1000, transcendentals=0),
+        name="layer_forward",
+    )(context, half_weight, residual, down, up)
 
 
 def local(
@@ -114,10 +233,7 @@
     far_mean = (dot(far_exp.astype(bf16), passages) / far_sum[:, None]).astype(bf16)
     returned = exchange(far_mean.reshape(device_count, slot_rows, MODEL_WIDTH))
     returned = returned.reshape(-1, MODEL_WIDTH)
-    far_mass, _ = lax.optimization_barrier((far_mass, far_mean))
     returned_mass = exchange(far_mass.reshape(device_count, slot_rows)).reshape(-1)
-    half_weight, returned_mass = lax.optimization_barrier((half_weight, returned_mass))
-    both_halves = lax.all_gather(half_weight, "pb_1", axis=0, tiled=False)
 
     hits = [key[t][:, None] == row_ids[None, :] for t in range(hard_count)]
     masses = [near_mass] + [
@@ -151,27 +267,27 @@
     ).astype(bf16)
     far_grad = lax.dot_general(far_weight, arrived, product_dims, preferred_element_type=f32)
     near_grad = lax.dot_general(near_weight, queries, product_dims, preferred_element_type=f32)
-    grad_passages = loss_scale * score_scale * (far_grad + near_grad)
-
-    narrow = dot(context, adapter_down_weight).astype(bf16)
-    frozen = jnp.concatenate([dot(context, both_halves[0]), dot(context, both_halves[1])], axis=1)
-    hidden = residual.astype(f32) + frozen + adapter_scale * dot(narrow, adapter_up_weight)
-    inverse_rms = lax.rsqrt(jnp.mean(hidden * hidden, axis=1, keepdims=True) + epsilon)
-    hidden_low = hidden.astype(bf16)
-    hidden_up = dot(hidden_low, adapter_up_weight.T)
+
+    hidden_low, narrow, hidden_up, inverse_rms = layer_forward(
+        context, half_weight, residual, adapter_down_weight.T, adapter_up_weight
+    )
     token_query = jnp.arange(context.shape[0], dtype=jnp.int32) // TQ
     of_query = token_query[:, None] == jnp.arange(RERUN_QUERIES, dtype=jnp.int32)[None, :]
     narrow_sums = jnp.sum(
-        (inverse_rms * narrow.astype(f32)).reshape(RERUN_QUERIES, TQ, -1), axis=1
-    )
-
-    returned, hidden_low, hidden_up, inverse_rms, narrow_sums = lax.optimization_barrier(
-        (returned, hidden_low, hidden_up, inverse_rms, narrow_sums)
+        (inverse_rms * narrow).reshape(RERUN_QUERIES, TQ, -1), axis=1
+    )
+
+    returned, hidden_low, hidden_up, inverse_rms, narrow_sums, far_grad = (
+        lax.optimization_barrier(
+            (returned, hidden_low, hidden_up, inverse_rms, narrow_sums, far_grad)
+        )
     )
     far_part = dot(mix_parts, returned)
     query_gradient = (loss_scale * score_scale) * (
         far_part[:query_count] + far_part[query_count:] + near_part
     )
+
+    grad_passages = loss_scale * score_scale * (far_grad + near_grad)
 
     scaled = final_norm_weight.astype(f32)[None, :] * (query_gradient[:RERUN_QUERIES] / TQ)
     products = dot(hidden_low, scaled.astype(bf16).T)
@@ -183,7 +299,7 @@
     ).reshape(context.shape[0], -1)
     grad_narrow = (adapter_scale * (inverse_rms * spread_up - slope * hidden_up)).astype(bf16)
     down_term = lax.dot_general(grad_narrow, context, product_dims, preferred_element_type=f32)
-    weighted = (slope * narrow.astype(f32)).astype(bf16)
+    weighted = (slope * narrow).astype(bf16)
     up_term = adapter_scale * (
         lax.dot_general(
             narrow_sums,

time: 348 us -> 333 us (0.957)
  blocking collectives: 144 us -> 0 us
  waiting for transfers between devices: 58.3 us -> 154 us
  starting transfers between devices: 23.3 us -> 54.8 us
  Pallas kernels: 0 us -> 25.2 us
  matrix products: 82.2 us -> 59.3 us
    all_to_all x3 -> x0, blocking collectives: 144 us -> none  [exchange(): return lax.all_to_all(array, PB_PA, split_axis=0, concat_axis=0, tiled=True)]
    all_to_all x2 -> x5, waiting for transfers between devices: 37.9 us -> 150 us  [exchange(): return lax.all_to_all(array, PB_PA, split_axis=0, concat_axis=0, tiled=True)]
    all_to_all x2 -> x5, starting transfers between devices: 15.9 us -> 47.5 us  [exchange(): return lax.all_to_all(array, PB_PA, split_axis=0, concat_axis=0, tiled=True)]
    pallas_call x0 -> x1, Pallas kernels: none -> 25.2 us  [layer_forward(): pl.pallas_call(layer_forward_kernel, out_shape=(jax.ShapeDtypeStruct((tok...]
    dot_general x12 -> x7, matrix products: 55.1 us -> 32.3 us  [dot(): return jnp.dot(a, b, preferred_element_type=f32, **kw)]
    all_gather x1, waiting for transfers between devices: 16.1 us -> 0.01 us  [local(): half_weight = lax.all_gather(weight_rows, CHIPS, axis=0, tiled=True)]
    unnamed x30 -> x25, local copies, waits for them, and re-layouts: 9.97 us -> 7.87 us
  transfers between devices with their start and end apart: 6 -> 8, of which waited for: 5 -> 7; matrix products, arithmetic and copies ran while one was open for 24% -> 17% of each run, Pallas kernels for 0% -> 8%
where the time goes in v1:
time: 333 us
  waiting for transfers between devices  154 us (46%)
  matrix products  59.3 us (18%)
  starting transfers between devices  54.8 us (16%)
  Pallas kernels  25.2 us (8%)
  local copies, waits for them, and re-layouts  17 us (5%)
  between operations  14.5 us (4%)
  other arithmetic  7.56 us (2%)
    all_to_all x5, waiting for transfers between devices, exchange(): return lax.all_to_all(array, PB_PA, split_axis=0, concat_axis=0, tiled=True)  150 us
    all_to_all x5, starting transfers between devices, exchange(): return lax.all_to_all(array, PB_PA, split_axis=0, concat_axis=0, tiled=True)  47.5 us
    dot_general x7, matrix products, dot(): return jnp.dot(a, b, preferred_element_type=f32, **kw)  32.3 us
    pallas_call x1, Pallas kernels, layer_forward(): pl.pallas_call(layer_forward_kernel, out_shape=(jax.ShapeDtypeStruct((tok...  25.2 us
    dot_general x1, matrix products, local(): lax.dot_general(far_weight, arrived, product_dims, preferred_element_type...  10.6 us
    unnamed x25, local copies, waits for them, and re-layouts  7.87 us
    dot_general x1, matrix products, local(): lax.dot_general(near_weight, queries, product_dims, preferred_element_typ...  7.37 us
  transfers between devices with their start and end apart: 8, of which 7 were waited for; matrix products, arithmetic and copies ran while one was open for 17% of the time, Pallas kernels for 8%

profile of v1, /device:TPU:1, one launch (start us, length us, event | category | flops | bytes accessed | tf_op | source)
XLA Modules:
  0.0 332.6 jit_solution(8701503941980592496)
XLA Ops:
  7.2 1.0 broadcast_select_fusion.1
  8.3 6.2 %collective-permute-start = (bf16[28,1792]{1,0:T(8,128)(2,1)S(1)}, bf16[28,1792]{1,0:T(8,128)(2,1)S(1)}, u32[]{:S(2)}, u32[]{:S(2)}) collective-permute-start(bf16[28,1792]{1,0:T(8,128)(2,1)S(1)} %get-tuple-element.36), channel_id=1, source_target_pairs={{0,0},{1,16},{2,1},{3,17},{4,2},{5,18},{6,3},{7,19},{8,4},{9,20},{... | collective-permute-start | bytes 301064 | tf_op jit(solution)/shard_map/ppermute | solution.py:49
  14.5 1.1 collective-permute-start.1
  15.6 3.1 collective-permute-done
  18.7 1.2 collective-permute-done.1
  22.2 5.1 %convolution_bitcast_fusion = bf16[128,8,3584]{2,1,0:T(8,128)(2,1)} fusion(bf16[128,3584]{1,0:T(8,128)(2,1)S(1)} %copy-done, s32[128]{0:T(128)S(1)} %get-tuple-element.43, s32[128]{0:T(128)S(1)} %get-tuple-element.41, s32[128]{0:T(128)S(1)} %get-tuple-element.42, s32[128]{0:T(128)S(1)} %get-tuple-element.40), kind=kOutput, calls=%fused_computation.7 | convolution fusion | flops 940441600 | bytes 8259584 | tf_op jit(solution)/shard_map/dot_general | solution.py:213
  27.3 14.8 %all-to-all-start = ((bf16[128,8,3584]{2,1,0:T(8,128)(2,1)}), bf16[128,8,3584]{2,1,0:T(8,128)(2,1)}, u32[]{:S(2)}, u32[]{:S(2)}) async-start(bf16[128,8,3584]{2,1,0:T(8,128)(2,1)} %convolution_bitcast_fusion), calls=%async_computation | async-start | bytes 14680064 | tf_op jit(solution)/shard_map/all_to_all | solution.py:57
  42.1 3.5 %fusion.60 = (f32[128]{0:T(128)S(1)}, f32[128,512]{1,0:T(8,128)S(1)}) fusion(bf16[128,3584]{1,0:T(8,128)(2,1)S(1)} %copy-done, bf16[512,3584]{1,0:T(8,128)(2,1)} %param.11), kind=kOutput, calls=%fused_computation.127 | convolution fusion | flops 469892992 | bytes 4850176 | tf_op jit(solution)/shard_map/dot_general | solution.py:28
  45.8 94.9 %all-to-all-done = bf16[128,8,3584]{2,1,0:T(8,128)(2,1)} async-done(((bf16[128,8,3584]{2,1,0:T(8,128)(2,1)}), bf16[128,8,3584]{2,1,0:T(8,128)(2,1)}, u32[]{:S(2)}, u32[]{:S(2)}) %all-to-all-start) | async-done | bytes 7340064 | tf_op jit(solution)/shard_map/all_to_all | solution.py:57
  140.7 7.4 %multiply_reduce_fusion = (f32[1024]{0:T(1024)S(1)}, f32[1024,512]{0,1:T(8,128)S(1)}) fusion(bf16[512,3584]{1,0:T(8,128)(2,1)} %param.11, bf16[128,8,3584]{2,1,0:T(8,128)(2,1)} %all-to-all-done), kind=kOutput, calls=%fused_computation.19 | convolution fusion | flops 3759143936 | bytes 13111296 | tf_op jit(solution)/shard_map/dot_general | solution.py:28
  148.1 1.3 copy-done.9
  150.5 8.5 %all-to-all-start.1 = ((f32[128,1,8]{2,1,0:T(1,128)}), f32[128,1,8]{2,1,0:T(1,128)S(1)}, u32[]{:S(2)}, u32[]{:S(2)}) async-start(f32[128,1,8]{2,1,0:T(1,128)} %bitcast.7), calls=%async_computation.1 | async-start | bytes 131072 | tf_op jit(solution)/shard_map/all_to_all | solution.py:57
  159.3 9.5 %all-to-all-done.1 = f32[128,1,8]{2,1,0:T(1,128)S(1)} async-done(((f32[128,1,8]{2,1,0:T(1,128)}), f32[128,1,8]{2,1,0:T(1,128)S(1)}, u32[]{:S(2)}, u32[]{:S(2)}) %all-to-all-start.1) | async-done | bytes 4128 | tf_op jit(solution)/shard_map/all_to_all | solution.py:57
  171.7 4.5 %all-to-all-start.3 = ((f32[128,1,8]{2,1,0:T(1,128)}), f32[128,1,8]{2,1,0:T(1,128)S(1)}, u32[]{:S(2)}, u32[]{:S(2)}) async-start(f32[128,1,8]{2,1,0:T(1,128)} %bitcast.12), calls=%async_computation.3 | async-start | bytes 131072 | tf_op jit(solution)/shard_map/all_to_all | solution.py:57
  176.2 9.8 %fusion.4 = bf16[128,8,3584]{2,1,0:T(8,128)(2,1)} fusion(f32[1024]{0:T(1024)S(1)} %fusion.7, bf16[512,3584]{1,0:T(8,128)(2,1)} %param.11, f32[1024,512]{0,1:T(8,128)} %copy-done.9, f32[1024]{0:T(1024)S(1)} %get-tuple-element.50), kind=kOutput, calls=%fused_computation.6 | convolution fusion | flops 3767009280 | bytes 13115392 | tf_op jit(solution)/shard_map/dot_general | solution.py:28
  186.1 10.1 %all-to-all-start.2 = ((bf16[128,8,3584]{2,1,0:T(8,128)(2,1)}), bf16[128,8,3584]{2,1,0:T(8,128)(2,1)}, u32[]{:S(2)}, u32[]{:S(2)}) async-start(bf16[128,8,3584]{2,1,0:T(8,128)(2,1)} %fusion.4), calls=%async_computation.2 | async-start | bytes 14680064 | tf_op jit(solution)/shard_map/all_to_all | solution.py:57
  196.4 5.1 %fusion.27 = f32[256,3584]{1,0:T(8,128)} fusion(bf16[512,3584]{1,0:T(8,128)(2,1)} %param.11, bf16[128,512]{1,0:T(8,128)(2,1)S(1)} %fusion.34, bf16[128,512]{1,0:T(8,128)(2,1)S(1)} %get-tuple-element.33), kind=kOutput, calls=%fused_computation.55 | convolution fusion | flops 940048384 | bytes 7602176 | tf_op jit(solution)/shard_map/dot_general | solution.py:28
  203.0 10.6 %fusion = f32[512,3584]{1,0:T(8,128)} fusion(bf16[128,8,3584]{2,1,0:T(8,128)(2,1)} %all-to-all-done, f32[1024,512]{0,1:T(8,128)} %copy-done.9, f32[1024]{0:T(1024)S(1)} %sub.234), kind=kOutput, calls=%fused_computation.1 | convolution fusion | flops 3759669248 | bytes 16781312 | tf_op jit(solution)/shard_map/dot_general | solution.py:268
  213.7 2.0 copy-done.3
  215.7 25.2 %layer_forward.1 = (bf16[512,3584]{1,0:T(8,128)(2,1)S(1)}, f32[512,16]{1,0:T(8,128)S(1)}, f32[512,16]{1,0:T(8,128)S(1)}, f32[512,1]{1,0:T(8,128)S(1)}) custom-call(bf16[512,3584]{1,0:T(8,128)(2,1)S(1)} %copy-done.3, bf16[3584,1792]{1,0:T(8,128)(2,1)} %all-gather.2.cloned.1.call-done.half_weight, bf16[512,3584]{1,0:T(8,128)(2,1)} %residual.1, ...), custom_call_target="tpu_custom_call" | custom-call | flops 1000 | bytes 1000 | tf_op jit(solution)/shard_map/layer_forward/pallas_call | solution.py:150
  240.9 1.9 copy-done.1
  243.0 39.5 %all-to-all-done.2 = bf16[128,8,3584]{2,1,0:T(8,128)(2,1)} async-done(((bf16[128,8,3584]{2,1,0:T(8,128)(2,1)}), bf16[128,8,3584]{2,1,0:T(8,128)(2,1)}, u32[]{:S(2)}, u32[]{:S(2)}) %all-to-all-start.2) | async-done | bytes 7340064 | tf_op jit(solution)/shard_map/all_to_all | solution.py:57
  282.5 5.3 %fusion.16 = f32[256,3584]{1,0:T(8,128)S(1)} fusion(bf16[1024,3584]{1,0:T(8,128)(2,1)} %bitcast.9, bf16[128,1024]{1,0:T(8,128)(2,1)S(1)} %subtract_convert_fusion, bf16[128,1024]{1,0:T(8,128)(2,1)S(1)} %fusion.20), kind=kOutput, calls=%fused_computation.27 | convolution fusion | flops 1880096768 | bytes 11534336 | tf_op jit(solution)/shard_map/dot_general | solution.py:28
  288.7 1.9 copy-done.2
  290.6 1.1 fusion.10
  292.4 2.9 fusion.5
  296.1 1.3 concatenate.20
  297.8 1.3 concatenate.21
  299.8 1.3 copy.37
  301.1 9.6 %all-to-all-start.4 = ((f32[128,1,896]{2,1,0:T(1,128)}), f32[128,1,896]{2,1,0:T(1,128)S(1)}, u32[]{:S(2)}, u32[]{:S(2)}) async-start(f32[128,1,896]{2,1,0:T(1,128)} %copy.37), calls=%async_computation.4 | async-start | bytes 917504 | tf_op jit(solution)/shard_map/all_to_all | solution.py:57
  310.7 7.4 %add_multiply_fusion = f32[512,3584]{1,0:T(8,128)} fusion(f32[512,3584]{1,0:T(8,128)} %fusion, bf16[128,3584]{1,0:T(8,128)(2,1)S(1)} %copy-done, f32[128,512]{1,0:T(8,128)S(1)} %get-tuple-element.49, f32[128]{0:T(128)S(1)} %get-tuple-element.31, s32[128]{0:T(128)S(1)} %copy-done.11), kind=kOutput, calls=%fused_computation.5 | convolution fusion | flops 473759744 | bytes 15860736 | tf_op jit(solution)/shard_map/dot_general | solution.py:269
  318.1 5.9 %all-to-all-done.4 = f32[128,1,896]{2,1,0:T(1,128)S(1)} async-done(((f32[128,1,896]{2,1,0:T(1,128)}), f32[128,1,896]{2,1,0:T(1,128)S(1)}, u32[]{:S(2)}, u32[]{:S(2)}) %all-to-all-start.4) | async-done | bytes 458784 | tf_op jit(solution)/shard_map/all_to_all | solution.py:57
  (78 shorter events, 14.0 us)
Async XLA Ops:
  7.2 15.0 %copy-start = (bf16[128,3584]{1,0:T(8,128)(2,1)S(1)}, bf16[128,3584]{1,0:T(8,128)(2,1)}, u32[]{:S(2)}) copy-start(bf16[128,3584]{1,0:T(8,128)(2,1)} %param.10) | copy-start | bytes 2752516
  7.2 206.4 %all-gather.2.cloned.1.call-start = ((), (), s32[]{:S(2)}) async-start(), calls=%async_computation.5 | async-start | bytes 13045760 | tf_op jit(solution)/shard_map/all_gather | solution.py:217
  8.3 10.4 %collective-permute-start = (bf16[28,1792]{1,0:T(8,128)(2,1)S(1)}, bf16[28,1792]{1,0:T(8,128)(2,1)S(1)}, u32[]{:S(2)}, u32[]{:S(2)}) collective-permute-start(bf16[28,1792]{1,0:T(8,128)(2,1)S(1)} %get-tuple-element.36), channel_id=1, source_target_pairs={{0,0},{1,16},{2,1},{3,17},{4,2},{5,18},{6,3},{7,19},{8,4},{9,20},{... | collective-permute-start | bytes 301064 | tf_op jit(solution)/shard_map/ppermute | solution.py:49
  14.5 5.4 %collective-permute-start.1 = (bf16[28,1792]{1,0:T(8,128)(2,1)S(1)}, bf16[28,1792]{1,0:T(8,128)(2,1)S(1)}, u32[]{:S(2)}, u32[]{:S(2)}) collective-permute-start(bf16[28,1792]{1,0:T(8,128)(2,1)S(1)} %get-tuple-element.37), channel_id=1, source_target_pairs={{0,16},{1,0},{2,17},{3,1},{4,18},{5,2},{6,19},{7,3},{8,20},{9,4},{... | collective-permute-start | bytes 301064 | tf_op jit(solution)/shard_map/ppermute | solution.py:50
  27.3 113.4 %all-to-all-start = ((bf16[128,8,3584]{2,1,0:T(8,128)(2,1)}), bf16[128,8,3584]{2,1,0:T(8,128)(2,1)}, u32[]{:S(2)}, u32[]{:S(2)}) async-start(bf16[128,8,3584]{2,1,0:T(8,128)(2,1)} %convolution_bitcast_fusion), calls=%async_computation | async-start | bytes 14680064 | tf_op jit(solution)/shard_map/all_to_all | solution.py:57
  148.1 1.3 copy-start.9
  150.5 18.4 %all-to-all-start.1 = ((f32[128,1,8]{2,1,0:T(1,128)}), f32[128,1,8]{2,1,0:T(1,128)S(1)}, u32[]{:S(2)}, u32[]{:S(2)}) async-start(f32[128,1,8]{2,1,0:T(1,128)} %bitcast.7), calls=%async_computation.1 | async-start | bytes 131072 | tf_op jit(solution)/shard_map/all_to_all | solution.py:57
  171.7 14.4 %all-to-all-start.3 = ((f32[128,1,8]{2,1,0:T(1,128)}), f32[128,1,8]{2,1,0:T(1,128)S(1)}, u32[]{:S(2)}, u32[]{:S(2)}) async-start(f32[128,1,8]{2,1,0:T(1,128)} %bitcast.12), calls=%async_computation.3 | async-start | bytes 131072 | tf_op jit(solution)/shard_map/all_to_all | solution.py:57
  186.0 10.2 %copy-start.10 = (bf16[3584]{0:T(1024)(128)(2,1)S(1)}, bf16[3584]{0:T(1024)(128)(2,1)}, u32[]{:S(2)}) copy-start(bf16[3584]{0:T(1024)(128)(2,1)} %param.19) | copy-start | bytes 21508
  186.0 10.2 %copy-start.11 = (s32[128]{0:T(128)S(1)}, s32[128]{0:T(128)}, u32[]{:S(2)}) copy-start(s32[128]{0:T(128)} %param.13) | copy-start | bytes 1540
  186.1 96.4 %all-to-all-start.2 = ((bf16[128,8,3584]{2,1,0:T(8,128)(2,1)}), bf16[128,8,3584]{2,1,0:T(8,128)(2,1)}, u32[]{:S(2)}, u32[]{:S(2)}) async-start(bf16[128,8,3584]{2,1,0:T(8,128)(2,1)} %fusion.4), calls=%async_computation.2 | async-start | bytes 14680064 | tf_op jit(solution)/shard_map/all_to_all | solution.py:57
  203.0 10.6 %copy-start.5 = (bf16[16,3584]{1,0:T(8,128)(2,1)S(1)}, bf16[16,3584]{1,0:T(8,128)(2,1)}, u32[]{:S(2)}) copy-start(bf16[16,3584]{1,0:T(8,128)(2,1)} %up.1) | copy-start | bytes 344068
  203.0 10.6 %copy-start.6 = (bf16[3584,16]{0,1:T(8,128)(2,1)S(1)}, bf16[3584,16]{0,1:T(8,128)(2,1)}, u32[]{:S(2)}) copy-start(bf16[3584,16]{0,1:T(8,128)(2,1)} %param.17) | copy-start | bytes 344068
  213.6 2.0 copy-start.3
  240.9 1.9 copy-start.1
  282.5 5.3 %copy-start.7 = (f32[256,3584]{1,0:T(8,128)S(1)}, f32[256,3584]{1,0:T(8,128)}, u32[]{:S(2)}) copy-start(f32[256,3584]{1,0:T(8,128)} %fusion.27) | copy-start | bytes 11010052
  287.8 2.7 copy-start.2
  288.4 3.2 copy-start.8
  292.2 3.3 %copy-start.4 = (bf16[512,3584]{1,0:T(8,128)(2,1)S(1)}, bf16[512,3584]{1,0:T(8,128)(2,1)}, u32[]{:S(2)}) copy-start(bf16[512,3584]{1,0:T(8,128)(2,1)} %context.1) | copy-start | bytes 11010052
  301.1 22.9 %all-to-all-start.4 = ((f32[128,1,896]{2,1,0:T(1,128)}), f32[128,1,896]{2,1,0:T(1,128)S(1)}, u32[]{:S(2)}, u32[]{:S(2)}) async-start(f32[128,1,896]{2,1,0:T(1,128)} %copy.37), calls=%async_computation.4 | async-start | bytes 917504 | tf_op jit(solution)/shard_map/all_to_all | solution.py:57
Sparse Core Ops, SparseCore 0:
  20.8 165.3 all-gather.1

commit v2 on v1

--- a/solution.py
+++ b/solution.py
@@ -1,3 +1,4 @@
+import functools
 import math
 
 import jax
@@ -171,6 +172,186 @@
         cost_estimate=pl.CostEstimate(flops=1000, bytes_accessed=1000, transcendentals=0),
         name="layer_forward",
     )(context, half_weight, residual, down, up)
+
+
+def far_kernel(score_scale, rows, passages, scores, mean, mass):
+    value = score_scale * lax.dot_general(
+        rows[...], passages[...], (((1,), (1,)), ((), ())), preferred_element_type=f32
+    )
+    scores[...] = value
+    peak = jnp.max(value, axis=1, keepdims=True)
+    weights = jnp.exp(value - peak)
+    total = jnp.sum(weights, axis=1, keepdims=True)
+    mass[...] = jnp.broadcast_to(peak + jnp.log(total), mass.shape)
+    inverse = 1.0 / total
+    weights = weights.astype(bf16)
+    tile = 512
+    for start in range(0, mean.shape[1], tile):
+        part = jnp.dot(
+            weights, passages[:, start : start + tile], preferred_element_type=f32
+        )
+        mean[:, start : start + tile] = (part * inverse).astype(bf16)
+
+
+def far_forward(rows, passages, score_scale):
+    count, width = rows.shape
+    passage_count = passages.shape[0]
+    block = 256
+    return pl.pallas_call(
+        functools.partial(far_kernel, score_scale),
+        out_shape=(
+            jax.ShapeDtypeStruct((count, passage_count), f32),
+            jax.ShapeDtypeStruct((count, width), bf16),
+            jax.ShapeDtypeStruct((count, 128), f32),
+        ),
+        grid=(count // block,),
+        in_specs=[
+            pl.BlockSpec((block, width), lambda i: (i, 0)),
+            pl.BlockSpec((passage_count, width), lambda i: (0, 0), pipeline_mode=pl.Buffered(1)),
+        ],
+        out_specs=(
+            pl.BlockSpec((block, passage_count), lambda i: (i, 0)),
+            pl.BlockSpec((block, width), lambda i: (i, 0)),
+            pl.BlockSpec((block, 128), lambda i: (i, 0)),
+        ),
+        compiler_params=pltpu.CompilerParams(vmem_limit_bytes=32 * 1024 * 1024),
+        name="far_forward",
+    )(rows, passages)
+
+
+def torus_place():
+    return tuple(lax.axis_index(axis) for axis in PB_PA)
+
+
+def flat_of(place):
+    return ((place[0] * 2 + place[1]) * 4 + place[2]) * 4 + place[3]
+
+
+def torus_peer(place, j):
+    return (
+        lax.rem(place[0] + lax.rem(j, 4), 4),
+        lax.rem(place[1] + j // 64, 2),
+        lax.rem(place[2] + lax.rem(j // 4, 4), 4),
+        lax.rem(place[3] + lax.rem(j // 16, 4), 4),
+    )
+
+
+def small_exchange_kernel(
+    mass, near_mass, key_column, key_row, mix, log_total, log_arrived,
+    mass_in, log_out, mass_send, mass_recv, log_send, log_recv,
+):
+    place = torus_place()
+    own = flat_of(place)
+    peers = mass.shape[0]
+    slot_rows = mass.shape[1]
+    all_rows = peers * slot_rows
+    hard_count = key_row.shape[0]
+    query_count = near_mass.shape[0]
+    barrier = pltpu.get_barrier_semaphore()
+
+    def greet(j, carry):
+        pl.semaphore_signal(
+            barrier, inc=1, device_id=torus_peer(place, j), device_id_type=MESH
+        )
+        return carry
+
+    lax.fori_loop(1, peers, greet, 0)
+    pl.semaphore_wait(barrier, peers - 1)
+
+    def sends(source, target, send_sem, recv_sem):
+        def body(j, carry):
+            peer = torus_peer(place, j)
+            pltpu.make_async_remote_copy(
+                source.at[flat_of(peer)], target.at[own], send_sem, recv_sem,
+                device_id=peer, device_id_type=MESH,
+            ).start()
+            return carry
+
+        lax.fori_loop(1, peers, body, 0)
+
+    def every(source, target, send_sem, recv_sem):
+        rest = pl.ds(0, peers - 1)
+        return pltpu.make_async_remote_copy(
+            source.at[rest], target.at[rest], send_sem, recv_sem,
+            device_id=torus_peer(place, 1), device_id_type=MESH,
+        )
+
+    sends(mass, mass_in, mass_send, mass_recv)
+    mass_in[own] = mass[own]
+    row_ids = lax.broadcasted_iota(jnp.int32, (query_count, all_rows), 1)
+    hits = [
+        key_column[t * query_count : (t + 1) * query_count, :] == row_ids
+        for t in range(hard_count)
+    ]
+    column_ids = lax.broadcasted_iota(jnp.int32, (all_rows, query_count), 0)
+    picks = jnp.zeros((all_rows, query_count), f32)
+    for t in range(hard_count):
+        picks = jnp.where(column_ids == key_row[t : t + 1, :], 1.0, picks)
+    filled = jnp.sum(picks, axis=1, keepdims=True) > 0.0
+    every(mass, mass_in, mass_send, mass_recv).wait_recv()
+    came = mass_in[...].reshape(all_rows, mass.shape[2])
+    masses = [jnp.broadcast_to(near_mass[...], (query_count, came.shape[1]))]
+    for hit in hits:
+        masses.append(
+            jnp.dot(
+                jnp.where(hit, 1.0, 0.0), came,
+                precision=lax.Precision.HIGHEST, preferred_element_type=f32,
+            )
+        )
+    peak = masses[0]
+    for value in masses[1:]:
+        peak = jnp.maximum(peak, value)
+    total = jnp.exp(masses[0] - peak)
+    for value in masses[1:]:
+        total = total + jnp.exp(value - peak)
+    log_value = peak + jnp.log(total)
+    log_total[...] = log_value
+    outgoing = jnp.dot(
+        picks, log_value, precision=lax.Precision.HIGHEST, preferred_element_type=f32
+    )
+    outgoing = jnp.where(filled, outgoing, absent_mass)
+    log_out[...] = outgoing.reshape(log_out.shape)
+    sends(log_out, log_arrived, log_send, log_recv)
+    log_arrived[own] = log_out[own]
+    shares = jnp.zeros((query_count, all_rows), f32)
+    for t in range(hard_count):
+        shares = jnp.where(hits[t], jnp.exp(masses[1 + t] - log_value)[:, :1], shares)
+    high = shares.astype(bf16)
+    mix[:query_count, :] = high
+    mix[query_count:, :] = (shares - high.astype(f32)).astype(bf16)
+    every(mass, mass_in, mass_send, mass_recv).wait_send()
+    last = every(log_out, log_arrived, log_send, log_recv)
+    last.wait_send()
+    last.wait_recv()
+
+
+def small_exchange(mass, near_mass, key):
+    peers, slot_rows, lanes = mass.shape
+    hard_count, query_count = key.shape
+    vmem = pl.BlockSpec(memory_space=pltpu.VMEM)
+    return pl.pallas_call(
+        small_exchange_kernel,
+        out_shape=(
+            jax.ShapeDtypeStruct((2 * query_count, peers * slot_rows), bf16),
+            jax.ShapeDtypeStruct((query_count, lanes), f32),
+            jax.ShapeDtypeStruct(mass.shape, f32),
+        ),
+        in_specs=[vmem] * 4,
+        out_specs=(vmem, vmem, vmem),
+        scratch_shapes=[
+            pltpu.VMEM(mass.shape, f32),
+            pltpu.VMEM(mass.shape, f32),
+            pltpu.SemaphoreType.DMA(()),
+            pltpu.SemaphoreType.DMA(()),
+            pltpu.SemaphoreType.DMA(()),
+            pltpu.SemaphoreType.DMA(()),
+        ],
+        compiler_params=pltpu.CompilerParams(
+            collective_id=2, has_side_effects=True, vmem_limit_bytes=24 * 1024 * 1024
+        ),
+        cost_estimate=pl.CostEstimate(flops=1000, bytes_accessed=1000, transcendentals=0),
+        name="small_exchange",
+    )(mass, near_mass[:, None], key.reshape(-1)[:, None], key)
 
 
 def local(
@@ -225,43 +406,19 @@
         jnp.concatenate([near_exp.astype(bf16), positive_hot.astype(bf16)], axis=0), passages
     )
 
-    far_scores = dot(arrived, passages.T) * score_scale
-    far_peak = jnp.max(far_scores, axis=1)
-    far_exp = jnp.exp(far_scores - far_peak[:, None])
-    far_sum = jnp.sum(far_exp, axis=1)
-    far_mass = far_peak + jnp.log(far_sum)
-    far_mean = (dot(far_exp.astype(bf16), passages) / far_sum[:, None]).astype(bf16)
+    far_scores, far_mean, far_mass = far_forward(arrived, passages, score_scale)
     returned = exchange(far_mean.reshape(device_count, slot_rows, MODEL_WIDTH))
     returned = returned.reshape(-1, MODEL_WIDTH)
-    returned_mass = exchange(far_mass.reshape(device_count, slot_rows)).reshape(-1)
-
-    hits = [key[t][:, None] == row_ids[None, :] for t in range(hard_count)]
-    masses = [near_mass] + [
-        jnp.sum(jnp.where(hit, returned_mass[None, :], 0.0), axis=1) for hit in hits
-    ]
-    peak = masses[0]
-    for mass in masses[1:]:
-        peak = jnp.maximum(peak, mass)
-    total = jnp.exp(masses[0] - peak)
-    for mass in masses[1:]:
-        total = total + jnp.exp(mass - peak)
-    log_total = peak + jnp.log(total)
-
-    filled = jnp.any(picks, axis=1)
-    log_outgoing = jnp.where(
-        filled, jnp.sum(jnp.where(picks, log_total[None, :], 0.0), axis=1), absent_mass
-    )
-    log_arrived = exchange(log_outgoing.reshape(device_count, slot_rows)).reshape(-1)
-
-    mix = jnp.zeros((query_count, all_rows), f32)
-    for t in range(hard_count):
-        mix = jnp.where(hits[t], jnp.exp(masses[1 + t] - log_total)[:, None], mix)
-    mix_parts = jnp.concatenate(two_parts(mix), axis=0)
+    mix_parts, log_total, log_arrived = small_exchange(
+        far_mass.reshape(device_count, slot_rows, -1), near_mass, key
+    )
+    log_total = log_total[:, 0]
+    log_arrived = log_arrived.reshape(all_rows, -1)[:, :1]
     near_share = jnp.exp(near_mass - log_total)
     near_part = (near_share / near_sum)[:, None] * stacked[:query_count] - stacked[query_count:]
 
     product_dims = (((0,), (0,)), ((), ()))
-    far_weight = jnp.exp(far_scores - log_arrived[:, None]).astype(bf16)
+    far_weight = jnp.exp(far_scores - log_arrived).astype(bf16)
     near_weight = (
         jnp.exp(near_scores - log_total[:, None]) - positive_hot.astype(f32)
     ).astype(bf16)

time: 333 us -> 383 us (1.15)
  waiting for transfers between devices: 154 us -> 10.2 us
  Pallas kernels: 25.2 us -> 156 us
  blocking collectives: 0 us -> 110 us
  starting transfers between devices: 54.8 us -> 20.8 us
  matrix products: 59.3 us -> 40.8 us
  local copies, waits for them, and re-layouts: 17 us -> 22.8 us
    all_to_all x5 -> x2, waiting for transfers between devices: 150 us -> 5.86 us  [exchange(): return lax.all_to_all(array, PB_PA, split_axis=0, concat_axis=0, tiled=True)]
    pallas_call x0 -> x2, Pallas kernels: none -> 131 us  [the longest x1 122 us: small_exchange(): pl.pallas_call(small_exchange_kernel, out_shape=(jax.ShapeDtypeStruct((2...]
    all_to_all x0 -> x1, blocking collectives: none -> 110 us  [exchange(): return lax.all_to_all(array, PB_PA, split_axis=0, concat_axis=0, tiled=True)]
    all_to_all x5 -> x2, starting transfers between devices: 47.5 us -> 13.5 us  [exchange(): return lax.all_to_all(array, PB_PA, split_axis=0, concat_axis=0, tiled=True)]
    dot_general x7 -> x5, matrix products: 32.3 us -> 15.4 us  [dot(): return jnp.dot(a, b, preferred_element_type=f32, **kw)]
    unnamed x25 -> x44, local copies, waits for them, and re-layouts: 7.87 us -> 14 us
  transfers between devices with their start and end apart: 8 -> 5, of which waited for: 7 -> 3; matrix products, arithmetic and copies ran while one was open for 17% -> 9% of each run, Pallas kernels for 8% -> 41%
where the time goes in v2:
time: 383 us; the launch traced here: 382 us
  Pallas kernels  156 us (41%)
  blocking collectives  110 us (29%)
  matrix products  40.8 us (11%)
  local copies, waits for them, and re-layouts  22.8 us (6%)
  starting transfers between devices  20.8 us (5%)
  between operations  14.5 us (4%)
  waiting for transfers between devices  10.2 us (3%)
  other arithmetic  7.02 us (2%)
    pallas_call x1, Pallas kernels, small_exchange(): pl.pallas_call(small_exchange_kernel, out_shape=(jax.ShapeDtypeStruct((2...  122 us
    all_to_all x1, blocking collectives, exchange(): return lax.all_to_all(array, PB_PA, split_axis=0, concat_axis=0, tiled=True)  110 us
    pallas_call x1, Pallas kernels, layer_forward(): pl.pallas_call(layer_forward_kernel, out_shape=(jax.ShapeDtypeStruct((tok...  24.3 us
    dot_general x5, matrix products, dot(): return jnp.dot(a, b, preferred_element_type=f32, **kw)  15.4 us
    unnamed x44, local copies, waits for them, and re-layouts  14 us
    all_to_all x2, starting transfers between devices, exchange(): return lax.all_to_all(array, PB_PA, split_axis=0, concat_axis=0, tiled=True)  13.5 us
    dot_general x1, matrix products, local(): lax.dot_general(far_weight, arrived, product_dims, preferred_element_type...  9.34 us
    pallas_call x1, Pallas kernels, far_forward(): pl.pallas_call(functools.partial(far_kernel, score_scale), out_shape=(jax...  9.09 us
  transfers between devices with their start and end apart: 5, of which 3 were waited for; matrix products, arithmetic and copies ran while one was open for 9% of the time, Pallas kernels for 41%

profile of v2, /device:TPU:1, one launch (start us, length us, event | category | flops | bytes accessed | tf_op | source)
XLA Modules:
  0.0 381.7 jit_solution(16319428717990575817)
XLA Ops:
  7.2 1.0 broadcast_select_fusion.1
  8.3 6.2 %collective-permute-start = (bf16[28,1792]{1,0:T(8,128)(2,1)S(1)}, bf16[28,1792]{1,0:T(8,128)(2,1)S(1)}, u32[]{:S(2)}, u32[]{:S(2)}) collective-permute-start(bf16[28,1792]{1,0:T(8,128)(2,1)S(1)} %get-tuple-element.44), channel_id=1, source_target_pairs={{0,0},{1,16},{2,1},{3,17},{4,2},{5,18},{6,3},{7,19},{8,4},{9,20},{... | collective-permute-start | bytes 301064 | tf_op jit(solution)/shard_map/ppermute | solution.py:50
  14.5 1.1 collective-permute-start.1
  15.6 3.1 collective-permute-done
  18.7 1.2 collective-permute-done.1
  22.2 2.1 convolution_bitcast_fusion
  24.3 109.8 %all_to_all.19 = bf16[128,8,3584]{2,1,0:T(8,128)(2,1)S(1)} all-to-all(bf16[128,8,3584]{2,1,0:T(8,128)(2,1)S(1)} %convolution_bitcast_fusion), channel_id=1, replica_groups=mesh['pb_0'=4,'pb_1'=2,'pa_0'=4,'pa_1'=4] {'pb_0','pb_1','pa_0','pa_1'}, dimensions={0} | all-to-all | bytes 14680064 | tf_op jit(solution)/shard_map/all_to_all | solution.py:58
  134.1 9.1 %far_forward.1 = (f32[1024,512]{1,0:T(8,128)S(1)}, bf16[1024,3584]{1,0:T(8,128)(2,1)S(1)}, f32[1024,128]{1,0:T(8,128)S(1)}) custom-call(bf16[1024,3584]{1,0:T(8,128)(2,1)S(1)} %bitcast.55, bf16[512,3584]{1,0:T(8,128)(2,1)S(1)} %copy-done.2), custom_call_target="tpu_custom_call" | custom-call | tf_op jit(solution)/shard_map/far_forward/pallas_call | solution.py:200
  143.2 3.0 copy-done.6
  147.0 9.3 %all-to-all-start.1 = ((bf16[128,8,3584]{2,1,0:T(8,128)(2,1)}), bf16[128,8,3584]{2,1,0:T(8,128)(2,1)}, u32[]{:S(2)}, u32[]{:S(2)}) async-start(bf16[128,8,3584]{2,1,0:T(8,128)(2,1)} %bitcast.56), calls=%async_computation.1 | async-start | bytes 14680064 | tf_op jit(solution)/shard_map/all_to_all | solution.py:58
  156.6 3.6 fusion.47
  162.7 0.8 add.94.near_mass
  165.0 5.1 %fusion.13 = f32[256,3584]{1,0:T(8,128)} fusion(bf16[512,3584]{1,0:T(8,128)(2,1)} %passages.1, bf16[128,512]{1,0:T(8,128)(2,1)S(1)} %fusion.20, bf16[128,512]{1,0:T(8,128)(2,1)S(1)} %get-tuple-element.41), kind=kOutput, calls=%fused_computation.27 | convolution fusion | flops 940048384 | bytes 7602176 | tf_op jit(solution)/shard_map/dot_general | solution.py:29
  170.1 122.4 %small_exchange.1 = (bf16[256,1024]{1,0:T(8,128)(2,1)S(1)}, f32[128,128]{1,0:T(8,128)S(1)}, f32[128,8,128]{2,1,0:T(8,128)S(1)}) custom-call(f32[128,8,128]{2,1,0:T(8,128)S(1)} %bitcast.58, f32[128,1]{1,0:T(8,128)S(1)} %add.94.near_mass, s32[512,1]{1,0:T(8,128)S(1)} %copy.60.key_column, s32[4,128]{1,0:T(4,128)S(1)} %broadcast_add_fusion.key_row), custom_call_target="tpu_custom_call" | custom-call | flops 1000 | bytes 1000 | tf_op jit(solution)/shard_map/small_exchange/pallas_call | solution.py:332
  294.1 1.2 copy.68
  295.3 1.0 slice_reduce_fusion
  296.3 9.3 %fusion.4 = f32[512,3584]{1,0:T(8,128)} fusion(f32[1024,512]{1,0:T(8,128)S(1)} %get-tuple-element.27, f32[1024]{0:T(1024)S(1)} %bitcast.60, bf16[128,8,3584]{2,1,0:T(8,128)(2,1)} %copy-done.1), kind=kOutput, calls=%fused_computation.13 | convolution fusion | flops 3759144960 | bytes 16781312 | tf_op jit(solution)/shard_map/dot_general | solution.py:425
  305.7 2.0 copy-done.5
  307.7 24.3 %layer_forward.1 = (bf16[512,3584]{1,0:T(8,128)(2,1)S(1)}, f32[512,16]{1,0:T(8,128)S(1)}, f32[512,16]{1,0:T(8,128)S(1)}, f32[512,1]{1,0:T(8,128)S(1)}) custom-call(bf16[512,3584]{1,0:T(8,128)(2,1)S(1)} %copy-done.5, bf16[3584,1792]{1,0:T(8,128)(2,1)} %all-gather.2.cloned.1.call-done.half_weight, bf16[512,3584]{1,0:T(8,128)(2,1)} %residual.1, ...), custom_call_target="tpu_custom_call" | custom-call | flops 1000 | bytes 1000 | tf_op jit(solution)/shard_map/layer_forward/pallas_call | solution.py:151
  332.0 1.9 copy-done.3
  334.2 5.3 %fusion.48 = f32[256,3584]{1,0:T(8,128)S(1)} fusion(bf16[256,1024]{1,0:T(8,128)(2,1)S(1)} %copy-done.13, bf16[1024,3584]{1,0:T(8,128)(2,1)} %bitcast.12), kind=kOutput, calls=%fused_computation.96 | convolution fusion | flops 1879048192 | bytes 11534336 | tf_op jit(solution)/shard_map/dot_general | solution.py:29
  340.4 1.8 copy-done.4
  342.2 1.1 fusion.3
  343.9 2.6 fusion.49
  346.5 1.3 concatenate.16
  348.2 1.3 fusion.27
  349.5 2.7 fusion
  352.3 1.3 concatenate.17
  354.3 1.3 copy.67
  355.6 4.2 %all-to-all-start.2 = ((f32[128,1,896]{2,1,0:T(1,128)}), f32[128,1,896]{2,1,0:T(1,128)S(1)}, u32[]{:S(2)}, u32[]{:S(2)}) async-start(f32[128,1,896]{2,1,0:T(1,128)} %copy.67), calls=%async_computation.2 | async-start | bytes 917504 | tf_op jit(solution)/shard_map/all_to_all | solution.py:58
  359.9 7.4 %add_multiply_fusion = f32[512,3584]{1,0:T(8,128)} fusion(f32[512,3584]{1,0:T(8,128)} %fusion.4, bf16[128,3584]{1,0:T(8,128)(2,1)S(1)} %copy-done, f32[128,512]{1,0:T(8,128)S(1)} %copy-done.17, f32[128]{0:T(128)S(1)} %get-tuple-element.38, s32[128]{0:T(128)S(1)} %copy-done.20), kind=kOutput, calls=%fused_computation | convolution fusion | flops 473759744 | bytes 15860736 | tf_op jit(solution)/shard_map/dot_general | solution.py:426
  367.2 5.9 %all-to-all-done.2 = f32[128,1,896]{2,1,0:T(1,128)S(1)} async-done(((f32[128,1,896]{2,1,0:T(1,128)}), f32[128,1,896]{2,1,0:T(1,128)S(1)}, u32[]{:S(2)}, u32[]{:S(2)}) %all-to-all-start.2) | async-done | bytes 458784 | tf_op jit(solution)/shard_map/all_to_all | solution.py:58
  (85 shorter events, 13.5 us)
Async XLA Ops:
  7.2 15.0 %copy-start = (bf16[128,3584]{1,0:T(8,128)(2,1)S(1)}, bf16[128,3584]{1,0:T(8,128)(2,1)}, u32[]{:S(2)}) copy-start(bf16[128,3584]{1,0:T(8,128)(2,1)} %param.10) | copy-start | bytes 2752516
  7.2 298.5 %all-gather.2.cloned.1.call-start = ((), (), s32[]{:S(2)}) async-start(), calls=%async_computation.3 | async-start | bytes 13045760 | tf_op jit(solution)/shard_map/all_gather | solution.py:398
  8.3 10.4 %collective-permute-start = (bf16[28,1792]{1,0:T(8,128)(2,1)S(1)}, bf16[28,1792]{1,0:T(8,128)(2,1)S(1)}, u32[]{:S(2)}, u32[]{:S(2)}) collective-permute-start(bf16[28,1792]{1,0:T(8,128)(2,1)S(1)} %get-tuple-element.44), channel_id=1, source_target_pairs={{0,0},{1,16},{2,1},{3,17},{4,2},{5,18},{6,3},{7,19},{8,4},{9,20},{... | collective-permute-start | bytes 301064 | tf_op jit(solution)/shard_map/ppermute | solution.py:50
  14.5 5.4 %collective-permute-start.1 = (bf16[28,1792]{1,0:T(8,128)(2,1)S(1)}, bf16[28,1792]{1,0:T(8,128)(2,1)S(1)}, u32[]{:S(2)}, u32[]{:S(2)}) collective-permute-start(bf16[28,1792]{1,0:T(8,128)(2,1)S(1)} %get-tuple-element.45), channel_id=1, source_target_pairs={{0,16},{1,0},{2,17},{3,1},{4,18},{5,2},{6,19},{7,3},{8,20},{9,4},{... | collective-permute-start | bytes 301064 | tf_op jit(solution)/shard_map/ppermute | solution.py:51
  24.3 109.8 %copy-start.2 = (bf16[512,3584]{1,0:T(8,128)(2,1)S(1)}, bf16[512,3584]{1,0:T(8,128)(2,1)}, u32[]{:S(2)}) copy-start(bf16[512,3584]{1,0:T(8,128)(2,1)} %passages.1) | copy-start | bytes 11010052
  134.1 9.1 %copy-start.1 = (bf16[128,8,3584]{2,1,0:T(8,128)(2,1)}, bf16[128,8,3584]{2,1,0:T(8,128)(2,1)S(1)}, u32[]{:S(2)}) copy-start(bf16[128,8,3584]{2,1,0:T(8,128)(2,1)S(1)} %all_to_all.19) | copy-start | bytes 22020100
  143.2 3.1 copy-start.6
  146.2 0.8 copy-start.8
  147.0 187.1 %all-to-all-start.1 = ((bf16[128,8,3584]{2,1,0:T(8,128)(2,1)}), bf16[128,8,3584]{2,1,0:T(8,128)(2,1)}, u32[]{:S(2)}, u32[]{:S(2)}) async-start(bf16[128,8,3584]{2,1,0:T(8,128)(2,1)} %bitcast.56), calls=%async_computation.1 | async-start | bytes 14680064 | tf_op jit(solution)/shard_map/all_to_all | solution.py:58
  156.3 7.3 %copy-start.19 = (bf16[3584]{0:T(1024)(128)(2,1)S(1)}, bf16[3584]{0:T(1024)(128)(2,1)}, u32[]{:S(2)}) copy-start(bf16[3584]{0:T(1024)(128)(2,1)} %param.19) | copy-start | bytes 21508
  160.2 0.7 copy-start.16
  164.9 5.1 %copy-start.9 = (f32[1024,128]{1,0:T(8,128)S(1)}, f32[1024,128]{1,0:T(8,128)}, u32[]{:S(2)}) copy-start(f32[1024,128]{1,0:T(8,128)} %copy-done.8) | copy-start | bytes 1572868
  292.5 0.8 copy-start.7
  293.3 0.8 copy-start.12
  296.3 9.4 %copy-start.10 = (bf16[16,3584]{1,0:T(8,128)(2,1)S(1)}, bf16[16,3584]{1,0:T(8,128)(2,1)}, u32[]{:S(2)}) copy-start(bf16[16,3584]{1,0:T(8,128)(2,1)} %up.1) | copy-start | bytes 344068
  296.3 9.4 %copy-start.11 = (bf16[3584,16]{0,1:T(8,128)(2,1)S(1)}, bf16[3584,16]{0,1:T(8,128)(2,1)}, u32[]{:S(2)}) copy-start(bf16[3584,16]{0,1:T(8,128)(2,1)} %param.17) | copy-start | bytes 344068
  305.7 2.0 copy-start.5
  307.7 26.5 %copy-start.13 = (bf16[256,1024]{1,0:T(8,128)(2,1)S(1)}, bf16[256,1024]{1,0:T(8,128)(2,1)}, u32[]{:S(2)}) copy-start(bf16[256,1024]{1,0:T(8,128)(2,1)} %copy-done.12) | copy-start | bytes 1572868
  332.0 1.9 copy-start.3
  334.2 5.3 %copy-start.14 = (f32[256,3584]{1,0:T(8,128)S(1)}, f32[256,3584]{1,0:T(8,128)}, u32[]{:S(2)}) copy-start(f32[256,3584]{1,0:T(8,128)} %fusion.13) | copy-start | bytes 11010052
  339.5 0.7 copy-start.18
  339.5 2.7 copy-start.4
  340.2 3.1 copy-start.15
  352.2 7.6 %copy-start.17 = (f32[128,512]{1,0:T(8,128)S(1)}, f32[128,512]{1,0:T(8,128)}, u32[]{:S(2)}) copy-start(f32[128,512]{1,0:T(8,128)} %copy-done.16) | copy-start | bytes 786436
  352.3 7.6 %copy-start.20 = (s32[128]{0:T(128)S(1)}, s32[128]{0:T(128)}, u32[]{:S(2)}) copy-start(s32[128]{0:T(128)} %param.13) | copy-start | bytes 1540
  355.6 17.5 %all-to-all-start.2 = ((f32[128,1,896]{2,1,0:T(1,128)}), f32[128,1,896]{2,1,0:T(1,128)S(1)}, u32[]{:S(2)}, u32[]{:S(2)}) async-start(f32[128,1,896]{2,1,0:T(1,128)} %copy.67), calls=%async_computation.2 | async-start | bytes 917504 | tf_op jit(solution)/shard_map/all_to_all | solution.py:58
Sparse Core Ops, SparseCore 0:
  20.8 233.0 all-gather.1

commit v3 on v2

--- a/solution.py
+++ b/solution.py
@@ -174,51 +174,6 @@
     )(context, half_weight, residual, down, up)
 
 
-def far_kernel(score_scale, rows, passages, scores, mean, mass):
-    value = score_scale * lax.dot_general(
-        rows[...], passages[...], (((1,), (1,)), ((), ())), preferred_element_type=f32
-    )
-    scores[...] = value
-    peak = jnp.max(value, axis=1, keepdims=True)
-    weights = jnp.exp(value - peak)
-    total = jnp.sum(weights, axis=1, keepdims=True)
-    mass[...] = jnp.broadcast_to(peak + jnp.log(total), mass.shape)
-    inverse = 1.0 / total
-    weights = weights.astype(bf16)
-    tile = 512
-    for start in range(0, mean.shape[1], tile):
-        part = jnp.dot(
-            weights, passages[:, start : start + tile], preferred_element_type=f32
-        )
-        mean[:, start : start + tile] = (part * inverse).astype(bf16)
-
-
-def far_forward(rows, passages, score_scale):
-    count, width = rows.shape
-    passage_count = passages.shape[0]
-    block = 256
-    return pl.pallas_call(
-        functools.partial(far_kernel, score_scale),
-        out_shape=(
-            jax.ShapeDtypeStruct((count, passage_count), f32),
-            jax.ShapeDtypeStruct((count, width), bf16),
-            jax.ShapeDtypeStruct((count, 128), f32),
-        ),
-        grid=(count // block,),
-        in_specs=[
-            pl.BlockSpec((block, width), lambda i: (i, 0)),
-            pl.BlockSpec((passage_count, width), lambda i: (0, 0), pipeline_mode=pl.Buffered(1)),
-        ],
-        out_specs=(
-            pl.BlockSpec((block, passage_count), lambda i: (i, 0)),
-            pl.BlockSpec((block, width), lambda i: (i, 0)),
-            pl.BlockSpec((block, 128), lambda i: (i, 0)),
-        ),
-        compiler_params=pltpu.CompilerParams(vmem_limit_bytes=32 * 1024 * 1024),
-        name="far_forward",
-    )(rows, passages)
-
-
 def torus_place():
     return tuple(lax.axis_index(axis) for axis in PB_PA)
 
@@ -236,17 +191,21 @@
     )
 
 
-def small_exchange_kernel(
-    mass, near_mass, key_column, key_row, mix, log_total, log_arrived,
-    mass_in, log_out, mass_send, mass_recv, log_send, log_recv,
+def far_kernel(
+    score_scale, arrived, passages, near_mass, key_column, key_row, mean, scores, mix, log_total,
+    log_arrived, rows, weights, inverse, means, mass, mass_in, log_out, row_sem, mean_sem,
+    mass_send, mass_recv, log_send, log_recv,
 ):
     place = torus_place()
     own = flat_of(place)
-    peers = mass.shape[0]
-    slot_rows = mass.shape[1]
+    peers, slot_rows, lanes = mass.shape
     all_rows = peers * slot_rows
     hard_count = key_row.shape[0]
     query_count = near_mass.shape[0]
+    width = passages.shape[1]
+    chunks = row_sem.shape[0]
+    block = all_rows // chunks
+    block_peers = peers // chunks
     barrier = pltpu.get_barrier_semaphore()
 
     def greet(j, carry):
@@ -255,7 +214,36 @@
         )
         return carry
 
+    def part(c):
+        return pl.ds(pl.multiple_of(c * block, block), block)
+
+    def came_in(c):
+        return pltpu.make_async_copy(arrived.at[part(c)], rows.at[part(c)], row_sem.at[c])
+
+    def went_out(c):
+        return pltpu.make_async_copy(means.at[part(c)], mean.at[part(c)], mean_sem.at[c])
+
+    for c in range(chunks):
+        came_in(c).start()
     lax.fori_loop(1, peers, greet, 0)
+
+    def score(c, carry):
+        came_in(c).wait()
+        value = score_scale * lax.dot_general(
+            rows[part(c), :], passages[...], (((1,), (1,)), ((), ())),
+            preferred_element_type=f32,
+        )
+        scores[part(c), :] = value
+        peak = jnp.max(value, axis=1, keepdims=True)
+        weight = jnp.exp(value - peak)
+        total = jnp.sum(weight, axis=1, keepdims=True)
+        weights[part(c), :] = weight.astype(bf16)
+        inverse[part(c), :] = 1.0 / total
+        spread = jnp.broadcast_to(peak + jnp.log(total), (block, lanes))
+        mass[pl.ds(c * block_peers, block_peers)] = spread.reshape(block_peers, slot_rows, lanes)
+        return carry
+
+    lax.fori_loop(0, chunks, score, 0)
     pl.semaphore_wait(barrier, peers - 1)
 
     def sends(source, target, send_sem, recv_sem):
@@ -278,6 +266,20 @@
 
     sends(mass, mass_in, mass_send, mass_recv)
     mass_in[own] = mass[own]
+
+    def average(c, carry):
+        weight = weights[part(c), :]
+        scale = inverse[part(c), :]
+        tile = 512
+        for start in range(0, width, tile):
+            value = jnp.dot(
+                weight, passages[:, start : start + tile], preferred_element_type=f32
+            )
+            means[part(c), start : start + tile] = (value * scale).astype(bf16)
+        went_out(c).start()
+        return carry
+
+    lax.fori_loop(0, chunks, average, 0)
     row_ids = lax.broadcasted_iota(jnp.int32, (query_count, all_rows), 1)
     hits = [
         key_column[t * query_count : (t + 1) * query_count, :] == row_ids
@@ -289,8 +291,8 @@
         picks = jnp.where(column_ids == key_row[t : t + 1, :], 1.0, picks)
     filled = jnp.sum(picks, axis=1, keepdims=True) > 0.0
     every(mass, mass_in, mass_send, mass_recv).wait_recv()
-    came = mass_in[...].reshape(all_rows, mass.shape[2])
-    masses = [jnp.broadcast_to(near_mass[...], (query_count, came.shape[1]))]
+    came = mass_in[...].reshape(all_rows, lanes)
+    masses = [jnp.broadcast_to(near_mass[...], (query_count, lanes))]
     for hit in hits:
         masses.append(
             jnp.dot(
@@ -320,38 +322,53 @@
     mix[:query_count, :] = high
     mix[query_count:, :] = (shares - high.astype(f32)).astype(bf16)
     every(mass, mass_in, mass_send, mass_recv).wait_send()
+    for c in range(chunks):
+        went_out(c).wait()
     last = every(log_out, log_arrived, log_send, log_recv)
     last.wait_send()
     last.wait_recv()
 
 
-def small_exchange(mass, near_mass, key):
-    peers, slot_rows, lanes = mass.shape
+def far_forward(arrived, passages, near_mass, key, peers, score_scale):
+    all_rows, width = arrived.shape
+    passage_count = passages.shape[0]
     hard_count, query_count = key.shape
+    lanes, chunks = 128, 4
+    small = (peers, all_rows // peers, lanes)
     vmem = pl.BlockSpec(memory_space=pltpu.VMEM)
+    hbm = pl.BlockSpec(memory_space=pl.ANY)
+    dma = pltpu.SemaphoreType.DMA
     return pl.pallas_call(
-        small_exchange_kernel,
+        functools.partial(far_kernel, score_scale),
         out_shape=(
-            jax.ShapeDtypeStruct((2 * query_count, peers * slot_rows), bf16),
+            jax.ShapeDtypeStruct((all_rows, width), bf16),
+            jax.ShapeDtypeStruct((all_rows, passage_count), f32),
+            jax.ShapeDtypeStruct((2 * query_count, all_rows), bf16),
             jax.ShapeDtypeStruct((query_count, lanes), f32),
-            jax.ShapeDtypeStruct(mass.shape, f32),
+            jax.ShapeDtypeStruct(small, f32),
         ),
-        in_specs=[vmem] * 4,
-        out_specs=(vmem, vmem, vmem),
+        in_specs=[hbm, vmem, vmem, vmem, vmem],
+        out_specs=(hbm, vmem, vmem, vmem, vmem),
         scratch_shapes=[
-            pltpu.VMEM(mass.shape, f32),
-            pltpu.VMEM(mass.shape, f32),
-            pltpu.SemaphoreType.DMA(()),
-            pltpu.SemaphoreType.DMA(()),
-            pltpu.SemaphoreType.DMA(()),
-            pltpu.SemaphoreType.DMA(()),
+            pltpu.VMEM((all_rows, width), bf16),
+            pltpu.VMEM((all_rows, passage_count), bf16),
+            pltpu.VMEM((all_rows, 1), f32),
+            pltpu.VMEM((all_rows, width), bf16),
+            pltpu.VMEM(small, f32),
+            pltpu.VMEM(small, f32),
+            pltpu.VMEM(small, f32),
+            dma((chunks,)),
+            dma((chunks,)),
+            dma(()),
+            dma(()),
+            dma(()),
+            dma(()),
         ],
         compiler_params=pltpu.CompilerParams(
-            collective_id=2, has_side_effects=True, vmem_limit_bytes=24 * 1024 * 1024
+            collective_id=2, has_side_effects=True, vmem_limit_bytes=44 * 1024 * 1024
         ),
-        cost_estimate=pl.CostEstimate(flops=1000, bytes_accessed=1000, transcendentals=0),
-        name="small_exchange",
-    )(mass, near_mass[:, None], key.reshape(-1)[:, None], key)
+        name="far_forward",
+    )(arrived, passages, near_mass[:, None], key.reshape(-1)[:, None], key)
 
 
 def local(
@@ -406,12 +423,11 @@
         jnp.concatenate([near_exp.astype(bf16), positive_hot.astype(bf16)], axis=0), passages
     )
 
-    far_scores, far_mean, far_mass = far_forward(arrived, passages, score_scale)
+    far_mean, far_scores, mix_parts, log_total, log_arrived = far_forward(
+        arrived, passages, near_mass, key, device_count, score_scale
+    )
     returned = exchange(far_mean.reshape(device_count, slot_rows, MODEL_WIDTH))
     returned = returned.reshape(-1, MODEL_WIDTH)
-    mix_parts, log_total, log_arrived = small_exchange(
-        far_mass.reshape(device_count, slot_rows, -1), near_mass, key
-    )
     log_total = log_total[:, 0]
     log_arrived = log_arrived.reshape(all_rows, -1)[:, :1]
     near_share = jnp.exp(near_mass - log_total)

time: 383 us -> 339 us (0.89)
  waiting for transfers between devices: 10.2 us -> 144 us
  blocking collectives: 110 us -> 0 us
  Pallas kernels: 156 us -> 73.1 us
  starting transfers between devices: 20.8 us -> 38.4 us
    all_to_all x2 -> x3, waiting for transfers between devices: 5.86 us -> 140 us  [exchange(): return lax.all_to_all(array, PB_PA, split_axis=0, concat_axis=0, tiled=True)]
    pallas_call x1 -> x0, Pallas kernels: 122 us -> none  [small_exchange(): pl.pallas_call(small_exchange_kernel, out_shape=(jax.ShapeDtypeStruct((2...]
    all_to_all x1 -> x0, blocking collectives: 110 us -> none  [exchange(): return lax.all_to_all(array, PB_PA, split_axis=0, concat_axis=0, tiled=True)]
    pallas_call x1, Pallas kernels: 9.09 us -> 48 us  [far_forward(): pl.pallas_call(functools.partial(far_kernel, score_scale), out_shape=(jax...]
    all_to_all x2 -> x3, starting transfers between devices: 13.5 us -> 31.1 us  [exchange(): return lax.all_to_all(array, PB_PA, split_axis=0, concat_axis=0, tiled=True)]
    unnamed x44 -> x34, local copies, waits for them, and re-layouts: 14 us -> 12.2 us
  transfers between devices with their start and end apart: 5 -> 6, of which waited for: 3 -> 5; matrix products, arithmetic and copies ran while one was open for 9% -> 10% of each run, Pallas kernels for 41% -> 22%
where the time goes in v3:
time: 339 us; the launch traced here: 338 us
  waiting for transfers between devices  144 us (42%)
  Pallas kernels  73.1 us (22%)
  matrix products  43.7 us (13%)
  starting transfers between devices  38.4 us (11%)
  local copies, waits for them, and re-layouts  19.8 us (6%)
  between operations  14.5 us (4%)
  other arithmetic  4.09 us (1%)
    all_to_all x3, waiting for transfers between devices, exchange(): return lax.all_to_all(array, PB_PA, split_axis=0, concat_axis=0, tiled=True)  140 us
    pallas_call x1, Pallas kernels, far_forward(): pl.pallas_call(functools.partial(far_kernel, score_scale), out_shape=(jax...  48 us
    all_to_all x3, starting transfers between devices, exchange(): return lax.all_to_all(array, PB_PA, split_axis=0, concat_axis=0, tiled=True)  31.1 us
    pallas_call x1, Pallas kernels, layer_forward(): pl.pallas_call(layer_forward_kernel, out_shape=(jax.ShapeDtypeStruct((tok...  25.2 us
    dot_general x5, matrix products, dot(): return jnp.dot(a, b, preferred_element_type=f32, **kw)  15.1 us
    unnamed x34, local copies, waits for them, and re-layouts  12.2 us
    dot_general x1, matrix products, local(): lax.dot_general(far_weight, arrived, product_dims, preferred_element_type...  9.38 us
    dot_general x1, matrix products, local(): lax.dot_general(near_weight, queries, product_dims, preferred_element_typ...  7.38 us
  transfers between devices with their start and end apart: 6, of which 5 were waited for; matrix products, arithmetic and copies ran while one was open for 10% of the time, Pallas kernels for 22%

profile of v3, /device:TPU:1, one launch (start us, length us, event | category | flops | bytes accessed | tf_op | source)
XLA Modules:
  0.0 337.6 jit_solution(9690360389756447156)
XLA Ops:
  7.2 1.0 broadcast_select_fusion.1
  8.3 6.2 %collective-permute-start = (bf16[28,1792]{1,0:T(8,128)(2,1)S(1)}, bf16[28,1792]{1,0:T(8,128)(2,1)S(1)}, u32[]{:S(2)}, u32[]{:S(2)}) collective-permute-start(bf16[28,1792]{1,0:T(8,128)(2,1)S(1)} %get-tuple-element.42), channel_id=1, source_target_pairs={{0,0},{1,16},{2,1},{3,17},{4,2},{5,18},{6,3},{7,19},{8,4},{9,20},{... | collective-permute-start | bytes 301064 | tf_op jit(solution)/shard_map/ppermute | solution.py:50
  14.5 1.1 collective-permute-start.1
  15.6 3.1 collective-permute-done
  18.7 1.2 collective-permute-done.1
  22.2 5.1 %convolution_bitcast_fusion = bf16[128,8,3584]{2,1,0:T(8,128)(2,1)} fusion(bf16[128,3584]{1,0:T(8,128)(2,1)S(1)} %copy-done, s32[128]{0:T(128)S(1)} %get-tuple-element.47, s32[128]{0:T(128)S(1)} %get-tuple-element.48, s32[128]{0:T(128)S(1)} %get-tuple-element.49, s32[128]{0:T(128)S(1)} %get-tuple-element.46), kind=kOutput, calls=%fused_computation.1 | convolution fusion | flops 940441600 | bytes 8259584 | tf_op jit(solution)/shard_map/dot_general | solution.py:411
  27.3 14.8 %all-to-all-start = ((bf16[128,8,3584]{2,1,0:T(8,128)(2,1)}), bf16[128,8,3584]{2,1,0:T(8,128)(2,1)}, u32[]{:S(2)}, u32[]{:S(2)}) async-start(bf16[128,8,3584]{2,1,0:T(8,128)(2,1)} %convolution_bitcast_fusion), calls=%async_computation | async-start | bytes 14680064 | tf_op jit(solution)/shard_map/all_to_all | solution.py:58
  42.4 3.5 %fusion.47 = (f32[128]{0:T(128)S(1)}, f32[128,512]{1,0:T(8,128)S(1)}) fusion(bf16[128,3584]{1,0:T(8,128)(2,1)S(1)} %copy-done, bf16[512,3584]{1,0:T(8,128)(2,1)} %passages.1), kind=kOutput, calls=%fused_computation.95 | convolution fusion | flops 469892992 | bytes 4850176 | tf_op jit(solution)/shard_map/dot_general | solution.py:29
  47.0 93.1 %all-to-all-done = bf16[128,8,3584]{2,1,0:T(8,128)(2,1)} async-done(((bf16[128,8,3584]{2,1,0:T(8,128)(2,1)}), bf16[128,8,3584]{2,1,0:T(8,128)(2,1)}, u32[]{:S(2)}, u32[]{:S(2)}) %all-to-all-start) | async-done | bytes 7340064 | tf_op jit(solution)/shard_map/all_to_all | solution.py:58
  140.2 2.0 copy-done.1
  142.2 48.0 %far_forward.1 = (bf16[1024,3584]{1,0:T(8,128)(2,1)}, f32[1024,512]{1,0:T(8,128)S(1)}, bf16[256,1024]{1,0:T(8,128)(2,1)S(1)}, f32[128,128]{1,0:T(8,128)S(1)}, f32[128,8,128]{2,1,0:T(8,128)S(1)}) custom-call(bf16[1024,3584]{1,0:T(8,128)(2,1)} %bitcast.6.arrived, bf16[512,3584]{1,0:T(8,128)(2,1)S(1)} %copy-done.1, f32[128,1]{1,0:T(8,128)S(1)} %add.94.near_mass, ...), custom_call_target="tpu_custom_call" | custom-call | tf_op jit(solution)/shard_map/far_forward/pallas_call | solution.py:341
  191.0 0.8 copy-done.8
  191.8 6.3 %all-to-all-start.1 = ((bf16[128,8,3584]{2,1,0:T(8,128)(2,1)}), bf16[128,8,3584]{2,1,0:T(8,128)(2,1)}, u32[]{:S(2)}, u32[]{:S(2)}) async-start(bf16[128,8,3584]{2,1,0:T(8,128)(2,1)} %bitcast.56), calls=%async_computation.1 | async-start | bytes 14680064 | tf_op jit(solution)/shard_map/all_to_all | solution.py:58
  198.3 5.1 %fusion.13 = f32[256,3584]{1,0:T(8,128)} fusion(bf16[512,3584]{1,0:T(8,128)(2,1)} %passages.1, bf16[128,512]{1,0:T(8,128)(2,1)S(1)} %fusion.20, bf16[128,512]{1,0:T(8,128)(2,1)S(1)} %get-tuple-element.39), kind=kOutput, calls=%fused_computation.27 | convolution fusion | flops 940048384 | bytes 7602176 | tf_op jit(solution)/shard_map/dot_general | solution.py:29
  203.4 1.2 copy.68
  204.8 9.4 %fusion.4 = f32[512,3584]{1,0:T(8,128)} fusion(f32[1024,512]{1,0:T(8,128)S(1)} %get-tuple-element.25, f32[1024]{0:T(1024)S(1)} %bitcast.57, bf16[128,8,3584]{2,1,0:T(8,128)(2,1)} %all-to-all-done), kind=kOutput, calls=%fused_computation.13 | convolution fusion | flops 3759144960 | bytes 16781312 | tf_op jit(solution)/shard_map/dot_general | solution.py:441
  214.2 2.0 copy-done.4
  216.2 25.2 %layer_forward.1 = (bf16[512,3584]{1,0:T(8,128)(2,1)S(1)}, f32[512,16]{1,0:T(8,128)S(1)}, f32[512,16]{1,0:T(8,128)S(1)}, f32[512,1]{1,0:T(8,128)S(1)}) custom-call(bf16[512,3584]{1,0:T(8,128)(2,1)S(1)} %copy-done.4, bf16[3584,1792]{1,0:T(8,128)(2,1)} %all-gather.2.cloned.1.call-done.half_weight, bf16[512,3584]{1,0:T(8,128)(2,1)} %residual.1, ...), custom_call_target="tpu_custom_call" | custom-call | flops 1000 | bytes 1000 | tf_op jit(solution)/shard_map/layer_forward/pallas_call | solution.py:151
  241.4 1.9 copy-done.2
  243.6 40.7 %all-to-all-done.1 = bf16[128,8,3584]{2,1,0:T(8,128)(2,1)} async-done(((bf16[128,8,3584]{2,1,0:T(8,128)(2,1)}), bf16[128,8,3584]{2,1,0:T(8,128)(2,1)}, u32[]{:S(2)}, u32[]{:S(2)}) %all-to-all-start.1) | async-done | bytes 7340064 | tf_op jit(solution)/shard_map/all_to_all | solution.py:58
  284.4 5.3 %fusion.48 = f32[256,3584]{1,0:T(8,128)S(1)} fusion(bf16[256,1024]{1,0:T(8,128)(2,1)S(1)} %copy-done.9, bf16[1024,3584]{1,0:T(8,128)(2,1)} %bitcast.11), kind=kOutput, calls=%fused_computation.96 | convolution fusion | flops 1879048192 | bytes 11534336 | tf_op jit(solution)/shard_map/dot_general | solution.py:29
  290.5 1.9 copy-done.3
  292.4 1.1 fusion.3
  294.1 2.6 fusion.49
  296.7 1.3 concatenate.16
  298.4 1.3 fusion.27
  299.7 2.7 fusion
  302.4 1.3 concatenate.17
  304.5 1.3 copy.67
  305.8 10.0 %all-to-all-start.2 = ((f32[128,1,896]{2,1,0:T(1,128)}), f32[128,1,896]{2,1,0:T(1,128)S(1)}, u32[]{:S(2)}, u32[]{:S(2)}) async-start(f32[128,1,896]{2,1,0:T(1,128)} %copy.67), calls=%async_computation.2 | async-start | bytes 917504 | tf_op jit(solution)/shard_map/all_to_all | solution.py:58
  315.8 7.4 %add_multiply_fusion = f32[512,3584]{1,0:T(8,128)} fusion(f32[512,3584]{1,0:T(8,128)} %fusion.4, bf16[128,3584]{1,0:T(8,128)(2,1)S(1)} %copy-done, f32[128,512]{1,0:T(8,128)S(1)} %copy-done.13, f32[128]{0:T(128)S(1)} %get-tuple-element.36, s32[128]{0:T(128)S(1)} %copy-done.15), kind=kOutput, calls=%fused_computation | convolution fusion | flops 473759744 | bytes 15860736 | tf_op jit(solution)/shard_map/dot_general | solution.py:442
  323.2 5.9 %all-to-all-done.2 = f32[128,1,896]{2,1,0:T(1,128)S(1)} async-done(((f32[128,1,896]{2,1,0:T(1,128)}), f32[128,1,896]{2,1,0:T(1,128)S(1)}, u32[]{:S(2)}, u32[]{:S(2)}) %all-to-all-start.2) | async-done | bytes 458784 | tf_op jit(solution)/shard_map/all_to_all | solution.py:58
  (75 shorter events, 9.4 us)
Async XLA Ops:
  7.2 15.0 %copy-start = (bf16[128,3584]{1,0:T(8,128)(2,1)S(1)}, bf16[128,3584]{1,0:T(8,128)(2,1)}, u32[]{:S(2)}) copy-start(bf16[128,3584]{1,0:T(8,128)(2,1)} %param.10) | copy-start | bytes 2752516
  7.2 207.0 %all-gather.2.cloned.1.call-start = ((), (), s32[]{:S(2)}) async-start(), calls=%async_computation.3 | async-start | bytes 13045760 | tf_op jit(solution)/shard_map/all_gather | solution.py:415
  8.3 10.4 %collective-permute-start = (bf16[28,1792]{1,0:T(8,128)(2,1)S(1)}, bf16[28,1792]{1,0:T(8,128)(2,1)S(1)}, u32[]{:S(2)}, u32[]{:S(2)}) collective-permute-start(bf16[28,1792]{1,0:T(8,128)(2,1)S(1)} %get-tuple-element.42), channel_id=1, source_target_pairs={{0,0},{1,16},{2,1},{3,17},{4,2},{5,18},{6,3},{7,19},{8,4},{9,20},{... | collective-permute-start | bytes 301064 | tf_op jit(solution)/shard_map/ppermute | solution.py:50
  14.5 5.4 %collective-permute-start.1 = (bf16[28,1792]{1,0:T(8,128)(2,1)S(1)}, bf16[28,1792]{1,0:T(8,128)(2,1)S(1)}, u32[]{:S(2)}, u32[]{:S(2)}) collective-permute-start(bf16[28,1792]{1,0:T(8,128)(2,1)S(1)} %get-tuple-element.43), channel_id=1, source_target_pairs={{0,16},{1,0},{2,17},{3,1},{4,18},{5,2},{6,19},{7,3},{8,20},{9,4},{... | collective-permute-start | bytes 301064 | tf_op jit(solution)/shard_map/ppermute | solution.py:51
  27.3 112.9 %all-to-all-start = ((bf16[128,8,3584]{2,1,0:T(8,128)(2,1)}), bf16[128,8,3584]{2,1,0:T(8,128)(2,1)}, u32[]{:S(2)}, u32[]{:S(2)}) async-start(bf16[128,8,3584]{2,1,0:T(8,128)(2,1)} %convolution_bitcast_fusion), calls=%async_computation | async-start | bytes 14680064 | tf_op jit(solution)/shard_map/all_to_all | solution.py:58
  45.9 0.7 copy-start.12
  140.2 2.0 copy-start.1
  190.2 0.8 copy-start.5
  191.0 0.8 copy-start.8
  191.8 6.4 %copy-start.14 = (bf16[3584]{0:T(1024)(128)(2,1)S(1)}, bf16[3584]{0:T(1024)(128)(2,1)}, u32[]{:S(2)}) copy-start(bf16[3584]{0:T(1024)(128)(2,1)} %param.19) | copy-start | bytes 21508
  191.8 6.4 %copy-start.15 = (s32[128]{0:T(128)S(1)}, s32[128]{0:T(128)}, u32[]{:S(2)}) copy-start(s32[128]{0:T(128)} %param.13) | copy-start | bytes 1540
  191.8 92.6 %all-to-all-start.1 = ((bf16[128,8,3584]{2,1,0:T(8,128)(2,1)}), bf16[128,8,3584]{2,1,0:T(8,128)(2,1)}, u32[]{:S(2)}, u32[]{:S(2)}) async-start(bf16[128,8,3584]{2,1,0:T(8,128)(2,1)} %bitcast.56), calls=%async_computation.1 | async-start | bytes 14680064 | tf_op jit(solution)/shard_map/all_to_all | solution.py:58
  204.8 9.4 %copy-start.6 = (bf16[16,3584]{1,0:T(8,128)(2,1)S(1)}, bf16[16,3584]{1,0:T(8,128)(2,1)}, u32[]{:S(2)}) copy-start(bf16[16,3584]{1,0:T(8,128)(2,1)} %up.1) | copy-start | bytes 344068
  204.8 9.4 %copy-start.7 = (bf16[3584,16]{0,1:T(8,128)(2,1)S(1)}, bf16[3584,16]{0,1:T(8,128)(2,1)}, u32[]{:S(2)}) copy-start(bf16[3584,16]{0,1:T(8,128)(2,1)} %param.17) | copy-start | bytes 344068
  214.2 2.0 copy-start.4
  216.2 68.2 %copy-start.9 = (bf16[256,1024]{1,0:T(8,128)(2,1)S(1)}, bf16[256,1024]{1,0:T(8,128)(2,1)}, u32[]{:S(2)}) copy-start(bf16[256,1024]{1,0:T(8,128)(2,1)} %copy-done.8) | copy-start | bytes 1572868
  241.4 1.9 copy-start.2
  284.4 5.3 %copy-start.10 = (f32[256,3584]{1,0:T(8,128)S(1)}, f32[256,3584]{1,0:T(8,128)}, u32[]{:S(2)}) copy-start(f32[256,3584]{1,0:T(8,128)} %fusion.13) | copy-start | bytes 11010052
  289.7 2.7 copy-start.3
  290.3 3.2 copy-start.11
  302.4 13.3 %copy-start.13 = (f32[128,512]{1,0:T(8,128)S(1)}, f32[128,512]{1,0:T(8,128)}, u32[]{:S(2)}) copy-start(f32[128,512]{1,0:T(8,128)} %copy-done.12) | copy-start | bytes 786436
  305.8 23.2 %all-to-all-start.2 = ((f32[128,1,896]{2,1,0:T(1,128)}), f32[128,1,896]{2,1,0:T(1,128)S(1)}, u32[]{:S(2)}, u32[]{:S(2)}) async-start(f32[128,1,896]{2,1,0:T(1,128)} %copy.67), calls=%async_computation.2 | async-start | bytes 917504 | tf_op jit(solution)/shard_map/all_to_all | solution.py:58
Sparse Core Ops, SparseCore 0:
  20.8 175.3 all-gather.1

commit v4 on v3

--- a/solution.py
+++ b/solution.py
@@ -371,6 +371,239 @@
     )(arrived, passages, near_mass[:, None], key.reshape(-1)[:, None], key)
 
 
+def tail_kernel(
+    gradient_scale, returned, mix, near_part, norm, hidden, context, up, narrow, hidden_up, inverse,
+    gradient, piece, rows, hid, ctx, grad, scaled, products, scaled_up, terms, first, part, second,
+    row_sem, hid_sem, ctx_sem, grad_sem, send1, recv1, send2, recv2,
+):
+    place = torus_place()
+    own = flat_of(place)
+    lane_group = place[3]
+    column = own // 4
+    peers = 128
+    tiles = row_sem.shape[0]
+    width = terms.shape[2] * terms.shape[0]
+    tile = width // tiles
+    lanes = terms.shape[2]
+    count = terms.shape[0]
+    columns = first.shape[0]
+    per_tile = tile // lanes
+    query_count = gradient.shape[0]
+    rerun = scaled.shape[0]
+    rank = up.shape[0]
+    tokens = narrow.shape[0]
+    exact = dict(precision=lax.Precision.HIGHEST, preferred_element_type=f32)
+    over_rows = (((0,), (0,)), ((), ()))
+    over_lanes = (((1,), (1,)), ((), ()))
+
+    def at(j):
+        return pl.ds(pl.multiple_of(j * tile, tile), tile)
+
+    def came_in(j):
+        return pltpu.make_async_copy(returned.at[:, at(j)], rows.at[:, at(j)], row_sem.at[j])
+
+    hid_in = pltpu.make_async_copy(hidden, hid, hid_sem)
+    ctx_in = pltpu.make_async_copy(context, ctx, ctx_sem)
+    came_in(0).start()
+    hid_in.start()
+    for j in range(1, tiles):
+        came_in(j).start()
+    ctx_in.start()
+    barrier = pltpu.get_barrier_semaphore()
+
+    def greet(j, carry):
+        pl.semaphore_signal(
+            barrier, inc=1, device_id=torus_peer(place, j), device_id_type=MESH
+        )
+        return carry
+
+    lax.fori_loop(1, peers, greet, 0)
+    products[...] = jnp.zeros_like(products)
+    scaled_up[...] = jnp.zeros_like(scaled_up)
+    hid_in.wait()
+
+    def mixing(j, carry):
+        came_in(j).wait()
+        both = jnp.dot(mix[...], rows[:, at(j)], preferred_element_type=f32)
+        value = gradient_scale * (both[:query_count] + both[query_count:] + near_part[:, at(j)])
+        grad[:, at(j)] = value
+        spread = norm[:, at(j)] * (value[:rerun] / TQ)
+        scaled[:, at(j)] = spread
+        products[...] += lax.dot_general(
+            hid[:, at(j)], spread.astype(bf16), over_lanes, preferred_element_type=f32
+        )
+        scaled_up[...] += lax.dot_general(spread, up[:, at(j)].astype(f32), over_lanes, **exact)
+        return carry
+
+    lax.fori_loop(0, tiles, mixing, 0)
+    gradient_out = pltpu.make_async_copy(grad, gradient, grad_sem)
+    gradient_out.start()
+
+    token_query = lax.broadcasted_iota(jnp.int32, (tokens, rerun), 0) // TQ
+    of_query = token_query == lax.broadcasted_iota(jnp.int32, (tokens, rerun), 1)
+    hot = jnp.where(of_query, 1.0, 0.0)
+    mean = jnp.sum(jnp.where(of_query, products[...], 0.0), axis=1, keepdims=True) / width
+    rms = inverse[...]
+    slope = rms * rms * rms * mean
+    spread_up = jnp.dot(hot, scaled_up[...], **exact)
+    grad_narrow = (adapter_scale * (rms * spread_up - slope * hidden_up[...])).astype(bf16)
+    weighted = (slope * narrow[...]).astype(bf16)
+    sums = lax.dot_general(hot, rms * narrow[...], over_rows, **exact)
+    ctx_in.wait()
+
+    def products_of(j, carry):
+        down = lax.dot_general(
+            grad_narrow, ctx[:, at(j)], over_rows, preferred_element_type=f32
+        ) / RERUN_QUERIES
+        up_part = (adapter_scale / RERUN_QUERIES) * (
+            lax.dot_general(sums, scaled[:, at(j)], over_rows, **exact)
+            - lax.dot_general(weighted, hid[:, at(j)], over_rows, preferred_element_type=f32)
+        )
+        for k in range(per_tile):
+            terms[j * per_tile + k, :rank, :] = down[:, k * lanes : (k + 1) * lanes]
+            terms[j * per_tile + k, rank:, :] = up_part[:, k * lanes : (k + 1) * lanes]
+        return carry
+
+    lax.fori_loop(0, tiles, products_of, 0)
+    pl.semaphore_wait(barrier, peers - 1)
+
+    def stage1(j):
+        to = (j // 8, lax.rem(j // 4, 2), lax.rem(j, 4), lane_group)
+        return pltpu.make_async_remote_copy(
+            terms.at[j], first.at[column], send1, recv1, device_id=to, device_id_type=MESH
+        )
+
+    def start1(j, carry):
+        @pl.when(j != column)
+        def _():
+            stage1(j).start()
+
+        return carry
+
+    lax.fori_loop(0, count, start1, 0)
+    gathers = column < count
+    base = (lanes * column) // 28
+    last = (lanes * column + lanes - 1) // 28
+    tile0 = (28 * own) // lanes
+    tile1 = (28 * own + 27) // lanes
+
+    def sized(buffer, n, send_sem, recv_sem):
+        piece_of = buffer.at[pl.ds(0, n)]
+        return pltpu.make_async_remote_copy(
+            piece_of, piece_of, send_sem, recv_sem,
+            device_id=torus_peer(place, 1), device_id_type=MESH,
+        )
+
+    @pl.when(tile0 == tile1)
+    def _():
+        second[1] = jnp.zeros(second.shape[1:], f32)
+
+    def stage2(i):
+        e = base + i
+        slot = column - (28 * e) // lanes
+        to = (e // 32, lax.rem(e // 16, 2), lax.rem(e // 4, 4), lax.rem(e, 4))
+        return pltpu.make_async_remote_copy(
+            part, second.at[slot, lane_group], send2.at[i], recv2.at[slot, lane_group],
+            device_id=to, device_id_type=MESH,
+        )
+
+    @pl.when(gathers)
+    def _():
+        first[column] = terms[column]
+        sized(first, columns - 1, send1, recv1).wait_recv()
+        part[...] = jnp.sum(first[...], axis=0)
+        for i in range(6):
+            e = base + i
+
+            @pl.when((e <= last) & (e != own))
+            def _():
+                stage2(i).start()
+
+            @pl.when((e <= last) & (e == own))
+            def _():
+                second[column - tile0, lane_group] = part[...]
+
+        sized(terms, count - 1, send1, recv1).wait_send()
+
+    @pl.when(column >= count)
+    def _():
+        sized(terms, count, send1, recv1).wait_send()
+
+    for slot in range(2):
+        from_tile = tile0 + slot
+        for b in range(4):
+            @pl.when((from_tile <= tile1) & ((from_tile != column) | (lane_group != b)))
+            def _():
+                pltpu.make_async_remote_copy(
+                    part, second.at[slot, b], send2.at[0], recv2.at[slot, b],
+                    device_id=torus_peer(place, 1), device_id_type=MESH,
+                ).wait_recv()
+
+    left = jnp.sum(second[0], axis=0)
+    right = jnp.sum(second[1], axis=0)
+    offset = 28 * own - lanes * tile0
+    source = lax.broadcasted_iota(jnp.int32, (lanes, lanes), 0)
+    target = lax.broadcasted_iota(jnp.int32, (lanes, lanes), 1) + offset
+    piece[...] = jnp.dot(left, jnp.where(source == target, 1.0, 0.0), **exact) + jnp.dot(
+        right, jnp.where(source + lanes == target, 1.0, 0.0), **exact
+    )
+
+    @pl.when(gathers)
+    def _():
+        for i in range(6):
+            e = base + i
+
+            @pl.when((e <= last) & (e != own))
+            def _():
+                stage2(i).wait_send()
+
+    gradient_out.wait()
+
+
+def tail(returned, mix, near_part, norm, hidden, context, up, narrow, hidden_up, inverse, scale):
+    all_rows, width = returned.shape
+    query_count = near_part.shape[0]
+    tokens, rank = narrow.shape
+    tiles, lanes, rerun = 7, 128, RERUN_QUERIES
+    vmem = pl.BlockSpec(memory_space=pltpu.VMEM)
+    hbm = pl.BlockSpec(memory_space=pl.ANY)
+    dma = pltpu.SemaphoreType.DMA
+    return pl.pallas_call(
+        functools.partial(tail_kernel, scale),
+        out_shape=(
+            jax.ShapeDtypeStruct((query_count, width), f32),
+            jax.ShapeDtypeStruct((2 * rank, lanes), f32),
+        ),
+        in_specs=[hbm, vmem, vmem, vmem, hbm, hbm, vmem, vmem, vmem, vmem],
+        out_specs=(hbm, vmem),
+        scratch_shapes=[
+            pltpu.VMEM((all_rows, width), bf16),
+            pltpu.VMEM((tokens, width), bf16),
+            pltpu.VMEM((tokens, width), bf16),
+            pltpu.VMEM((query_count, width), f32),
+            pltpu.VMEM((rerun, width), f32),
+            pltpu.VMEM((tokens, rerun), f32),
+            pltpu.VMEM((rerun, rank), f32),
+            pltpu.VMEM((width // lanes, 2 * rank, lanes), f32),
+            pltpu.VMEM((32, 2 * rank, lanes), f32),
+            pltpu.VMEM((2 * rank, lanes), f32),
+            pltpu.VMEM((2, 4, 2 * rank, lanes), f32),
+            dma((tiles,)),
+            dma(()),
+            dma(()),
+            dma(()),
+            dma(()),
+            dma(()),
+            dma((6,)),
+            dma((2, 4)),
+        ],
+        compiler_params=pltpu.CompilerParams(
+            collective_id=3, has_side_effects=True, vmem_limit_bytes=44 * 1024 * 1024
+        ),
+        name="tail",
+    )(returned, mix, near_part, norm, hidden, context, up, narrow, hidden_up, inverse)
+
+
 def local(
     queries,
     passages,
@@ -444,51 +677,32 @@
     hidden_low, narrow, hidden_up, inverse_rms = layer_forward(
         context, half_weight, residual, adapter_down_weight.T, adapter_up_weight
     )
-    token_query = jnp.arange(context.shape[0], dtype=jnp.int32) // TQ
-    of_query = token_query[:, None] == jnp.arange(RERUN_QUERIES, dtype=jnp.int32)[None, :]
-    narrow_sums = jnp.sum(
-        (inverse_rms * narrow).reshape(RERUN_QUERIES, TQ, -1), axis=1
-    )
-
-    returned, hidden_low, hidden_up, inverse_rms, narrow_sums, far_grad = (
-        lax.optimization_barrier(
-            (returned, hidden_low, hidden_up, inverse_rms, narrow_sums, far_grad)
-        )
-    )
-    far_part = dot(mix_parts, returned)
-    query_gradient = (loss_scale * score_scale) * (
-        far_part[:query_count] + far_part[query_count:] + near_part
-    )
-
     grad_passages = loss_scale * score_scale * (far_grad + near_grad)
 
-    scaled = final_norm_weight.astype(f32)[None, :] * (query_gradient[:RERUN_QUERIES] / TQ)
-    products = dot(hidden_low, scaled.astype(bf16).T)
-    mean = jnp.sum(jnp.where(of_query, products, 0.0), axis=1, keepdims=True) / MODEL_WIDTH
-    slope = inverse_rms**3 * mean
-    scaled_up = dot(scaled, adapter_up_weight.astype(f32).T, precision=lax.Precision.HIGHEST)
-    spread_up = jnp.broadcast_to(
-        scaled_up[:, None, :], (RERUN_QUERIES, TQ, scaled_up.shape[1])
-    ).reshape(context.shape[0], -1)
-    grad_narrow = (adapter_scale * (inverse_rms * spread_up - slope * hidden_up)).astype(bf16)
-    down_term = lax.dot_general(grad_narrow, context, product_dims, preferred_element_type=f32)
-    weighted = (slope * narrow).astype(bf16)
-    up_term = adapter_scale * (
-        lax.dot_general(
-            narrow_sums,
-            scaled,
-            product_dims,
-            precision=lax.Precision.HIGHEST,
-            preferred_element_type=f32,
-        )
-        - lax.dot_general(weighted, hidden_low, product_dims, preferred_element_type=f32)
-    )
-    terms = jnp.concatenate([down_term, up_term], axis=0) / RERUN_QUERIES
+    returned, near_part, hidden_low, grad_passages = lax.optimization_barrier(
+        (returned, near_part, hidden_low, grad_passages)
+    )
+    query_gradient, sums = tail(
+        returned,
+        mix_parts,
+        near_part,
+        final_norm_weight.astype(f32)[None, :],
+        hidden_low,
+        context,
+        adapter_up_weight,
+        narrow,
+        hidden_up,
+        inverse_rms,
+        loss_scale * score_scale,
+    )
     rank = narrow.shape[1]
     columns = MODEL_WIDTH // device_count
-    pieces = jnp.transpose(terms.reshape(2 * rank, device_count, columns), (1, 0, 2))
-    sums = jnp.sum(exchange(pieces.reshape(device_count, -1)), axis=0).reshape(2 * rank, columns)
-    return (query_gradient, grad_passages, sums[:rank].T, sums[rank:])
+    return (
+        query_gradient,
+        grad_passages,
+        sums[:rank, :columns].T,
+        sums[rank:, :columns],
+    )
 
 
 def solution(mesh):

time: 339 us -> 327 us (0.965)
  Pallas kernels: 73.1 us -> 100 us
  matrix products: 43.7 us -> 24.6 us
  starting transfers between devices: 38.4 us -> 29 us
  waiting for transfers between devices: 144 us -> 135 us
    pallas_call x0 -> x1, Pallas kernels: none -> 28 us  [tail(): pl.pallas_call(functools.partial(tail_kernel, scale), out_shape=(jax.Shap...]
    all_to_all x3 -> x2, waiting for transfers between devices: 140 us -> 130 us  [exchange(): return lax.all_to_all(array, PB_PA, split_axis=0, concat_axis=0, tiled=True)]
    all_to_all x3 -> x2, starting transfers between devices: 31.1 us -> 21.7 us  [exchange(): return lax.all_to_all(array, PB_PA, split_axis=0, concat_axis=0, tiled=True)]
    dot_general x3 -> x0, matrix products: 6.7 us -> none  [the longest x1 2.73 us: local(): lax.dot_general(weighted, hidden_low, product_dims, preferred_element_typ...]
    dot_general x5 -> x2, matrix products: 15.1 us -> 8.5 us  [dot(): return jnp.dot(a, b, preferred_element_type=f32, **kw)]
    unnamed x34 -> x51, local copies, waits for them, and re-layouts: 12.2 us -> 18.8 us
  transfers between devices with their start and end apart: 6 -> 5, of which waited for: 5 -> 4; matrix products, arithmetic and copies ran while one was open for 10% -> 9% of each run, Pallas kernels for 22% -> 22%
where the time goes in v4:
time: 327 us; the launch traced here: 326 us
  waiting for transfers between devices  135 us (41%)
  Pallas kernels  100 us (31%)
  starting transfers between devices  29 us (9%)
  matrix products  24.6 us (8%)
  local copies, waits for them, and re-layouts  20.5 us (6%)
  between operations  14.3 us (4%)
    all_to_all x2, waiting for transfers between devices, exchange(): return lax.all_to_all(array, PB_PA, split_axis=0, concat_axis=0, tiled=True)  130 us
    pallas_call x1, Pallas kernels, far_forward(): pl.pallas_call(functools.partial(far_kernel, score_scale), out_shape=(jax...  47 us
    pallas_call x1, Pallas kernels, tail(): pl.pallas_call(functools.partial(tail_kernel, scale), out_shape=(jax.Shap...  28 us
    pallas_call x1, Pallas kernels, layer_forward(): pl.pallas_call(layer_forward_kernel, out_shape=(jax.ShapeDtypeStruct((tok...  25.2 us
    all_to_all x2, starting transfers between devices, exchange(): return lax.all_to_all(array, PB_PA, split_axis=0, concat_axis=0, tiled=True)  21.7 us
    unnamed x51, local copies, waits for them, and re-layouts  18.8 us
    dot_general x2, matrix products, dot(): return jnp.dot(a, b, preferred_element_type=f32, **kw)  8.5 us
    dot_general x1, matrix products, local(): lax.dot_general(far_weight, arrived, product_dims, preferred_element_type...  6.67 us
  transfers between devices with their start and end apart: 5, of which 4 were waited for; matrix products, arithmetic and copies ran while one was open for 9% of the time, Pallas kernels for 22%

profile of v4, /device:TPU:1, one launch (start us, length us, event | category | flops | bytes accessed | tf_op | source)
XLA Modules:
  0.0 325.9 jit_solution(12314712910442646329)
XLA Ops:
  7.2 1.0 broadcast_select_fusion.1
  8.3 6.2 %collective-permute-start = (bf16[28,1792]{1,0:T(8,128)(2,1)S(1)}, bf16[28,1792]{1,0:T(8,128)(2,1)S(1)}, u32[]{:S(2)}, u32[]{:S(2)}) collective-permute-start(bf16[28,1792]{1,0:T(8,128)(2,1)S(1)} %get-tuple-element.40), channel_id=1, source_target_pairs={{0,0},{1,16},{2,1},{3,17},{4,2},{5,18},{6,3},{7,19},{8,4},{9,20},{... | collective-permute-start | bytes 301064 | tf_op jit(solution)/shard_map/ppermute | solution.py:50
  14.5 1.1 collective-permute-start.1
  15.6 3.1 collective-permute-done
  18.7 1.2 collective-permute-done.1
  19.9 0.7 pad_maximum_fusion
  20.7 0.8 copy.36
  22.2 5.1 %convolution_bitcast_fusion = bf16[128,8,3584]{2,1,0:T(8,128)(2,1)} fusion(bf16[128,3584]{1,0:T(8,128)(2,1)S(1)} %copy-done, s32[128]{0:T(128)S(1)} %get-tuple-element.45, s32[128]{0:T(128)S(1)} %get-tuple-element.46, s32[128]{0:T(128)S(1)} %get-tuple-element.47, s32[128]{0:T(128)S(1)} %get-tuple-element.44), kind=kOutput, calls=%fused_computation.1 | convolution fusion | flops 940441600 | bytes 8259584 | tf_op jit(solution)/shard_map/dot_general | solution.py:644
  27.3 14.8 %all-to-all-start = ((bf16[128,8,3584]{2,1,0:T(8,128)(2,1)}), bf16[128,8,3584]{2,1,0:T(8,128)(2,1)}, u32[]{:S(2)}, u32[]{:S(2)}) async-start(bf16[128,8,3584]{2,1,0:T(8,128)(2,1)} %convolution_bitcast_fusion), calls=%async_computation | async-start | bytes 14680064 | tf_op jit(solution)/shard_map/all_to_all | solution.py:58
  42.4 3.5 %fusion.25 = (f32[128]{0:T(128)S(1)}, f32[128,512]{1,0:T(8,128)S(1)}) fusion(bf16[128,3584]{1,0:T(8,128)(2,1)S(1)} %copy-done, bf16[512,3584]{1,0:T(8,128)(2,1)} %passages.1), kind=kOutput, calls=%fused_computation.58 | convolution fusion | flops 469892992 | bytes 4850176 | tf_op jit(solution)/shard_map/dot_general | solution.py:29
  46.8 93.6 %all-to-all-done = bf16[128,8,3584]{2,1,0:T(8,128)(2,1)} async-done(((bf16[128,8,3584]{2,1,0:T(8,128)(2,1)}), bf16[128,8,3584]{2,1,0:T(8,128)(2,1)}, u32[]{:S(2)}, u32[]{:S(2)}) %all-to-all-start) | async-done | bytes 7340064 | tf_op jit(solution)/shard_map/all_to_all | solution.py:58
  140.4 2.0 copy-done.2
  142.5 47.0 %far_forward.1 = (bf16[1024,3584]{1,0:T(8,128)(2,1)}, f32[1024,512]{1,0:T(8,128)S(1)}, bf16[256,1024]{1,0:T(8,128)(2,1)S(1)}, f32[128,128]{1,0:T(8,128)S(1)}, f32[128,8,128]{2,1,0:T(8,128)S(1)}) custom-call(bf16[1024,3584]{1,0:T(8,128)(2,1)} %bitcast.6.arrived, bf16[512,3584]{1,0:T(8,128)(2,1)S(1)} %copy-done.2, f32[128,1]{1,0:T(8,128)S(1)} %add.83.near_mass, ...), custom_call_target="tpu_custom_call" | custom-call | tf_op jit(solution)/shard_map/far_forward/pallas_call | solution.py:341
  189.5 0.8 copy-done.6
  190.3 0.8 copy-done.8
  191.1 6.9 %all-to-all-start.1 = ((bf16[128,8,3584]{2,1,0:T(8,128)(2,1)}), bf16[128,8,3584]{2,1,0:T(8,128)(2,1)}, u32[]{:S(2)}, u32[]{:S(2)}) async-start(bf16[128,8,3584]{2,1,0:T(8,128)(2,1)} %bitcast.34), calls=%async_computation.1 | async-start | bytes 14680064 | tf_op jit(solution)/shard_map/all_to_all | solution.py:58
  198.3 5.0 %fusion.6 = f32[256,3584]{1,0:T(8,128)} fusion(bf16[512,3584]{1,0:T(8,128)(2,1)} %passages.1, bf16[128,512]{1,0:T(8,128)(2,1)S(1)} %fusion.10, bf16[128,512]{1,0:T(8,128)(2,1)S(1)} %get-tuple-element.36), kind=kOutput, calls=%fused_computation.15 | convolution fusion | flops 940048384 | bytes 7602176 | tf_op jit(solution)/shard_map/dot_general | solution.py:29
  203.3 1.2 copy.43
  204.7 6.7 %fusion = f32[512,3584]{1,0:T(8,128)S(1)} fusion(f32[1024,512]{1,0:T(8,128)S(1)} %get-tuple-element.22, f32[1024]{0:T(1024)S(1)} %bitcast.35, bf16[128,8,3584]{2,1,0:T(8,128)(2,1)} %all-to-all-done), kind=kOutput, calls=%fused_computation.6 | convolution fusion | flops 3759144960 | bytes 16781312 | tf_op jit(solution)/shard_map/dot_general | solution.py:674
  211.3 4.3 %add_multiply_fusion = f32[512,3584]{1,0:T(8,128)} fusion(f32[512,3584]{1,0:T(8,128)S(1)} %fusion, bf16[128,3584]{1,0:T(8,128)(2,1)S(1)} %copy-done, f32[128,512]{1,0:T(8,128)S(1)} %copy-done.19, f32[128]{0:T(128)S(1)} %get-tuple-element.34, s32[128]{0:T(128)S(1)} %copy-done.21), kind=kOutput, calls=%fused_computation | convolution fusion | flops 473759744 | bytes 15860736 | tf_op jit(solution)/shard_map/dot_general | solution.py:675
  216.6 2.0 copy-done.3
  218.7 25.2 %layer_forward.1 = (bf16[512,3584]{1,0:T(8,128)(2,1)S(1)}, f32[512,16]{1,0:T(8,128)S(1)}, f32[512,16]{1,0:T(8,128)S(1)}, f32[512,1]{1,0:T(8,128)S(1)}) custom-call(bf16[512,3584]{1,0:T(8,128)(2,1)S(1)} %copy-done.3, bf16[3584,1792]{1,0:T(8,128)(2,1)} %all-gather.2.cloned.1.call-done.half_weight, bf16[512,3584]{1,0:T(8,128)(2,1)} %residual.1, ...), custom_call_target="tpu_custom_call" | custom-call | flops 1000 | bytes 1000 | tf_op jit(solution)/shard_map/layer_forward/pallas_call | solution.py:151
  243.9 1.8 copy-done.4
  246.3 0.7 copy-done.12
  247.0 0.7 copy-done.14
  247.7 36.6 %all-to-all-done.1 = bf16[128,8,3584]{2,1,0:T(8,128)(2,1)} async-done(((bf16[128,8,3584]{2,1,0:T(8,128)(2,1)}), bf16[128,8,3584]{2,1,0:T(8,128)(2,1)}, u32[]{:S(2)}, u32[]{:S(2)}) %all-to-all-start.1) | async-done | bytes 7340064 | tf_op jit(solution)/shard_map/all_to_all | solution.py:58
  284.3 2.0 copy-done.5
  286.4 0.9 copy-done.11
  287.3 0.9 copy-done.13
  288.3 0.9 copy-done.15
  289.2 28.0 %tail.1 = (f32[128,3584]{1,0:T(8,128)S(1)}, f32[32,128]{1,0:T(8,128)S(1)}) custom-call(bf16[1024,3584]{1,0:T(8,128)(2,1)} %bitcast.11.returned, bf16[256,1024]{1,0:T(8,128)(2,1)S(1)} %copy-done.7, f32[128,3584]{1,0:T(8,128)S(1)} %slice_subtract_fusion.near_part, f32[1,3584]{1,0:T(1,128)S(1)} %reshape.87.norm, bf16[512,3584]{1,0:T(8,128)(2,1)S(1)} %copy-done.5, ...), custom_call_target="tpu_custom_call" | custom-call | tf_op jit(solution)/shard_map/tail/pallas_call | solution.py:571
  317.8 1.2 copy.45
  (67 shorter events, 4.6 us)
Async XLA Ops:
  7.2 15.1 %copy-start = (bf16[128,3584]{1,0:T(8,128)(2,1)S(1)}, bf16[128,3584]{1,0:T(8,128)(2,1)}, u32[]{:S(2)}) copy-start(bf16[128,3584]{1,0:T(8,128)(2,1)} %param.10) | copy-start | bytes 2752516
  7.2 208.8 %all-gather.2.cloned.1.call-start = ((), (), s32[]{:S(2)}) async-start(), calls=%async_computation.2 | async-start | bytes 13045760 | tf_op jit(solution)/shard_map/all_gather | solution.py:648
  8.3 10.4 %collective-permute-start = (bf16[28,1792]{1,0:T(8,128)(2,1)S(1)}, bf16[28,1792]{1,0:T(8,128)(2,1)S(1)}, u32[]{:S(2)}, u32[]{:S(2)}) collective-permute-start(bf16[28,1792]{1,0:T(8,128)(2,1)S(1)} %get-tuple-element.40), channel_id=1, source_target_pairs={{0,0},{1,16},{2,1},{3,17},{4,2},{5,18},{6,3},{7,19},{8,4},{9,20},{... | collective-permute-start | bytes 301064 | tf_op jit(solution)/shard_map/ppermute | solution.py:50
  14.5 5.4 %collective-permute-start.1 = (bf16[28,1792]{1,0:T(8,128)(2,1)S(1)}, bf16[28,1792]{1,0:T(8,128)(2,1)S(1)}, u32[]{:S(2)}, u32[]{:S(2)}) collective-permute-start(bf16[28,1792]{1,0:T(8,128)(2,1)S(1)} %get-tuple-element.41), channel_id=1, source_target_pairs={{0,16},{1,0},{2,17},{3,1},{4,18},{5,2},{6,19},{7,3},{8,20},{9,4},{... | collective-permute-start | bytes 301064 | tf_op jit(solution)/shard_map/ppermute | solution.py:51
  27.3 113.1 %all-to-all-start = ((bf16[128,8,3584]{2,1,0:T(8,128)(2,1)}), bf16[128,8,3584]{2,1,0:T(8,128)(2,1)}, u32[]{:S(2)}, u32[]{:S(2)}) async-start(bf16[128,8,3584]{2,1,0:T(8,128)(2,1)} %convolution_bitcast_fusion), calls=%async_computation | async-start | bytes 14680064 | tf_op jit(solution)/shard_map/all_to_all | solution.py:58
  45.9 94.6 %copy-start.18 = (f32[128,512]{1,0:T(8,128)}, f32[128,512]{1,0:T(8,128)S(1)}, u32[]{:S(2)}) copy-start(f32[128,512]{1,0:T(8,128)S(1)} %get-tuple-element.49) | copy-start | bytes 786436
  46.2 0.5 copy-start.22
  140.4 2.0 copy-start.2
  189.5 0.8 copy-start.6
  190.3 0.8 copy-start.8
  191.1 7.0 %copy-start.20 = (bf16[3584]{0:T(1024)(128)(2,1)S(1)}, bf16[3584]{0:T(1024)(128)(2,1)}, u32[]{:S(2)}) copy-start(bf16[3584]{0:T(1024)(128)(2,1)} %param.19) | copy-start | bytes 21508
  191.1 7.0 %copy-start.23 = (f32[128]{0:T(128)S(1)}, f32[128]{0:T(128)}, u32[]{:S(2)}) copy-start(f32[128]{0:T(128)} %copy-done.22) | copy-start | bytes 1540
  191.1 7.1 %copy-start.21 = (s32[128]{0:T(128)S(1)}, s32[128]{0:T(128)}, u32[]{:S(2)}) copy-start(s32[128]{0:T(128)} %param.13) | copy-start | bytes 1540
  191.1 93.2 %all-to-all-start.1 = ((bf16[128,8,3584]{2,1,0:T(8,128)(2,1)}), bf16[128,8,3584]{2,1,0:T(8,128)(2,1)}, u32[]{:S(2)}, u32[]{:S(2)}) async-start(bf16[128,8,3584]{2,1,0:T(8,128)(2,1)} %bitcast.34), calls=%async_computation.1 | async-start | bytes 14680064 | tf_op jit(solution)/shard_map/all_to_all | solution.py:58
  204.6 6.7 %copy-start.19 = (f32[128,512]{1,0:T(8,128)S(1)}, f32[128,512]{1,0:T(8,128)}, u32[]{:S(2)}) copy-start(f32[128,512]{1,0:T(8,128)} %copy-done.18) | copy-start | bytes 786436
  211.3 4.3 %copy-start.17 = (f32[256,3584]{1,0:T(8,128)S(1)}, f32[256,3584]{1,0:T(8,128)}, u32[]{:S(2)}) copy-start(f32[256,3584]{1,0:T(8,128)} %fusion.6) | copy-start | bytes 11010052
  215.7 0.9 copy-start.9
  215.7 1.0 copy-start.16
  216.6 2.0 copy-start.3
  218.7 65.7 %copy-start.7 = (bf16[256,1024]{1,0:T(8,128)(2,1)S(1)}, bf16[256,1024]{1,0:T(8,128)(2,1)}, u32[]{:S(2)}) copy-start(bf16[256,1024]{1,0:T(8,128)(2,1)} %copy-done.6) | copy-start | bytes 1572868
  243.9 1.8 copy-start.4
  245.6 0.7 copy-start.10
  246.3 0.7 copy-start.12
  247.0 0.7 copy-start.14
  284.3 2.0 copy-start.5
  286.4 0.9 copy-start.11
  287.3 0.9 copy-start.13
  288.3 0.9 copy-start.15
  289.2 29.8 %copy-start.1 = (bf16[128,3584]{1,0:T(8,128)(2,1)S(1)}, bf16[128,3584]{1,0:T(8,128)(2,1)}, u32[]{:S(2)}) copy-start(bf16[128,3584]{1,0:T(8,128)(2,1)} %param.10) | copy-start | bytes 2752516
Sparse Core Ops, SparseCore 0:
  20.8 175.2 all-gather.1

commit v5 on v4

--- a/solution.py
+++ b/solution.py
@@ -38,17 +38,21 @@
     return (chip // per_plane) * 2 * per_plane + core * per_plane + chip % per_plane
 
 
-def gathered_weight_input(rows):
+def weight_halves_sent(rows):
     count = lax.axis_size(PB_PA)
     per_plane = lax.axis_size("pa_0") * lax.axis_size("pa_1")
     half = rows.shape[1] // 2
     left, right = rows[:, :half], rows[:, half:]
     odd = lax.axis_index("pa_1") % 2 == 1
-    core = lax.axis_index("pb_1")
     same = [(f, device_of(f // 2, f % 2, per_plane)) for f in range(count)]
     other = [(f, device_of(f // 2, 1 - f % 2, per_plane)) for f in range(count)]
     first = lax.ppermute(jnp.where(odd, right, left), PB_PA, same)
     second = lax.ppermute(jnp.where(odd, left, right), PB_PA, other)
+    return first, second
+
+
+def gather_input(first, second):
+    core = lax.axis_index("pb_1")
     low = jnp.where(core == 0, first, second)
     high = jnp.where(core == 0, second, first)
     return jnp.concatenate([low, high], axis=0)
@@ -192,27 +196,31 @@
 
 
 def far_kernel(
-    score_scale, arrived, passages, near_mass, key_column, key_row, mean, scores, mix, log_total,
-    log_arrived, rows, weights, inverse, means, mass, mass_in, log_out, row_sem, mean_sem,
-    mass_send, mass_recv, log_send, log_recv,
+    score_scale, arrived, passages_in, near_mass, key_column, mean, scores, mix, log_total,
+    log_column, rows, passages, weights, inverse, means, mass, log_out, mass1, mass2, mass3, log1,
+    log2, log3, row_sem, passage_sem, mean_sem, send_sem, recv_sem,
 ):
     place = torus_place()
-    own = flat_of(place)
-    peers, slot_rows, lanes = mass.shape
-    all_rows = peers * slot_rows
-    hard_count = key_row.shape[0]
+    outer = place[0] * 2 + place[1]
+    inner = place[2] * 4 + place[3]
+    outers, inners, lanes = mass.shape
+    peers = outers * inners
     query_count = near_mass.shape[0]
+    hard_count = key_column.shape[0] // query_count
+    all_rows, passage_count = scores.shape
+    slot_rows = all_rows // peers
     width = passages.shape[1]
     chunks = row_sem.shape[0]
     block = all_rows // chunks
-    block_peers = peers // chunks
-    barrier = pltpu.get_barrier_semaphore()
-
-    def greet(j, carry):
-        pl.semaphore_signal(
-            barrier, inc=1, device_id=torus_peer(place, j), device_id_type=MESH
-        )
-        return carry
+    exact = dict(precision=lax.Precision.HIGHEST, preferred_element_type=f32)
+
+    def along_outer(d):
+        to = lax.rem(outer + d, outers)
+        return to, (to // 2, lax.rem(to, 2), place[2], place[3])
+
+    def along_inner(d):
+        to = lax.rem(inner + d, inners)
+        return to, (place[0], place[1], to // 4, lax.rem(to, 4))
 
     def part(c):
         return pl.ds(pl.multiple_of(c * block, block), block)
@@ -223,9 +231,22 @@
     def went_out(c):
         return pltpu.make_async_copy(means.at[part(c)], mean.at[part(c)], mean_sem.at[c])
 
+    passages_here = pltpu.make_async_copy(passages_in, passages, passage_sem)
+    passages_here.start()
     for c in range(chunks):
         came_in(c).start()
-    lax.fori_loop(1, peers, greet, 0)
+    barrier = pltpu.get_barrier_semaphore()
+    for d in range(1, outers):
+        pl.semaphore_signal(barrier, inc=1, device_id=along_outer(d)[1], device_id_type=MESH)
+    for d in range(1, inners):
+        pl.semaphore_signal(barrier, inc=1, device_id=along_inner(d)[1], device_id_type=MESH)
+    passages_here.wait()
+    lane_ids = lax.broadcasted_iota(jnp.int32, (block, lanes), 1)
+    slot_ids = lax.rem(lax.broadcasted_iota(jnp.int32, (block, lanes), 0), slot_rows)
+    block_peers = block // slot_rows
+    peer_ids = lax.broadcasted_iota(jnp.int32, (block_peers, block), 0)
+    peer_rows = lax.broadcasted_iota(jnp.int32, (block_peers, block), 1) // slot_rows
+    gather_rows = jnp.where(peer_ids == peer_rows, 1.0, 0.0)
 
     def score(c, carry):
         came_in(c).wait()
@@ -239,33 +260,43 @@
         total = jnp.sum(weight, axis=1, keepdims=True)
         weights[part(c), :] = weight.astype(bf16)
         inverse[part(c), :] = 1.0 / total
-        spread = jnp.broadcast_to(peak + jnp.log(total), (block, lanes))
-        mass[pl.ds(c * block_peers, block_peers)] = spread.reshape(block_peers, slot_rows, lanes)
+        spread = jnp.where(lane_ids == slot_ids, peak + jnp.log(total), 0.0)
+        compact = jnp.dot(gather_rows, spread, **exact)
+        step = block_peers // inners
+        mass[pl.ds(c * step, step)] = compact.reshape(step, inners, lanes)
         return carry
 
     lax.fori_loop(0, chunks, score, 0)
-    pl.semaphore_wait(barrier, peers - 1)
-
-    def sends(source, target, send_sem, recv_sem):
-        def body(j, carry):
-            peer = torus_peer(place, j)
+    pl.semaphore_wait(barrier, outers - 1 + inners - 1)
+
+    def hop1(source, target, which):
+        for d in range(1, outers):
+            to, device = along_outer(d)
             pltpu.make_async_remote_copy(
-                source.at[flat_of(peer)], target.at[own], send_sem, recv_sem,
-                device_id=peer, device_id_type=MESH,
+                source.at[to], target.at[outer], send_sem.at[which], recv_sem.at[which],
+                device_id=device, device_id_type=MESH,
             ).start()
-            return carry
-
-        lax.fori_loop(1, peers, body, 0)
-
-    def every(source, target, send_sem, recv_sem):
-        rest = pl.ds(0, peers - 1)
+        target[outer] = source[outer]
+
+    def hop2(source, target, which):
+        for d in range(1, inners):
+            to, device = along_inner(d)
+            pltpu.make_async_remote_copy(
+                source.at[to], target.at[inner], send_sem.at[which], recv_sem.at[which],
+                device_id=device, device_id_type=MESH,
+            ).start()
+        target[inner] = source[inner]
+
+    def others(source, target, which):
+        rest = pl.ds(0, source.shape[0] - 1)
         return pltpu.make_async_remote_copy(
-            source.at[rest], target.at[rest], send_sem, recv_sem,
-            device_id=torus_peer(place, 1), device_id_type=MESH,
-        )
-
-    sends(mass, mass_in, mass_send, mass_recv)
-    mass_in[own] = mass[own]
+            source.at[rest], target.at[rest], send_sem.at[which], recv_sem.at[which],
+            device_id=along_outer(1)[1], device_id_type=MESH,
+        )
+
+    def repack(source, target):
+        for r in range(inners):
+            target[r] = source[:, r, :]
 
     def average(c, carry):
         weight = weights[part(c), :]
@@ -279,27 +310,27 @@
         went_out(c).start()
         return carry
 
-    lax.fori_loop(0, chunks, average, 0)
-    row_ids = lax.broadcasted_iota(jnp.int32, (query_count, all_rows), 1)
-    hits = [
-        key_column[t * query_count : (t + 1) * query_count, :] == row_ids
-        for t in range(hard_count)
+    hop1(mass, mass1, 0)
+    lax.fori_loop(0, chunks // 2, average, 0)
+    others(mass, mass1, 0).wait_recv()
+    repack(mass1, mass2)
+    hop2(mass2, mass3, 1)
+    lax.fori_loop(chunks // 2, chunks, average, 0)
+
+    key = key_column[...]
+    peer = key // slot_rows
+    slot = lax.rem(key, slot_rows)
+    pairs = key.shape[0]
+    ids = lax.broadcasted_iota(jnp.int32, (pairs, peers), 1)
+    at_slot = lax.broadcasted_iota(jnp.int32, (pairs, lanes), 1) == slot
+    to_peer = jnp.where(ids == peer, 1.0, 0.0)
+    from_peer = jnp.where(ids == lax.rem(peer, inners) * outers + peer // inners, 1.0, 0.0)
+    others(mass2, mass3, 1).wait_recv()
+    came = jnp.dot(from_peer, mass3[...].reshape(peers, lanes), **exact)
+    came = jnp.sum(jnp.where(at_slot, came, 0.0), axis=1, keepdims=True)
+    masses = [near_mass[...]] + [
+        came[t * query_count : (t + 1) * query_count] for t in range(hard_count)
     ]
-    column_ids = lax.broadcasted_iota(jnp.int32, (all_rows, query_count), 0)
-    picks = jnp.zeros((all_rows, query_count), f32)
-    for t in range(hard_count):
-        picks = jnp.where(column_ids == key_row[t : t + 1, :], 1.0, picks)
-    filled = jnp.sum(picks, axis=1, keepdims=True) > 0.0
-    every(mass, mass_in, mass_send, mass_recv).wait_recv()
-    came = mass_in[...].reshape(all_rows, lanes)
-    masses = [jnp.broadcast_to(near_mass[...], (query_count, lanes))]
-    for hit in hits:
-        masses.append(
-            jnp.dot(
-                jnp.where(hit, 1.0, 0.0), came,
-                precision=lax.Precision.HIGHEST, preferred_element_type=f32,
-            )
-        )
     peak = masses[0]
     for value in masses[1:]:
         peak = jnp.maximum(peak, value)
@@ -308,35 +339,54 @@
         total = total + jnp.exp(value - peak)
     log_value = peak + jnp.log(total)
     log_total[...] = log_value
-    outgoing = jnp.dot(
-        picks, log_value, precision=lax.Precision.HIGHEST, preferred_element_type=f32
-    )
-    outgoing = jnp.where(filled, outgoing, absent_mass)
+    log_pairs = jnp.concatenate([log_value] * hard_count, axis=0)
+    over_pairs = (((0,), (0,)), ((), ()))
+    outgoing = lax.dot_general(to_peer, jnp.where(at_slot, log_pairs, 0.0), over_pairs, **exact)
+    filled = lax.dot_general(to_peer, jnp.where(at_slot, 1.0, 0.0), over_pairs, **exact)
+    outgoing = jnp.where(filled > 0.5, outgoing, absent_mass)
     log_out[...] = outgoing.reshape(log_out.shape)
-    sends(log_out, log_arrived, log_send, log_recv)
-    log_arrived[own] = log_out[own]
+    hop1(log_out, log1, 2)
+    row_ids = lax.broadcasted_iota(jnp.int32, (query_count, all_rows), 1)
     shares = jnp.zeros((query_count, all_rows), f32)
     for t in range(hard_count):
-        shares = jnp.where(hits[t], jnp.exp(masses[1 + t] - log_value)[:, :1], shares)
+        hit = key[t * query_count : (t + 1) * query_count] == row_ids
+        shares = jnp.where(hit, jnp.exp(masses[1 + t] - log_value), shares)
     high = shares.astype(bf16)
     mix[:query_count, :] = high
     mix[query_count:, :] = (shares - high.astype(f32)).astype(bf16)
-    every(mass, mass_in, mass_send, mass_recv).wait_send()
+    others(log_out, log1, 2).wait_recv()
+    repack(log1, log2)
+    hop2(log2, log3, 3)
+    row = lax.broadcasted_iota(jnp.int32, (all_rows, peers), 0)
+    row_peer = row // slot_rows
+    back = lax.rem(row_peer, inners) * outers + row_peer // inners
+    spread = jnp.where(
+        lax.broadcasted_iota(jnp.int32, (all_rows, peers), 1) == back, 1.0, 0.0
+    )
+    mine = lax.broadcasted_iota(jnp.int32, (all_rows, lanes), 1) == lax.rem(
+        lax.broadcasted_iota(jnp.int32, (all_rows, lanes), 0), slot_rows
+    )
     for c in range(chunks):
         went_out(c).wait()
-    last = every(log_out, log_arrived, log_send, log_recv)
-    last.wait_send()
-    last.wait_recv()
+    others(mass, mass1, 0).wait_send()
+    others(mass2, mass3, 1).wait_send()
+    others(log_out, log1, 2).wait_send()
+    others(log2, log3, 3).wait_recv()
+    logs = jnp.dot(spread, log3[...].reshape(peers, lanes), **exact)
+    log_column[...] = jnp.sum(jnp.where(mine, logs, 0.0), axis=1, keepdims=True)
+    others(log2, log3, 3).wait_send()
 
 
 def far_forward(arrived, passages, near_mass, key, peers, score_scale):
     all_rows, width = arrived.shape
     passage_count = passages.shape[0]
     hard_count, query_count = key.shape
-    lanes, chunks = 128, 4
-    small = (peers, all_rows // peers, lanes)
+    lanes, chunks, outers = 128, 4, 8
+    inners = peers // outers
+    by_outer = pltpu.VMEM((outers, inners, lanes), f32)
+    by_inner = pltpu.VMEM((inners, outers, lanes), f32)
     vmem = pl.BlockSpec(memory_space=pltpu.VMEM)
-    hbm = pl.BlockSpec(memory_space=pl.ANY)
+    hbm = pl.BlockSpec(memory_space=pltpu.HBM)
     dma = pltpu.SemaphoreType.DMA
     return pl.pallas_call(
         functools.partial(far_kernel, score_scale),
@@ -344,31 +394,36 @@
             jax.ShapeDtypeStruct((all_rows, width), bf16),
             jax.ShapeDtypeStruct((all_rows, passage_count), f32),
             jax.ShapeDtypeStruct((2 * query_count, all_rows), bf16),
-            jax.ShapeDtypeStruct((query_count, lanes), f32),
-            jax.ShapeDtypeStruct(small, f32),
+            jax.ShapeDtypeStruct((query_count, 1), f32),
+            jax.ShapeDtypeStruct((all_rows, 1), f32),
         ),
-        in_specs=[hbm, vmem, vmem, vmem, vmem],
+        in_specs=[hbm, hbm, vmem, vmem],
         out_specs=(hbm, vmem, vmem, vmem, vmem),
         scratch_shapes=[
             pltpu.VMEM((all_rows, width), bf16),
+            pltpu.VMEM((passage_count, width), bf16),
             pltpu.VMEM((all_rows, passage_count), bf16),
             pltpu.VMEM((all_rows, 1), f32),
             pltpu.VMEM((all_rows, width), bf16),
-            pltpu.VMEM(small, f32),
-            pltpu.VMEM(small, f32),
-            pltpu.VMEM(small, f32),
-            dma((chunks,)),
+            by_outer,
+            by_outer,
+            by_outer,
+            by_inner,
+            by_inner,
+            by_outer,
+            by_inner,
+            by_inner,
             dma((chunks,)),
             dma(()),
-            dma(()),
-            dma(()),
-            dma(()),
+            dma((chunks,)),
+            dma((4,)),
+            dma((4,)),
         ],
         compiler_params=pltpu.CompilerParams(
             collective_id=2, has_side_effects=True, vmem_limit_bytes=44 * 1024 * 1024
         ),
         name="far_forward",
-    )(arrived, passages, near_mass[:, None], key.reshape(-1)[:, None], key)
+    )(arrived, passages, near_mass[:, None], key.reshape(-1)[:, None])
 
 
 def tail_kernel(
@@ -380,7 +435,6 @@
     own = flat_of(place)
     lane_group = place[3]
     column = own // 4
-    peers = 128
     tiles = row_sem.shape[0]
     width = terms.shape[2] * terms.shape[0]
     tile = width // tiles
@@ -411,13 +465,28 @@
     ctx_in.start()
     barrier = pltpu.get_barrier_semaphore()
 
-    def greet(j, carry):
-        pl.semaphore_signal(
-            barrier, inc=1, device_id=torus_peer(place, j), device_id_type=MESH
-        )
-        return carry
-
-    lax.fori_loop(1, peers, greet, 0)
+    gathers = column < count
+    base = (lanes * column) // 28
+    last = (lanes * column + lanes - 1) // 28
+    tile0 = (28 * own) // lanes
+    tile1 = (28 * own + 27) // lanes
+
+    def of_column(j, b):
+        return (j // 8, lax.rem(j // 4, 2), lax.rem(j, 4), b)
+
+    def greet(d, carry):
+        to = of_column(lax.rem(column + d, columns), lane_group)
+        pl.semaphore_signal(barrier, inc=1, device_id=to, device_id_type=MESH)
+        return carry
+
+    lax.fori_loop(1, columns, greet, 0)
+    for slot in range(2):
+        for b in range(4):
+            @pl.when((tile0 + slot <= tile1) & ((tile0 + slot != column) | (lane_group != b)))
+            def _():
+                to = of_column(tile0 + slot, b)
+                pl.semaphore_signal(barrier, inc=1, device_id=to, device_id_type=MESH)
+
     products[...] = jnp.zeros_like(products)
     scaled_up[...] = jnp.zeros_like(scaled_up)
     hid_in.wait()
@@ -465,7 +534,8 @@
         return carry
 
     lax.fori_loop(0, tiles, products_of, 0)
-    pl.semaphore_wait(barrier, peers - 1)
+    inside = jnp.where((base <= own) & (own <= last), 1, 0)
+    pl.semaphore_wait(barrier, columns - 1 + jnp.where(gathers, last - base + 1 - inside, 0))
 
     def stage1(j):
         to = (j // 8, lax.rem(j // 4, 2), lax.rem(j, 4), lane_group)
@@ -481,11 +551,6 @@
         return carry
 
     lax.fori_loop(0, count, start1, 0)
-    gathers = column < count
-    base = (lanes * column) // 28
-    last = (lanes * column + lanes - 1) // 28
-    tile0 = (28 * own) // lanes
-    tile1 = (28 * own + 27) // lanes
 
     def sized(buffer, n, send_sem, recv_sem):
         piece_of = buffer.at[pl.ds(0, n)]
@@ -566,7 +631,7 @@
     tokens, rank = narrow.shape
     tiles, lanes, rerun = 7, 128, RERUN_QUERIES
     vmem = pl.BlockSpec(memory_space=pltpu.VMEM)
-    hbm = pl.BlockSpec(memory_space=pl.ANY)
+    hbm = pl.BlockSpec(memory_space=pltpu.HBM)
     dma = pltpu.SemaphoreType.DMA
     return pl.pallas_call(
         functools.partial(tail_kernel, scale),
@@ -626,7 +691,6 @@
     passage_count = passages.shape[0]
     score_scale = inverse_temp / math.sqrt(MODEL_WIDTH)
 
-    weight_rows = gathered_weight_input(output_weight)
 
     source = lax.axis_index(PB_PA)
     target = ((source + 1 + hard_block_offsets) % device_count).reshape(-1)
@@ -642,6 +706,10 @@
     for t in range(1, hard_count):
         picks = picks | (row_ids[:, None] == key[t][None, :])
     outgoing = jnp.dot(picks.astype(bf16), queries, preferred_element_type=bf16)
+    outgoing, first, second = lax.optimization_barrier(
+        (outgoing, *weight_halves_sent(output_weight))
+    )
+    weight_rows = gather_input(first, second)
     arrived = exchange(outgoing.reshape(device_count, slot_rows, MODEL_WIDTH))
     arrived = arrived.reshape(-1, MODEL_WIDTH)
 
@@ -662,7 +730,6 @@
     returned = exchange(far_mean.reshape(device_count, slot_rows, MODEL_WIDTH))
     returned = returned.reshape(-1, MODEL_WIDTH)
     log_total = log_total[:, 0]
-    log_arrived = log_arrived.reshape(all_rows, -1)[:, :1]
     near_share = jnp.exp(near_mass - log_total)
     near_part = (near_share / near_sum)[:, None] * stacked[:query_count] - stacked[query_count:]
 

time: 327 us -> 311 us (0.951)
  waiting for transfers between devices: 135 us -> 127 us
  Pallas kernels: 100 us -> 95.3 us
  starting transfers between devices: 29 us -> 24.4 us
    all_to_all x2, waiting for transfers between devices: 130 us -> 97.2 us  [exchange(): return lax.all_to_all(array, PB_PA, split_axis=0, concat_axis=0, tiled=True)]
    all_gather x1, waiting for transfers between devices: 0.02 us -> 30.3 us  [local(): half_weight = lax.all_gather(weight_rows, CHIPS, axis=0, tiled=True)]
    pallas_call x1, Pallas kernels: 47 us -> 36.5 us  [far_forward(): pl.pallas_call(functools.partial(far_kernel, score_scale), out_shape=(jax...]
    ppermute x2, waiting for transfers between devices: 4.32 us -> 0.01 us  [the longest x1 0.01 us: weight_halves_sent(): second = lax.ppermute(jnp.where(odd, left, right), PB_PA, other)]
    all_to_all x2, starting transfers between devices: 21.7 us -> 18 us  [exchange(): return lax.all_to_all(array, PB_PA, split_axis=0, concat_axis=0, tiled=True)]
    unnamed x51 -> x56, local copies, waits for them, and re-layouts: 18.8 us -> 17.2 us
  transfers between devices with their start and end apart: 5 -> 5, of which waited for: 4 -> 3; matrix products, arithmetic and copies ran while one was open for 9% -> 10% of each run, Pallas kernels for 22% -> 21%
where the time goes in v5:
time: 311 us; the launch traced here: 310 us
  waiting for transfers between devices  127 us (41%)
  Pallas kernels  95.3 us (31%)
  matrix products  24.7 us (8%)
  starting transfers between devices  24.4 us (8%)
  local copies, waits for them, and re-layouts  18.7 us (6%)
  between operations  14.4 us (5%)
  other arithmetic  4.99 us (2%)
    all_to_all x2, waiting for transfers between devices, exchange(): return lax.all_to_all(array, PB_PA, split_axis=0, concat_axis=0, tiled=True)  97.2 us
    pallas_call x1, Pallas kernels, far_forward(): pl.pallas_call(functools.partial(far_kernel, score_scale), out_shape=(jax...  36.5 us
    pallas_call x1, Pallas kernels, tail(): pl.pallas_call(functools.partial(tail_kernel, scale), out_shape=(jax.Shap...  30.7 us
    all_gather x1, waiting for transfers between devices, local(): half_weight = lax.all_gather(weight_rows, CHIPS, axis=0, tiled=True)  30.3 us
    pallas_call x1, Pallas kernels, layer_forward(): pl.pallas_call(layer_forward_kernel, out_shape=(jax.ShapeDtypeStruct((tok...  28.1 us
    all_to_all x2, starting transfers between devices, exchange(): return lax.all_to_all(array, PB_PA, split_axis=0, concat_axis=0, tiled=True)  18 us
    unnamed x56, local copies, waits for them, and re-layouts  17.2 us
    dot_general x2, matrix products, dot(): return jnp.dot(a, b, preferred_element_type=f32, **kw)  8.65 us
  transfers between devices with their start and end apart: 5, of which 3 were waited for; matrix products, arithmetic and copies ran while one was open for 10% of the time, Pallas kernels for 21%

profile of v5, /device:TPU:1, one launch (start us, length us, event | category | flops | bytes accessed | tf_op | source)
XLA Modules:
  0.0 309.9 jit_solution(774230473888518365)
XLA Ops:
  7.2 1.0 broadcast_select_fusion.2
  8.3 3.8 %collective-permute-start.1 = (bf16[28,1792]{1,0:T(8,128)(2,1)S(1)}, bf16[28,1792]{1,0:T(8,128)(2,1)S(1)}, u32[]{:S(2)}, u32[]{:S(2)}) collective-permute-start(bf16[28,1792]{1,0:T(8,128)(2,1)S(1)} %get-tuple-element.46), channel_id=1, source_target_pairs={{0,16},{1,0},{2,17},{3,1},{4,18},{5,2},{6,19},{7,3},{8,20},{9,4},{... | collective-permute-start | bytes 301064 | tf_op jit(solution)/shard_map/ppermute | solution.py:50
  12.1 2.5 collective-permute-start
  14.6 0.8 copy.33
  16.1 5.1 %fusion.5 = bf16[1024,3584]{1,0:T(8,128)(2,1)} fusion(bf16[128,3584]{1,0:T(8,128)(2,1)S(1)} %copy-done, s32[128]{0:T(128)S(1)} %get-tuple-element.51, s32[128]{0:T(128)S(1)} %get-tuple-element.52, s32[128]{0:T(128)S(1)} %get-tuple-element.53, s32[128]{0:T(128)S(1)} %get-tuple-element.50), kind=kOutput, calls=%fused_computation.14 | convolution fusion | flops 940441600 | bytes 8259584 | tf_op jit(solution)/shard_map/dot_general | solution.py:708
  21.3 0.7 pad_maximum_fusion
  22.0 11.6 %all-to-all-start = ((bf16[128,8,3584]{2,1,0:T(8,128)(2,1)}), bf16[128,8,3584]{2,1,0:T(8,128)(2,1)}, u32[]{:S(2)}, u32[]{:S(2)}) async-start(bf16[128,8,3584]{2,1,0:T(8,128)(2,1)} %bitcast.28), calls=%async_computation | async-start | bytes 14680064 | tf_op jit(solution)/shard_map/all_to_all | solution.py:62
  33.9 3.5 %fusion.27 = (f32[128]{0:T(128)S(1)}, f32[128,512]{1,0:T(8,128)S(1)}) fusion(bf16[128,3584]{1,0:T(8,128)(2,1)S(1)} %copy-done, bf16[512,3584]{1,0:T(8,128)(2,1)} %passages_in.1), kind=kOutput, calls=%fused_computation.58 | convolution fusion | flops 469892992 | bytes 4850176 | tf_op jit(solution)/shard_map/dot_general | solution.py:29
  37.5 0.8 fusion.16
  38.5 85.7 %all-to-all-done = bf16[128,8,3584]{2,1,0:T(8,128)(2,1)} async-done(((bf16[128,8,3584]{2,1,0:T(8,128)(2,1)}), bf16[128,8,3584]{2,1,0:T(8,128)(2,1)}, u32[]{:S(2)}, u32[]{:S(2)}) %all-to-all-start) | async-done | bytes 7340064 | tf_op jit(solution)/shard_map/all_to_all | solution.py:62
  124.2 2.1 copy-done.2
  126.3 36.5 %far_forward.1 = (bf16[1024,3584]{1,0:T(8,128)(2,1)}, f32[1024,512]{1,0:T(8,128)S(1)}, bf16[256,1024]{1,0:T(8,128)(2,1)S(1)}, f32[128,1]{1,0:T(8,128)S(1)}, f32[1024,1]{1,0:T(8,128)S(1)}) custom-call(bf16[1024,3584]{1,0:T(8,128)(2,1)} %bitcast.6.arrived, bf16[512,3584]{1,0:T(8,128)(2,1)S(1)} %copy-done.2, f32[128,1]{1,0:T(8,128)S(1)} %log_add_fusion.near_mass, ...), custom_call_target="tpu_custom_call" | custom-call | tf_op jit(solution)/shard_map/far_forward/pallas_call | solution.py:391
  162.8 0.8 copy-done.6
  163.6 0.8 copy-done.8
  165.0 6.4 %all-to-all-start.1 = ((bf16[128,8,3584]{2,1,0:T(8,128)(2,1)}), bf16[128,8,3584]{2,1,0:T(8,128)(2,1)}, u32[]{:S(2)}, u32[]{:S(2)}) async-start(bf16[128,8,3584]{2,1,0:T(8,128)(2,1)} %bitcast.29), calls=%async_computation.1 | async-start | bytes 14680064 | tf_op jit(solution)/shard_map/all_to_all | solution.py:62
  171.6 5.1 %fusion.7 = f32[256,3584]{1,0:T(8,128)} fusion(bf16[512,3584]{1,0:T(8,128)(2,1)} %passages_in.1, bf16[128,512]{1,0:T(8,128)(2,1)S(1)} %fusion.11, bf16[128,512]{1,0:T(8,128)(2,1)} %get-tuple-element.42), kind=kOutput, calls=%fused_computation.15 | convolution fusion | flops 940048384 | bytes 7602176 | tf_op jit(solution)/shard_map/dot_general | solution.py:29
  176.7 0.8 reduce.1
  177.6 1.0 fusion.25
  178.6 6.7 %fusion = f32[512,3584]{1,0:T(8,128)S(1)} fusion(f32[1024,512]{1,0:T(8,128)S(1)} %get-tuple-element.28, f32[1024]{0:T(1024)} %reduce.1, bf16[128,8,3584]{2,1,0:T(8,128)(2,1)} %all-to-all-done), kind=kOutput, calls=%fused_computation.5 | convolution fusion | flops 3759144960 | bytes 16781312 | tf_op jit(solution)/shard_map/dot_general | solution.py:741
  185.3 4.3 %add_multiply_fusion = f32[512,3584]{1,0:T(8,128)} fusion(f32[512,3584]{1,0:T(8,128)S(1)} %fusion, bf16[128,3584]{1,0:T(8,128)(2,1)S(1)} %copy-done, f32[128,512]{1,0:T(8,128)S(1)} %copy-done.21, f32[128]{0:T(128)S(1)} %get-tuple-element.40, s32[128]{0:T(128)S(1)} %copy-done.26), kind=kOutput, calls=%fused_computation | convolution fusion | flops 473759744 | bytes 15860736 | tf_op jit(solution)/shard_map/dot_general | solution.py:742
  189.9 30.3 %all-gather.2.cloned.1.call-done.half_weight = bf16[3584,1792]{1,0:T(8,128)(2,1)} async-done(((bf16[56,1792]{1,0:T(8,128)(2,1)}), bf16[3584,1792]{1,0:T(8,128)(2,1)}) %all-gather.2.cloned.1.call-update) | async-done | bytes 12845072 | tf_op jit(solution)/shard_map/all_gather | solution.py:716
  220.2 2.0 copy-done.3
  222.2 28.1 %layer_forward.1 = (bf16[512,3584]{1,0:T(8,128)(2,1)S(1)}, f32[512,16]{1,0:T(8,128)S(1)}, f32[512,16]{1,0:T(8,128)S(1)}, f32[512,1]{1,0:T(8,128)S(1)}) custom-call(bf16[512,3584]{1,0:T(8,128)(2,1)S(1)} %copy-done.3, bf16[3584,1792]{1,0:T(8,128)(2,1)} %all-gather.2.cloned.1.call-done.half_weight, bf16[512,3584]{1,0:T(8,128)(2,1)} %residual.1, ...), custom_call_target="tpu_custom_call" | custom-call | flops 1000 | bytes 1000 | tf_op jit(solution)/shard_map/layer_forward/pallas_call | solution.py:155
  250.3 1.8 copy-done.4
  253.5 0.7 copy-done.15
  254.2 11.4 %all-to-all-done.1 = bf16[128,8,3584]{2,1,0:T(8,128)(2,1)} async-done(((bf16[128,8,3584]{2,1,0:T(8,128)(2,1)}), bf16[128,8,3584]{2,1,0:T(8,128)(2,1)}, u32[]{:S(2)}, u32[]{:S(2)}) %all-to-all-start.1) | async-done | bytes 7340064 | tf_op jit(solution)/shard_map/all_to_all | solution.py:62
  265.6 2.0 copy-done.5
  267.7 0.9 copy-done.12
  268.6 0.9 copy-done.14
  269.6 0.9 copy-done.16
  270.5 30.7 %tail.1 = (f32[128,3584]{1,0:T(8,128)S(1)}, f32[32,128]{1,0:T(8,128)S(1)}) custom-call(bf16[1024,3584]{1,0:T(8,128)(2,1)} %bitcast.11.returned, bf16[256,1024]{1,0:T(8,128)(2,1)S(1)} %copy-done.7, f32[128,3584]{1,0:T(8,128)S(1)} %slice_subtract_fusion.near_part, f32[1,3584]{1,0:T(1,128)S(1)} %reshape.83.norm, bf16[512,3584]{1,0:T(8,128)(2,1)S(1)} %copy-done.5, ...), custom_call_target="tpu_custom_call" | custom-call | tf_op jit(solution)/shard_map/tail/pallas_call | solution.py:636
  301.9 1.2 copy.40
  (71 shorter events, 4.4 us)
Async XLA Ops:
  7.2 9.0 %copy-start = (bf16[128,3584]{1,0:T(8,128)(2,1)S(1)}, bf16[128,3584]{1,0:T(8,128)(2,1)}, u32[]{:S(2)}) copy-start(bf16[128,3584]{1,0:T(8,128)(2,1)} %param.10) | copy-start | bytes 2752516
  7.2 213.0 %all-gather.2.cloned.1.call-start = ((), (), s32[]{:S(2)}) async-start(), calls=%async_computation.2 | async-start | bytes 13045760 | tf_op jit(solution)/shard_map/all_gather | solution.py:716
  8.3 13.0 %collective-permute-start.1 = (bf16[28,1792]{1,0:T(8,128)(2,1)S(1)}, bf16[28,1792]{1,0:T(8,128)(2,1)S(1)}, u32[]{:S(2)}, u32[]{:S(2)}) collective-permute-start(bf16[28,1792]{1,0:T(8,128)(2,1)S(1)} %get-tuple-element.46), channel_id=1, source_target_pairs={{0,16},{1,0},{2,17},{3,1},{4,18},{5,2},{6,19},{7,3},{8,20},{9,4},{... | collective-permute-start | bytes 301064 | tf_op jit(solution)/shard_map/ppermute | solution.py:50
  12.1 9.1 %collective-permute-start = (bf16[28,1792]{1,0:T(8,128)(2,1)S(1)}, bf16[28,1792]{1,0:T(8,128)(2,1)S(1)}, u32[]{:S(2)}, u32[]{:S(2)}) collective-permute-start(bf16[28,1792]{1,0:T(8,128)(2,1)S(1)} %get-tuple-element.47), channel_id=1, source_target_pairs={{0,0},{1,16},{2,1},{3,17},{4,2},{5,18},{6,3},{7,19},{8,4},{9,20},{... | collective-permute-start | bytes 301064 | tf_op jit(solution)/shard_map/ppermute | solution.py:49
  22.0 102.2 %all-to-all-start = ((bf16[128,8,3584]{2,1,0:T(8,128)(2,1)}), bf16[128,8,3584]{2,1,0:T(8,128)(2,1)}, u32[]{:S(2)}, u32[]{:S(2)}) async-start(bf16[128,8,3584]{2,1,0:T(8,128)(2,1)} %bitcast.28), calls=%async_computation | async-start | bytes 14680064 | tf_op jit(solution)/shard_map/all_to_all | solution.py:62
  37.4 86.8 %copy-start.20 = (f32[128,512]{1,0:T(8,128)}, f32[128,512]{1,0:T(8,128)S(1)}, u32[]{:S(2)}) copy-start(f32[128,512]{1,0:T(8,128)S(1)} %get-tuple-element.55) | copy-start | bytes 786436
  37.5 86.7 %copy-start.22 = (f32[128,1]{1,0:T(8,128)}, f32[128,1]{1,0:T(8,128)S(1)}, u32[]{:S(2)}) copy-start(f32[128,1]{1,0:T(8,128)S(1)} %copy.36) | copy-start | bytes 1540
  38.4 85.8 %copy-start.23 = (f32[128,1]{1,0:T(8,128)}, f32[128,1]{1,0:T(8,128)S(1)}, u32[]{:S(2)}) copy-start(f32[128,1]{1,0:T(8,128)S(1)} %copy.35) | copy-start | bytes 1540
  124.2 2.1 copy-start.2
  162.8 0.8 copy-start.6
  163.6 0.8 copy-start.8
  164.4 0.6 copy-start.18
  165.0 6.4 %copy-start.24 = (bf16[3584]{0:T(1024)(128)(2,1)S(1)}, bf16[3584]{0:T(1024)(128)(2,1)}, u32[]{:S(2)}) copy-start(bf16[3584]{0:T(1024)(128)(2,1)} %param.19) | copy-start | bytes 21508
  165.0 6.4 %copy-start.25 = (s32[128]{0:T(128)S(1)}, s32[128]{0:T(128)}, u32[]{:S(2)}) copy-start(s32[128]{0:T(128)} %param.13) | copy-start | bytes 1540
  165.0 100.6 %all-to-all-start.1 = ((bf16[128,8,3584]{2,1,0:T(8,128)(2,1)}), bf16[128,8,3584]{2,1,0:T(8,128)(2,1)}, u32[]{:S(2)}, u32[]{:S(2)}) async-start(bf16[128,8,3584]{2,1,0:T(8,128)(2,1)} %bitcast.29), calls=%async_computation.1 | async-start | bytes 14680064 | tf_op jit(solution)/shard_map/all_to_all | solution.py:62
  171.6 5.2 %copy-start.9 = (f32[1024,1]{1,0:T(8,128)S(1)}, f32[1024,1]{1,0:T(8,128)}, u32[]{:S(2)}) copy-start(f32[1024,1]{1,0:T(8,128)} %copy-done.8) | copy-start | bytes 12292
  178.6 6.7 %copy-start.21 = (f32[128,512]{1,0:T(8,128)S(1)}, f32[128,512]{1,0:T(8,128)}, u32[]{:S(2)}) copy-start(f32[128,512]{1,0:T(8,128)} %copy-done.20) | copy-start | bytes 786436
  178.6 6.7 %copy-start.26 = (s32[128]{0:T(128)S(1)}, s32[128]{0:T(128)}, u32[]{:S(2)}) copy-start(s32[128]{0:T(128)} %param.13) | copy-start | bytes 1540
  185.3 4.3 %copy-start.19 = (f32[256,3584]{1,0:T(8,128)S(1)}, f32[256,3584]{1,0:T(8,128)}, u32[]{:S(2)}) copy-start(f32[256,3584]{1,0:T(8,128)} %fusion.7) | copy-start | bytes 11010052
  189.6 30.6 %copy-start.10 = (bf16[16,3584]{1,0:T(8,128)(2,1)S(1)}, bf16[16,3584]{1,0:T(8,128)(2,1)}, u32[]{:S(2)}) copy-start(bf16[16,3584]{1,0:T(8,128)(2,1)} %up.3) | copy-start | bytes 344068
  189.6 30.6 %copy-start.17 = (bf16[3584,16]{0,1:T(8,128)(2,1)S(1)}, bf16[3584,16]{0,1:T(8,128)(2,1)}, u32[]{:S(2)}) copy-start(bf16[3584,16]{0,1:T(8,128)(2,1)} %param.17) | copy-start | bytes 344068
  220.2 2.0 copy-start.3
  222.2 43.4 %copy-start.7 = (bf16[256,1024]{1,0:T(8,128)(2,1)S(1)}, bf16[256,1024]{1,0:T(8,128)(2,1)}, u32[]{:S(2)}) copy-start(bf16[256,1024]{1,0:T(8,128)(2,1)} %copy-done.6) | copy-start | bytes 1572868
  250.3 1.8 copy-start.4
  252.1 0.7 copy-start.11
  252.8 0.7 copy-start.13
  253.5 0.7 copy-start.15
  265.6 2.0 copy-start.5
  267.7 0.9 copy-start.12
  268.6 0.9 copy-start.14
  269.6 0.9 copy-start.16
  270.5 32.6 %copy-start.1 = (bf16[128,3584]{1,0:T(8,128)(2,1)S(1)}, bf16[128,3584]{1,0:T(8,128)(2,1)}, u32[]{:S(2)}) copy-start(bf16[128,3584]{1,0:T(8,128)(2,1)} %param.10) | copy-start | bytes 2752516
Sparse Core Ops, SparseCore 0:
  22.1 197.9 all-gather.1

commit v6 on v5

--- a/solution.py
+++ b/solution.py
@@ -12,6 +12,7 @@
 MODEL_WIDTH = 3584
 RERUN_QUERIES = 16
 TQ = 32
+SPLIT = 1024
 PB_PA = ("pb_0", "pb_1", "pa_0", "pa_1")
 CHIPS = ("pb_0", "pa_0", "pa_1")
 
@@ -63,39 +64,33 @@
 
 
 def layer_forward_kernel(
-    context, half_weight, residual, down, up, hidden, narrow, hidden_up, inverse,
+    context, weight_a, weight_b, residual, down, up, hidden, narrow, hidden_up, inverse,
     own, other, own_sem, send_sem, recv_sem, squares,
 ):
     core = lax.axis_index("pb_1")
     twin = (lax.axis_index("pb_0"), 1 - core, lax.axis_index("pa_0"), lax.axis_index("pa_1"))
     tile = own.shape[2]
-    half = half_weight.shape[1]
-    tiles = half // tile
+    tiles_a = weight_a.shape[1] // tile
+    tiles_b = weight_b.shape[1] // tile
+    half = weight_a.shape[1] + weight_b.shape[1]
+    tiles = tiles_a + tiles_b
     barrier = pltpu.get_barrier_semaphore()
     pl.semaphore_signal(barrier, inc=1, device_id=twin, device_id_type=MESH)
     pl.semaphore_wait(barrier, 1)
 
-    def columns(j):
-        return pl.ds(pl.multiple_of(j * tile, tile), tile)
-
-    def sent(j):
+    def tile_of(j):
+        source, k = (weight_a, j) if j < tiles_a else (weight_b, j - tiles_a)
+        return source.at[:, k * tile : (k + 1) * tile]
+
+    def sent(j, source):
         return pltpu.make_async_remote_copy(
-            half_weight.at[:, columns(j)], other.at[j], send_sem.at[j], recv_sem.at[j],
+            source, other.at[j], send_sem.at[j], recv_sem.at[j],
             device_id=twin, device_id_type=MESH,
         )
 
-    def fetched(j):
-        return pltpu.make_async_copy(
-            half_weight.at[:, columns(j)], own.at[lax.rem(j, 2)], own_sem.at[lax.rem(j, 2)]
-        )
-
-    fetched(0).start()
-
-    def send(j, carry):
-        sent(j).start()
-        return carry
-
-    lax.fori_loop(0, tiles, send, 0)
+    for j in range(tiles):
+        pltpu.make_async_copy(tile_of(j), own.at[j], own_sem.at[j]).start()
+        sent(j, tile_of(j)).start()
     low = lax.dot_general(
         context[...], down[...], (((1,), (1,)), ((), ())), preferred_element_type=f32
     ).astype(bf16)
@@ -119,19 +114,14 @@
         )
 
     def own_step(j, carry):
-        fetched(j).wait()
-
-        @pl.when(j + 1 < tiles)
-        def _():
-            fetched(j + 1).start()
-
-        step(own[lax.rem(j, 2)], core * half + j * tile)
+        pltpu.make_async_copy(own.at[j], own.at[j], own_sem.at[j]).wait()
+        step(own[j], core * half + j * tile)
         return carry
 
     lax.fori_loop(0, tiles, own_step, 0)
 
     def other_step(j, carry):
-        sent(j).wait_recv()
+        sent(j, own.at[j]).wait_recv()
         step(other[j], (1 - core) * half + j * tile)
         return carry
 
@@ -139,19 +129,20 @@
     inverse[...] = lax.rsqrt(squares[...] / MODEL_WIDTH + epsilon)
 
     def done(j, carry):
-        sent(j).wait_send()
+        sent(j, own.at[j]).wait_send()
         return carry
 
     lax.fori_loop(0, tiles, done, 0)
 
 
-def layer_forward(context, half_weight, residual, down, up):
+def layer_forward(context, weight_a, weight_b, residual, down, up):
     tokens, width = context.shape
-    half = half_weight.shape[1]
+    half = weight_a.shape[1] + weight_b.shape[1]
     tile = 256
     tiles = half // tile
     rank = up.shape[0]
     vmem = pl.BlockSpec(memory_space=pltpu.VMEM)
+    hbm = pl.BlockSpec(memory_space=pltpu.HBM)
     return pl.pallas_call(
         layer_forward_kernel,
         out_shape=(
@@ -160,22 +151,22 @@
             jax.ShapeDtypeStruct((tokens, rank), f32),
             jax.ShapeDtypeStruct((tokens, 1), f32),
         ),
-        in_specs=[vmem, pl.BlockSpec(memory_space=pl.ANY), vmem, vmem, vmem],
+        in_specs=[vmem, hbm, hbm, vmem, vmem, vmem],
         out_specs=(vmem, vmem, vmem, vmem),
         scratch_shapes=[
-            pltpu.VMEM((2, width, tile), bf16),
             pltpu.VMEM((tiles, width, tile), bf16),
-            pltpu.SemaphoreType.DMA((2,)),
+            pltpu.VMEM((tiles, width, tile), bf16),
+            pltpu.SemaphoreType.DMA((tiles,)),
             pltpu.SemaphoreType.DMA((tiles,)),
             pltpu.SemaphoreType.DMA((tiles,)),
             pltpu.VMEM((tokens, 1), f32),
         ],
         compiler_params=pltpu.CompilerParams(
-            collective_id=1, has_side_effects=True, vmem_limit_bytes=44 * 1024 * 1024
+            collective_id=1, has_side_effects=True, vmem_limit_bytes=58 * 1024 * 1024
         ),
         cost_estimate=pl.CostEstimate(flops=1000, bytes_accessed=1000, transcendentals=0),
         name="layer_forward",
-    )(context, half_weight, residual, down, up)
+    )(context, weight_a, weight_b, residual, down, up)
 
 
 def torus_place():
@@ -420,7 +411,7 @@
             dma((4,)),
         ],
         compiler_params=pltpu.CompilerParams(
-            collective_id=2, has_side_effects=True, vmem_limit_bytes=44 * 1024 * 1024
+            collective_id=2, has_side_effects=True, vmem_limit_bytes=58 * 1024 * 1024
         ),
         name="far_forward",
     )(arrived, passages, near_mass[:, None], key.reshape(-1)[:, None])
@@ -663,7 +654,7 @@
             dma((2, 4)),
         ],
         compiler_params=pltpu.CompilerParams(
-            collective_id=3, has_side_effects=True, vmem_limit_bytes=44 * 1024 * 1024
+            collective_id=3, has_side_effects=True, vmem_limit_bytes=58 * 1024 * 1024
         ),
         name="tail",
     )(returned, mix, near_part, norm, hidden, context, up, narrow, hidden_up, inverse)
@@ -713,7 +704,8 @@
     arrived = exchange(outgoing.reshape(device_count, slot_rows, MODEL_WIDTH))
     arrived = arrived.reshape(-1, MODEL_WIDTH)
 
-    half_weight = lax.all_gather(weight_rows, CHIPS, axis=0, tiled=True)
+    weight_a = lax.all_gather(weight_rows[:, :SPLIT], CHIPS, axis=0, tiled=True)
+    weight_b = lax.all_gather(weight_rows[:, SPLIT:], CHIPS, axis=0, tiled=True)
     near_scores = dot(queries, passages.T) * score_scale
     near_peak = jnp.max(near_scores, axis=1)
     near_exp = jnp.exp(near_scores - near_peak[:, None])
@@ -742,7 +734,7 @@
     near_grad = lax.dot_general(near_weight, queries, product_dims, preferred_element_type=f32)
 
     hidden_low, narrow, hidden_up, inverse_rms = layer_forward(
-        context, half_weight, residual, adapter_down_weight.T, adapter_up_weight
+        context, weight_a, weight_b, residual, adapter_down_weight.T, adapter_up_weight
     )
     grad_passages = loss_scale * score_scale * (far_grad + near_grad)
 

time: 311 us -> 363 us (1.17)
  waiting for transfers between devices: 127 us -> 189 us
  local copies, waits for them, and re-layouts: 18.7 us -> 7.27 us
    all_gather x1 -> x2, waiting for transfers between devices: 30.3 us -> 107 us  [the longest x1 107 us: local(): weight_a = lax.all_gather(weight_rows[:, :SPLIT], CHIPS, axis=0, tiled=True)]
    all_to_all x2, waiting for transfers between devices: 97.2 us -> 81.9 us  [exchange(): return lax.all_to_all(array, PB_PA, split_axis=0, concat_axis=0, tiled=True)]
    unnamed x56 -> x12, local copies, waits for them, and re-layouts: 17.2 us -> 3.65 us
  transfers between devices with their start and end apart: 5 -> 6, of which waited for: 3 -> 2; matrix products, arithmetic and copies ran while one was open for 10% -> 9% of each run, Pallas kernels for 21% -> 18%
where the time goes in v6:
time: 363 us; the launch traced here: 362 us
  waiting for transfers between devices  189 us (52%)
  Pallas kernels  95.9 us (26%)
  matrix products  24.8 us (7%)
  starting transfers between devices  23.8 us (7%)
  between operations  14.3 us (4%)
  local copies, waits for them, and re-layouts  7.27 us (2%)
  other arithmetic  7.25 us (2%)
    all_gather x1, waiting for transfers between devices, local(): weight_a = lax.all_gather(weight_rows[:, :SPLIT], CHIPS, axis=0, tiled=True)  107 us
    all_to_all x2, waiting for transfers between devices, exchange(): return lax.all_to_all(array, PB_PA, split_axis=0, concat_axis=0, tiled=True)  81.9 us
    pallas_call x1, Pallas kernels, far_forward(): pl.pallas_call(functools.partial(far_kernel, score_scale), out_shape=(jax...  40 us
    pallas_call x1, Pallas kernels, tail(): pl.pallas_call(functools.partial(tail_kernel, scale), out_shape=(jax.Shap...  29 us
    pallas_call x1, Pallas kernels, layer_forward(): pl.pallas_call(layer_forward_kernel, out_shape=(jax.ShapeDtypeStruct((tok...  27 us
    all_to_all x2, starting transfers between devices, exchange(): return lax.all_to_all(array, PB_PA, split_axis=0, concat_axis=0, tiled=True)  17.5 us
    dot_general x2, matrix products, dot(): return jnp.dot(a, b, preferred_element_type=f32, **kw)  8.71 us
  transfers between devices with their start and end apart: 6, of which 2 were waited for; matrix products, arithmetic and copies ran while one was open for 9% of the time, Pallas kernels for 18%

profile of v6, /device:TPU:1, one launch (start us, length us, event | category | flops | bytes accessed | tf_op | source)
XLA Modules:
  0.0 362.3 jit_solution(7750510507368571253)
XLA Ops:
  7.2 1.0 broadcast_select_fusion.2
  8.3 3.8 %collective-permute-start.1 = (bf16[28,1792]{1,0:T(8,128)(2,1)S(1)}, bf16[28,1792]{1,0:T(8,128)(2,1)S(1)}, u32[]{:S(2)}, u32[]{:S(2)}) collective-permute-start(bf16[28,1792]{1,0:T(8,128)(2,1)S(1)} %get-tuple-element.46), channel_id=1, source_target_pairs={{0,16},{1,0},{2,17},{3,1},{4,18},{5,2},{6,19},{7,3},{8,20},{9,4},{... | collective-permute-start | bytes 301064 | tf_op jit(solution)/shard_map/ppermute | solution.py:51
  12.1 2.5 collective-permute-start
  14.6 0.8 copy.33
  15.5 0.2 convert_reduce_fusion
  15.7 0.1 reduce_sum.23
  16.0 0.1 mul.71
  16.1 5.1 %fusion.5 = bf16[1024,3584]{1,0:T(8,128)(2,1)} fusion(bf16[128,3584]{1,0:T(8,128)(2,1)S(1)} %copy-done, s32[128]{0:T(128)S(1)} %get-tuple-element.51, s32[128]{0:T(128)S(1)} %get-tuple-element.52, s32[128]{0:T(128)S(1)} %get-tuple-element.53, s32[128]{0:T(128)S(1)} %get-tuple-element.50), kind=kOutput, calls=%fused_computation.14 | convolution fusion | flops 940441600 | bytes 8259584 | tf_op jit(solution)/shard_map/dot_general | solution.py:699
  21.3 0.7 pad_maximum_fusion
  21.9 11.6 %all-to-all-start = ((bf16[128,8,3584]{2,1,0:T(8,128)(2,1)}), bf16[128,8,3584]{2,1,0:T(8,128)(2,1)}, u32[]{:S(2)}, u32[]{:S(2)}) async-start(bf16[128,8,3584]{2,1,0:T(8,128)(2,1)} %bitcast.27), calls=%async_computation | async-start | bytes 14680064 | tf_op jit(solution)/shard_map/all_to_all | solution.py:63
  33.6 0.7 fusion.20
  34.5 0.9 copy.37.key_column
  35.3 3.5 fusion.28
  38.8 0.1 copy.36
  38.9 0.2 fusion.16
  39.1 0.1 copy.35
  39.2 0.6 log_add_fusion.near_mass
  39.8 81.9 %all-to-all-done = bf16[128,8,3584]{2,1,0:T(8,128)(2,1)} async-done(((bf16[128,8,3584]{2,1,0:T(8,128)(2,1)}), bf16[128,8,3584]{2,1,0:T(8,128)(2,1)}, u32[]{:S(2)}, u32[]{:S(2)}) %all-to-all-start) | async-done | bytes 7340064 | tf_op jit(solution)/shard_map/all_to_all | solution.py:63
  121.7 40.0 %far_forward.1 = (bf16[1024,3584]{1,0:T(8,128)(2,1)}, f32[1024,512]{1,0:T(8,128)}, bf16[256,1024]{1,0:T(8,128)(2,1)}, f32[128,1]{1,0:T(8,128)}, f32[1024,1]{1,0:T(8,128)}) custom-call(bf16[1024,3584]{1,0:T(8,128)(2,1)} %bitcast.6.arrived, bf16[512,3584]{1,0:T(8,128)(2,1)} %passages_in.1, f32[128,1]{1,0:T(8,128)} %log_add_fusion.near_mass, ...), custom_call_target="tpu_custom_call" | custom-call | tf_op jit(solution)/shard_map/far_forward/pallas_call | solution.py:382
  161.7 5.9 %all-to-all-start.1 = ((bf16[128,8,3584]{2,1,0:T(8,128)(2,1)}), bf16[128,8,3584]{2,1,0:T(8,128)(2,1)}, u32[]{:S(2)}, u32[]{:S(2)}) async-start(bf16[128,8,3584]{2,1,0:T(8,128)(2,1)} %bitcast.28), calls=%async_computation.1 | async-start | bytes 14680064 | tf_op jit(solution)/shard_map/all_to_all | solution.py:63
  167.6 0.6 reshape.83.norm
  168.3 5.3 %fusion.7 = f32[256,3584]{1,0:T(8,128)} fusion(bf16[512,3584]{1,0:T(8,128)(2,1)} %passages_in.1, bf16[128,512]{1,0:T(8,128)(2,1)S(1)} %fusion.11, bf16[128,512]{1,0:T(8,128)(2,1)S(1)} %get-tuple-element.42), kind=kOutput, calls=%fused_computation.15 | convolution fusion | flops 940048384 | bytes 7602176 | tf_op jit(solution)/shard_map/dot_general | solution.py:30
  173.6 1.2 reduce.1
  174.8 1.0 fusion.26
  175.8 6.6 %fusion = f32[512,3584]{1,0:T(8,128)S(1)} fusion(f32[1024,512]{1,0:T(8,128)S(1)} %copy-done.2, f32[1024]{0:T(1024)S(1)} %reduce.1, bf16[128,8,3584]{2,1,0:T(8,128)(2,1)} %all-to-all-done), kind=kOutput, calls=%fused_computation.5 | convolution fusion | flops 3759144960 | bytes 16781312 | tf_op jit(solution)/shard_map/dot_general | solution.py:733
  182.5 4.3 %add_multiply_fusion = f32[512,3584]{1,0:T(8,128)} fusion(f32[512,3584]{1,0:T(8,128)S(1)} %fusion, bf16[128,3584]{1,0:T(8,128)(2,1)S(1)} %copy-done, f32[128,512]{1,0:T(8,128)S(1)} %get-tuple-element.55, f32[128]{0:T(128)S(1)} %get-tuple-element.40, s32[128]{0:T(128)S(1)} %copy-done.4), kind=kOutput, calls=%fused_computation | convolution fusion | flops 473759744 | bytes 15860736 | tf_op jit(solution)/shard_map/dot_general | solution.py:734
  186.8 1.5 slice_subtract_fusion.near_part
  188.3 107.0 %all-gather.3.cloned.1.call-done.weight_a = bf16[3584,1024]{1,0:T(8,128)(2,1)} async-done(((bf16[56,1024]{1,0:T(8,128)(2,1)}), bf16[3584,1024]{1,0:T(8,128)(2,1)}) %all-gather.3.cloned.1.call-update) | async-done | bytes 7340048 | tf_op jit(solution)/shard_map/all_gather | solution.py:707
  295.3 27.0 %layer_forward.1 = (bf16[512,3584]{1,0:T(8,128)(2,1)}, f32[512,16]{1,0:T(8,128)}, f32[512,16]{1,0:T(8,128)}, f32[512,1]{1,0:T(8,128)}) custom-call(bf16[512,3584]{1,0:T(8,128)(2,1)} %context.3, bf16[3584,1024]{1,0:T(8,128)(2,1)} %all-gather.3.cloned.1.call-done.weight_a, bf16[3584,768]{1,0:T(8,128)(2,1)} %all-gather.5.cloned.1.call-done.weight_b, ...), custom_call_target="tpu_custom_call" | custom-call | flops 1000 | bytes 1000 | tf_op jit(solution)/shard_map/layer_forward/pallas_call | solution.py:146
  322.3 29.0 %tail.1 = (f32[128,3584]{1,0:T(8,128)}, f32[32,128]{1,0:T(8,128)}) custom-call(bf16[1024,3584]{1,0:T(8,128)(2,1)} %bitcast.11.returned, bf16[256,1024]{1,0:T(8,128)(2,1)} %get-tuple-element.31.mix, f32[128,3584]{1,0:T(8,128)} %slice_subtract_fusion.near_part, f32[1,3584]{1,0:T(1,128)} %reshape.83.norm, bf16[512,3584]{1,0:T(8,128)(2,1)} %get-tuple-element.33.hidden, ...), custom_call_target="tpu_custom_call" | custom-call | tf_op jit(solution)/shard_map/tail/pallas_call | solution.py:627
  351.3 1.3 fusion.27
  352.6 2.9 copy.40
  (31 shorter events, 0.7 us)
Async XLA Ops:
  7.2 9.0 %copy-start = (bf16[128,3584]{1,0:T(8,128)(2,1)S(1)}, bf16[128,3584]{1,0:T(8,128)(2,1)}, u32[]{:S(2)}) copy-start(bf16[128,3584]{1,0:T(8,128)(2,1)} %param.10) | copy-start | bytes 2752516
  7.2 181.1 %all-gather.5.cloned.1.call-start = ((), (), s32[]{:S(2)}) async-start(), calls=%async_computation.3 | async-start | bytes 5591040 | tf_op jit(solution)/shard_map/all_gather | solution.py:708
  8.3 13.0 %collective-permute-start.1 = (bf16[28,1792]{1,0:T(8,128)(2,1)S(1)}, bf16[28,1792]{1,0:T(8,128)(2,1)S(1)}, u32[]{:S(2)}, u32[]{:S(2)}) collective-permute-start(bf16[28,1792]{1,0:T(8,128)(2,1)S(1)} %get-tuple-element.46), channel_id=1, source_target_pairs={{0,16},{1,0},{2,17},{3,1},{4,18},{5,2},{6,19},{7,3},{8,20},{9,4},{... | collective-permute-start | bytes 301064 | tf_op jit(solution)/shard_map/ppermute | solution.py:51
  12.1 9.1 %collective-permute-start = (bf16[28,1792]{1,0:T(8,128)(2,1)S(1)}, bf16[28,1792]{1,0:T(8,128)(2,1)S(1)}, u32[]{:S(2)}, u32[]{:S(2)}) collective-permute-start(bf16[28,1792]{1,0:T(8,128)(2,1)S(1)} %get-tuple-element.47), channel_id=1, source_target_pairs={{0,0},{1,16},{2,1},{3,17},{4,2},{5,18},{6,3},{7,19},{8,4},{9,20},{... | collective-permute-start | bytes 301064 | tf_op jit(solution)/shard_map/ppermute | solution.py:50
  21.9 99.8 %all-to-all-start = ((bf16[128,8,3584]{2,1,0:T(8,128)(2,1)}), bf16[128,8,3584]{2,1,0:T(8,128)(2,1)}, u32[]{:S(2)}, u32[]{:S(2)}) async-start(bf16[128,8,3584]{2,1,0:T(8,128)(2,1)} %bitcast.27), calls=%async_computation | async-start | bytes 14680064 | tf_op jit(solution)/shard_map/all_to_all | solution.py:63
  33.6 261.7 %all-gather.3.cloned.1.call-start = ((), (), s32[]{:S(2)}) async-start(), calls=%async_computation.2 | async-start | bytes 7454720 | tf_op jit(solution)/shard_map/all_gather | solution.py:707
  161.7 5.9 %copy-start.3 = (bf16[3584]{0:T(1024)(128)(2,1)S(1)}, bf16[3584]{0:T(1024)(128)(2,1)}, u32[]{:S(2)}) copy-start(bf16[3584]{0:T(1024)(128)(2,1)} %param.19) | copy-start | bytes 21508
  161.7 6.5 %copy-start.4 = (s32[128]{0:T(128)S(1)}, s32[128]{0:T(128)}, u32[]{:S(2)}) copy-start(s32[128]{0:T(128)} %param.13) | copy-start | bytes 1540
  161.7 160.5 %all-to-all-start.1 = ((bf16[128,8,3584]{2,1,0:T(8,128)(2,1)}), bf16[128,8,3584]{2,1,0:T(8,128)(2,1)}, u32[]{:S(2)}, u32[]{:S(2)}) async-start(bf16[128,8,3584]{2,1,0:T(8,128)(2,1)} %bitcast.28), calls=%async_computation.1 | async-start | bytes 14680064 | tf_op jit(solution)/shard_map/all_to_all | solution.py:63
  168.3 7.5 %copy-start.2 = (f32[1024,512]{1,0:T(8,128)S(1)}, f32[1024,512]{1,0:T(8,128)}, u32[]{:S(2)}) copy-start(f32[1024,512]{1,0:T(8,128)} %get-tuple-element.28) | copy-start | bytes 6291460
  182.5 4.3 %copy-start.1 = (f32[256,3584]{1,0:T(8,128)S(1)}, f32[256,3584]{1,0:T(8,128)}, u32[]{:S(2)}) copy-start(f32[256,3584]{1,0:T(8,128)} %fusion.7) | copy-start | bytes 11010052
Sparse Core Ops, SparseCore 0:
  22.1 133.0 all-gather.4
  157.9 137.2 all-gather.2

commit v7 on v5

--- a/solution.py
+++ b/solution.py
@@ -64,7 +64,7 @@
 
 def layer_forward_kernel(
     context, half_weight, residual, down, up, hidden, narrow, hidden_up, inverse,
-    own, other, own_sem, send_sem, recv_sem, squares,
+    own, other, block, own_sem, send_sem, recv_sem, out_sem, squares,
 ):
     core = lax.axis_index("pb_1")
     twin = (lax.axis_index("pb_0"), 1 - core, lax.axis_index("pa_0"), lax.axis_index("pa_1"))
@@ -103,7 +103,12 @@
     squares[...] = jnp.zeros_like(squares)
     hidden_up[...] = jnp.zeros_like(hidden_up)
 
-    def step(weight, start):
+    def stored(columns, k):
+        return pltpu.make_async_copy(
+            block.at[:, columns], hidden.at[:, columns], out_sem.at[k]
+        )
+
+    def step(weight, start, k):
         at = pl.ds(pl.multiple_of(start, tile), tile)
         up_tile = up[:, at]
         value = (
@@ -113,7 +118,8 @@
         )
         squares[...] += jnp.sum(value * value, axis=1, keepdims=True)
         value = value.astype(bf16)
-        hidden[:, at] = value
+        block[:, at] = value
+        stored(at, k).start()
         hidden_up[...] += lax.dot_general(
             value, up_tile, (((1,), (1,)), ((), ())), preferred_element_type=f32
         )
@@ -125,14 +131,14 @@
         def _():
             fetched(j + 1).start()
 
-        step(own[lax.rem(j, 2)], core * half + j * tile)
+        step(own[lax.rem(j, 2)], core * half + j * tile, j)
         return carry
 
     lax.fori_loop(0, tiles, own_step, 0)
 
     def other_step(j, carry):
         sent(j).wait_recv()
-        step(other[j], (1 - core) * half + j * tile)
+        step(other[j], (1 - core) * half + j * tile, tiles + j)
         return carry
 
     lax.fori_loop(0, tiles, other_step, 0)
@@ -140,6 +146,8 @@
 
     def done(j, carry):
         sent(j).wait_send()
+        stored(columns(j), j).wait()
+        stored(columns(j), tiles + j).wait()
         return carry
 
     lax.fori_loop(0, tiles, done, 0)
@@ -161,17 +169,19 @@
             jax.ShapeDtypeStruct((tokens, 1), f32),
         ),
         in_specs=[vmem, pl.BlockSpec(memory_space=pl.ANY), vmem, vmem, vmem],
-        out_specs=(vmem, vmem, vmem, vmem),
+        out_specs=(pl.BlockSpec(memory_space=pltpu.HBM), vmem, vmem, vmem),
         scratch_shapes=[
             pltpu.VMEM((2, width, tile), bf16),
             pltpu.VMEM((tiles, width, tile), bf16),
+            pltpu.VMEM((tokens, width), bf16),
             pltpu.SemaphoreType.DMA((2,)),
             pltpu.SemaphoreType.DMA((tiles,)),
             pltpu.SemaphoreType.DMA((tiles,)),
+            pltpu.SemaphoreType.DMA((2 * tiles,)),
             pltpu.VMEM((tokens, 1), f32),
         ],
         compiler_params=pltpu.CompilerParams(
-            collective_id=1, has_side_effects=True, vmem_limit_bytes=44 * 1024 * 1024
+            collective_id=1, has_side_effects=True, vmem_limit_bytes=58 * 1024 * 1024
         ),
         cost_estimate=pl.CostEstimate(flops=1000, bytes_accessed=1000, transcendentals=0),
         name="layer_forward",
@@ -196,8 +206,8 @@
 
 
 def far_kernel(
-    score_scale, arrived, passages_in, near_mass, key_column, mean, scores, mix, log_total,
-    log_column, rows, passages, weights, inverse, means, mass, log_out, mass1, mass2, mass3, log1,
+    score_scale, arrived, passages_in, near_mass, key_column, mean, scores_out, mix_out, log_total,
+    log_column, scores, mix, score_sem, mix_sem, rows, passages, weights, inverse, means, mass, log_out, mass1, mass2, mass3, log1,
     log2, log3, row_sem, passage_sem, mean_sem, send_sem, recv_sem,
 ):
     place = torus_place()
@@ -231,6 +241,12 @@
     def went_out(c):
         return pltpu.make_async_copy(means.at[part(c)], mean.at[part(c)], mean_sem.at[c])
 
+    def scores_stored(c):
+        return pltpu.make_async_copy(
+            scores.at[part(c)], scores_out.at[part(c)], score_sem.at[c]
+        )
+
+    mix_stored = pltpu.make_async_copy(mix, mix_out, mix_sem)
     passages_here = pltpu.make_async_copy(passages_in, passages, passage_sem)
     passages_here.start()
     for c in range(chunks):
@@ -255,6 +271,7 @@
             preferred_element_type=f32,
         )
         scores[part(c), :] = value
+        scores_stored(c).start()
         peak = jnp.max(value, axis=1, keepdims=True)
         weight = jnp.exp(value - peak)
         total = jnp.sum(weight, axis=1, keepdims=True)
@@ -354,6 +371,7 @@
     high = shares.astype(bf16)
     mix[:query_count, :] = high
     mix[query_count:, :] = (shares - high.astype(f32)).astype(bf16)
+    mix_stored.start()
     others(log_out, log1, 2).wait_recv()
     repack(log1, log2)
     hop2(log2, log3, 3)
@@ -368,6 +386,8 @@
     )
     for c in range(chunks):
         went_out(c).wait()
+        scores_stored(c).wait()
+    mix_stored.wait()
     others(mass, mass1, 0).wait_send()
     others(mass2, mass3, 1).wait_send()
     others(log_out, log1, 2).wait_send()
@@ -398,8 +418,12 @@
             jax.ShapeDtypeStruct((all_rows, 1), f32),
         ),
         in_specs=[hbm, hbm, vmem, vmem],
-        out_specs=(hbm, vmem, vmem, vmem, vmem),
+        out_specs=(hbm, hbm, hbm, vmem, vmem),
         scratch_shapes=[
+            pltpu.VMEM((all_rows, passage_count), f32),
+            pltpu.VMEM((2 * query_count, all_rows), bf16),
+            dma((chunks,)),
+            dma(()),
             pltpu.VMEM((all_rows, width), bf16),
             pltpu.VMEM((passage_count, width), bf16),
             pltpu.VMEM((all_rows, passage_count), bf16),
@@ -420,15 +444,15 @@
             dma((4,)),
         ],
         compiler_params=pltpu.CompilerParams(
-            collective_id=2, has_side_effects=True, vmem_limit_bytes=44 * 1024 * 1024
+            collective_id=2, has_side_effects=True, vmem_limit_bytes=58 * 1024 * 1024
         ),
         name="far_forward",
     )(arrived, passages, near_mass[:, None], key.reshape(-1)[:, None])
 
 
 def tail_kernel(
-    gradient_scale, returned, mix, near_part, norm, hidden, context, up, narrow, hidden_up, inverse,
-    gradient, piece, rows, hid, ctx, grad, scaled, products, scaled_up, terms, first, part, second,
+    gradient_scale, returned, mix_in, near_in, norm, hidden, context, up, narrow_in, hidden_up_in,
+    inverse_in, gradient, piece, mix, near_part, narrow, hidden_up, inverse, small_sem, near_sem, rows, hid, ctx, grad, scaled, products, scaled_up, terms, first, part, second,
     row_sem, hid_sem, ctx_sem, grad_sem, send1, recv1, send2, recv2,
 ):
     place = torus_place()
@@ -458,10 +482,28 @@
 
     hid_in = pltpu.make_async_copy(hidden, hid, hid_sem)
     ctx_in = pltpu.make_async_copy(context, ctx, ctx_sem)
+    mix_here = pltpu.make_async_copy(mix_in, mix, small_sem.at[0])
+    small_here = [
+        pltpu.make_async_copy(source, target, small_sem.at[1 + k])
+        for k, (source, target) in enumerate(
+            ((narrow_in, narrow), (hidden_up_in, hidden_up), (inverse_in, inverse))
+        )
+    ]
+
+    def near_here(j):
+        return pltpu.make_async_copy(
+            near_in.at[:, at(j)], near_part.at[:, at(j)], near_sem.at[j]
+        )
+
+    mix_here.start()
     came_in(0).start()
+    near_here(0).start()
     hid_in.start()
     for j in range(1, tiles):
         came_in(j).start()
+        near_here(j).start()
+    for copy in small_here:
+        copy.start()
     ctx_in.start()
     barrier = pltpu.get_barrier_semaphore()
 
@@ -489,10 +531,12 @@
 
     products[...] = jnp.zeros_like(products)
     scaled_up[...] = jnp.zeros_like(scaled_up)
+    mix_here.wait()
     hid_in.wait()
 
     def mixing(j, carry):
         came_in(j).wait()
+        near_here(j).wait()
         both = jnp.dot(mix[...], rows[:, at(j)], preferred_element_type=f32)
         value = gradient_scale * (both[:query_count] + both[query_count:] + near_part[:, at(j)])
         grad[:, at(j)] = value
@@ -508,6 +552,8 @@
     gradient_out = pltpu.make_async_copy(grad, gradient, grad_sem)
     gradient_out.start()
 
+    for copy in small_here:
+        copy.wait()
     token_query = lax.broadcasted_iota(jnp.int32, (tokens, rerun), 0) // TQ
     of_query = token_query == lax.broadcasted_iota(jnp.int32, (tokens, rerun), 1)
     hot = jnp.where(of_query, 1.0, 0.0)
@@ -639,9 +685,16 @@
             jax.ShapeDtypeStruct((query_count, width), f32),
             jax.ShapeDtypeStruct((2 * rank, lanes), f32),
         ),
-        in_specs=[hbm, vmem, vmem, vmem, hbm, hbm, vmem, vmem, vmem, vmem],
+        in_specs=[hbm, hbm, hbm, vmem, hbm, hbm, vmem, hbm, hbm, hbm],
         out_specs=(hbm, vmem),
         scratch_shapes=[
+            pltpu.VMEM(mix.shape, bf16),
+            pltpu.VMEM(near_part.shape, f32),
+            pltpu.VMEM(narrow.shape, f32),
+            pltpu.VMEM(hidden_up.shape, f32),
+            pltpu.VMEM(inverse.shape, f32),
+            dma((4,)),
+            dma((tiles,)),
             pltpu.VMEM((all_rows, width), bf16),
             pltpu.VMEM((tokens, width), bf16),
             pltpu.VMEM((tokens, width), bf16),
@@ -663,7 +716,7 @@
             dma((2, 4)),
         ],
         compiler_params=pltpu.CompilerParams(
-            collective_id=3, has_side_effects=True, vmem_limit_bytes=44 * 1024 * 1024
+            collective_id=3, has_side_effects=True, vmem_limit_bytes=58 * 1024 * 1024
         ),
         name="tail",
     )(returned, mix, near_part, norm, hidden, context, up, narrow, hidden_up, inverse)

time: 311 us -> 313 us (level)
  local copies, waits for them, and re-layouts: 18.7 us -> 7.27 us
  Pallas kernels: 95.3 us -> 105 us
    unnamed x56 -> x14, local copies, waits for them, and re-layouts: 17.2 us -> 3.66 us
    pallas_call x1, Pallas kernels: 36.5 us -> 40.5 us  [far_forward(): pl.pallas_call(functools.partial(far_kernel, score_scale), out_shape=(jax...]
  transfers between devices with their start and end apart: 5 -> 5, of which waited for: 3 -> 3; matrix products, arithmetic and copies ran while one was open for 10% -> 11% of each run, Pallas kernels for 21% -> 23%
where the time goes in v7:
time: 313 us; the launch traced here: 311 us
  waiting for transfers between devices  128 us (41%)
  Pallas kernels  105 us (34%)
  matrix products  24.8 us (8%)
  starting transfers between devices  24.4 us (8%)
  between operations  14.3 us (5%)
  local copies, waits for them, and re-layouts  7.27 us (2%)
  other arithmetic  6.65 us (2%)
    all_to_all x2, waiting for transfers between devices, exchange(): return lax.all_to_all(array, PB_PA, split_axis=0, concat_axis=0, tiled=True)  99.7 us
    pallas_call x1, Pallas kernels, far_forward(): pl.pallas_call(functools.partial(far_kernel, score_scale), out_shape=(jax...  40.5 us
    pallas_call x1, Pallas kernels, tail(): pl.pallas_call(functools.partial(tail_kernel, scale), out_shape=(jax.Shap...  33.8 us
    pallas_call x1, Pallas kernels, layer_forward(): pl.pallas_call(layer_forward_kernel, out_shape=(jax.ShapeDtypeStruct((tok...  30.7 us
    all_gather x1, waiting for transfers between devices, local(): half_weight = lax.all_gather(weight_rows, CHIPS, axis=0, tiled=True)  28.4 us
    all_to_all x2, starting transfers between devices, exchange(): return lax.all_to_all(array, PB_PA, split_axis=0, concat_axis=0, tiled=True)  18.1 us
    dot_general x2, matrix products, dot(): return jnp.dot(a, b, preferred_element_type=f32, **kw)  8.73 us
    dot_general x1, matrix products, local(): lax.dot_general(far_weight, arrived, product_dims, preferred_element_type...  6.63 us
  transfers between devices with their start and end apart: 5, of which 3 were waited for; matrix products, arithmetic and copies ran while one was open for 11% of the time, Pallas kernels for 23%

profile of v7, /device:TPU:1, one launch (start us, length us, event | category | flops | bytes accessed | tf_op | source)
XLA Modules:
  0.0 310.6 jit_solution(336392161620767164)
XLA Ops:
  7.2 1.0 broadcast_select_fusion.2
  8.3 3.8 %collective-permute-start.1 = (bf16[28,1792]{1,0:T(8,128)(2,1)S(1)}, bf16[28,1792]{1,0:T(8,128)(2,1)S(1)}, u32[]{:S(2)}, u32[]{:S(2)}) collective-permute-start(bf16[28,1792]{1,0:T(8,128)(2,1)S(1)} %get-tuple-element.46), channel_id=1, source_target_pairs={{0,16},{1,0},{2,17},{3,1},{4,18},{5,2},{6,19},{7,3},{8,20},{9,4},{... | collective-permute-start | bytes 301064 | tf_op jit(solution)/shard_map/ppermute | solution.py:50
  12.1 2.5 collective-permute-start
  14.6 0.8 copy.33
  15.5 0.2 convert_reduce_fusion
  15.7 0.1 reduce_sum.23
  16.0 0.1 mul.71
  16.1 5.1 %fusion.5 = bf16[1024,3584]{1,0:T(8,128)(2,1)} fusion(bf16[128,3584]{1,0:T(8,128)(2,1)S(1)} %copy-done, s32[128]{0:T(128)S(1)} %get-tuple-element.51, s32[128]{0:T(128)S(1)} %get-tuple-element.52, s32[128]{0:T(128)S(1)} %get-tuple-element.53, s32[128]{0:T(128)S(1)} %get-tuple-element.50), kind=kOutput, calls=%fused_computation.14 | convolution fusion | flops 940441600 | bytes 8259584 | tf_op jit(solution)/shard_map/dot_general | solution.py:761
  21.3 0.7 pad_maximum_fusion
  22.0 11.6 %all-to-all-start = ((bf16[128,8,3584]{2,1,0:T(8,128)(2,1)}), bf16[128,8,3584]{2,1,0:T(8,128)(2,1)}, u32[]{:S(2)}, u32[]{:S(2)}) async-start(bf16[128,8,3584]{2,1,0:T(8,128)(2,1)} %bitcast.27), calls=%async_computation | async-start | bytes 14680064 | tf_op jit(solution)/shard_map/all_to_all | solution.py:62
  33.8 0.9 copy.37.key_column
  34.6 3.5 %fusion.27 = (f32[128]{0:T(128)S(1)}, f32[128,512]{1,0:T(8,128)S(1)}) fusion(bf16[128,3584]{1,0:T(8,128)(2,1)S(1)} %copy-done, bf16[512,3584]{1,0:T(8,128)(2,1)} %passages_in.1), kind=kOutput, calls=%fused_computation.58 | convolution fusion | flops 469892992 | bytes 4850176 | tf_op jit(solution)/shard_map/dot_general | solution.py:29
  38.1 0.1 copy.36
  38.3 0.2 fusion.16
  38.5 0.1 copy.35
  38.6 0.6 log_add_fusion.near_mass
  39.2 85.0 %all-to-all-done = bf16[128,8,3584]{2,1,0:T(8,128)(2,1)} async-done(((bf16[128,8,3584]{2,1,0:T(8,128)(2,1)}), bf16[128,8,3584]{2,1,0:T(8,128)(2,1)}, u32[]{:S(2)}, u32[]{:S(2)}) %all-to-all-start) | async-done | bytes 7340064 | tf_op jit(solution)/shard_map/all_to_all | solution.py:62
  124.2 40.5 %far_forward.1 = (bf16[1024,3584]{1,0:T(8,128)(2,1)}, f32[1024,512]{1,0:T(8,128)}, bf16[256,1024]{1,0:T(8,128)(2,1)}, f32[128,1]{1,0:T(8,128)}, f32[1024,1]{1,0:T(8,128)}) custom-call(bf16[1024,3584]{1,0:T(8,128)(2,1)} %bitcast.6.arrived, bf16[512,3584]{1,0:T(8,128)(2,1)} %passages_in.1, f32[128,1]{1,0:T(8,128)} %log_add_fusion.near_mass, ...), custom_call_target="tpu_custom_call" | custom-call | tf_op jit(solution)/shard_map/far_forward/pallas_call | solution.py:411
  164.8 6.5 %all-to-all-start.1 = ((bf16[128,8,3584]{2,1,0:T(8,128)(2,1)}), bf16[128,8,3584]{2,1,0:T(8,128)(2,1)}, u32[]{:S(2)}, u32[]{:S(2)}) async-start(bf16[128,8,3584]{2,1,0:T(8,128)(2,1)} %bitcast.28), calls=%async_computation.1 | async-start | bytes 14680064 | tf_op jit(solution)/shard_map/all_to_all | solution.py:62
  171.3 0.6 reshape.83.norm
  172.0 5.2 %fusion.7 = f32[256,3584]{1,0:T(8,128)} fusion(bf16[512,3584]{1,0:T(8,128)(2,1)} %passages_in.1, bf16[128,512]{1,0:T(8,128)(2,1)S(1)} %fusion.11, bf16[128,512]{1,0:T(8,128)(2,1)S(1)} %get-tuple-element.42), kind=kOutput, calls=%fused_computation.15 | convolution fusion | flops 940048384 | bytes 7602176 | tf_op jit(solution)/shard_map/dot_general | solution.py:29
  177.2 1.2 reduce.1
  178.4 1.0 fusion.25
  179.4 6.6 %fusion = f32[512,3584]{1,0:T(8,128)S(1)} fusion(f32[1024,512]{1,0:T(8,128)S(1)} %copy-done.3, f32[1024]{0:T(1024)S(1)} %reduce.1, bf16[128,8,3584]{2,1,0:T(8,128)(2,1)} %all-to-all-done), kind=kOutput, calls=%fused_computation.5 | convolution fusion | flops 3759144960 | bytes 16781312 | tf_op jit(solution)/shard_map/dot_general | solution.py:794
  186.1 4.3 %add_multiply_fusion = f32[512,3584]{1,0:T(8,128)} fusion(f32[512,3584]{1,0:T(8,128)S(1)} %fusion, bf16[128,3584]{1,0:T(8,128)(2,1)S(1)} %copy-done, f32[128,512]{1,0:T(8,128)S(1)} %get-tuple-element.55, f32[128]{0:T(128)S(1)} %get-tuple-element.40, s32[128]{0:T(128)S(1)} %copy-done.5), kind=kOutput, calls=%fused_computation | convolution fusion | flops 473759744 | bytes 15860736 | tf_op jit(solution)/shard_map/dot_general | solution.py:795
  190.4 1.5 slice_subtract_fusion.near_in
  191.9 28.4 %all-gather.2.cloned.1.call-done.half_weight = bf16[3584,1792]{1,0:T(8,128)(2,1)} async-done(((bf16[56,1792]{1,0:T(8,128)(2,1)}), bf16[3584,1792]{1,0:T(8,128)(2,1)}) %all-gather.2.cloned.1.call-update) | async-done | bytes 12845072 | tf_op jit(solution)/shard_map/all_gather | solution.py:769
  220.3 30.7 %layer_forward.1 = (bf16[512,3584]{1,0:T(8,128)(2,1)}, f32[512,16]{1,0:T(8,128)}, f32[512,16]{1,0:T(8,128)}, f32[512,1]{1,0:T(8,128)}) custom-call(bf16[512,3584]{1,0:T(8,128)(2,1)} %context.3, bf16[3584,1792]{1,0:T(8,128)(2,1)} %all-gather.2.cloned.1.call-done.half_weight, bf16[512,3584]{1,0:T(8,128)(2,1)} %residual.1, bf16[16,3584]{1,0:T(8,128)(2,1)} %bitcast.29, ...), custom_call_target="tpu_custom_call" | custom-call | flops 1000 | bytes 1000 | tf_op jit(solution)/shard_map/layer_forward/pallas_call | solution.py:163
  251.1 14.7 %all-to-all-done.1 = bf16[128,8,3584]{2,1,0:T(8,128)(2,1)} async-done(((bf16[128,8,3584]{2,1,0:T(8,128)(2,1)}), bf16[128,8,3584]{2,1,0:T(8,128)(2,1)}, u32[]{:S(2)}, u32[]{:S(2)}) %all-to-all-start.1) | async-done | bytes 7340064 | tf_op jit(solution)/shard_map/all_to_all | solution.py:62
  265.8 33.8 %tail.1 = (f32[128,3584]{1,0:T(8,128)}, f32[32,128]{1,0:T(8,128)}) custom-call(bf16[1024,3584]{1,0:T(8,128)(2,1)} %bitcast.11.returned, bf16[256,1024]{1,0:T(8,128)(2,1)} %get-tuple-element.31.mix_in, f32[128,3584]{1,0:T(8,128)} %slice_subtract_fusion.near_in, f32[1,3584]{1,0:T(1,128)} %reshape.83.norm, bf16[512,3584]{1,0:T(8,128)(2,1)} %get-tuple-element.33.hidden, ...), custom_call_target="tpu_custom_call" | custom-call | tf_op jit(solution)/shard_map/tail/pallas_call | solution.py:682
  299.6 1.3 fusion.26
  300.9 2.9 copy.40
  (29 shorter events, 0.6 us)
Async XLA Ops:
  7.2 9.0 %copy-start = (bf16[128,3584]{1,0:T(8,128)(2,1)S(1)}, bf16[128,3584]{1,0:T(8,128)(2,1)}, u32[]{:S(2)}) copy-start(bf16[128,3584]{1,0:T(8,128)(2,1)} %param.10) | copy-start | bytes 2752516
  7.2 213.2 %all-gather.2.cloned.1.call-start = ((), (), s32[]{:S(2)}) async-start(), calls=%async_computation.2 | async-start | bytes 13045760 | tf_op jit(solution)/shard_map/all_gather | solution.py:769
  8.3 13.0 %collective-permute-start.1 = (bf16[28,1792]{1,0:T(8,128)(2,1)S(1)}, bf16[28,1792]{1,0:T(8,128)(2,1)S(1)}, u32[]{:S(2)}, u32[]{:S(2)}) collective-permute-start(bf16[28,1792]{1,0:T(8,128)(2,1)S(1)} %get-tuple-element.46), channel_id=1, source_target_pairs={{0,16},{1,0},{2,17},{3,1},{4,18},{5,2},{6,19},{7,3},{8,20},{9,4},{... | collective-permute-start | bytes 301064 | tf_op jit(solution)/shard_map/ppermute | solution.py:50
  12.1 9.1 %collective-permute-start = (bf16[28,1792]{1,0:T(8,128)(2,1)S(1)}, bf16[28,1792]{1,0:T(8,128)(2,1)S(1)}, u32[]{:S(2)}, u32[]{:S(2)}) collective-permute-start(bf16[28,1792]{1,0:T(8,128)(2,1)S(1)} %get-tuple-element.47), channel_id=1, source_target_pairs={{0,0},{1,16},{2,1},{3,17},{4,2},{5,18},{6,3},{7,19},{8,4},{9,20},{... | collective-permute-start | bytes 301064 | tf_op jit(solution)/shard_map/ppermute | solution.py:49
  22.0 102.2 %all-to-all-start = ((bf16[128,8,3584]{2,1,0:T(8,128)(2,1)}), bf16[128,8,3584]{2,1,0:T(8,128)(2,1)}, u32[]{:S(2)}, u32[]{:S(2)}) async-start(bf16[128,8,3584]{2,1,0:T(8,128)(2,1)} %bitcast.27), calls=%async_computation | async-start | bytes 14680064 | tf_op jit(solution)/shard_map/all_to_all | solution.py:62
  164.7 6.5 %copy-start.4 = (bf16[3584]{0:T(1024)(128)(2,1)S(1)}, bf16[3584]{0:T(1024)(128)(2,1)}, u32[]{:S(2)}) copy-start(bf16[3584]{0:T(1024)(128)(2,1)} %param.19) | copy-start | bytes 21508
  164.8 7.1 %copy-start.5 = (s32[128]{0:T(128)S(1)}, s32[128]{0:T(128)}, u32[]{:S(2)}) copy-start(s32[128]{0:T(128)} %param.13) | copy-start | bytes 1540
  164.8 101.0 %all-to-all-start.1 = ((bf16[128,8,3584]{2,1,0:T(8,128)(2,1)}), bf16[128,8,3584]{2,1,0:T(8,128)(2,1)}, u32[]{:S(2)}, u32[]{:S(2)}) async-start(bf16[128,8,3584]{2,1,0:T(8,128)(2,1)} %bitcast.28), calls=%async_computation.1 | async-start | bytes 14680064 | tf_op jit(solution)/shard_map/all_to_all | solution.py:62
  172.0 7.4 %copy-start.3 = (f32[1024,512]{1,0:T(8,128)S(1)}, f32[1024,512]{1,0:T(8,128)}, u32[]{:S(2)}) copy-start(f32[1024,512]{1,0:T(8,128)} %get-tuple-element.28) | copy-start | bytes 6291460
  186.1 4.3 %copy-start.2 = (f32[256,3584]{1,0:T(8,128)S(1)}, f32[256,3584]{1,0:T(8,128)}, u32[]{:S(2)}) copy-start(f32[256,3584]{1,0:T(8,128)} %fusion.7) | copy-start | bytes 11010052
  265.8 38.0 %copy-start.1 = (bf16[128,3584]{1,0:T(8,128)(2,1)S(1)}, bf16[128,3584]{1,0:T(8,128)(2,1)}, u32[]{:S(2)}) copy-start(bf16[128,3584]{1,0:T(8,128)(2,1)} %param.10) | copy-start | bytes 2752516
Sparse Core Ops, SparseCore 0:
  22.1 198.1 all-gather.1

commit v8 on v7

--- a/solution.py
+++ b/solution.py
@@ -755,14 +755,12 @@
         jnp.arange(query_count, dtype=jnp.int32) % block_rows
     )
     row_ids = jnp.arange(all_rows, dtype=jnp.int32)
+    key, first, second = lax.optimization_barrier((key, *weight_halves_sent(output_weight)))
+    weight_rows = gather_input(first, second)
     picks = row_ids[:, None] == key[0][None, :]
     for t in range(1, hard_count):
         picks = picks | (row_ids[:, None] == key[t][None, :])
     outgoing = jnp.dot(picks.astype(bf16), queries, preferred_element_type=bf16)
-    outgoing, first, second = lax.optimization_barrier(
-        (outgoing, *weight_halves_sent(output_weight))
-    )
-    weight_rows = gather_input(first, second)
     arrived = exchange(outgoing.reshape(device_count, slot_rows, MODEL_WIDTH))
     arrived = arrived.reshape(-1, MODEL_WIDTH)
 

time: 313 us -> 306 us (0.978)
  Pallas kernels: 105 us -> 94.8 us
    all_gather x1, waiting for transfers between devices: 28.4 us -> 0.01 us  [local(): half_weight = lax.all_gather(weight_rows, CHIPS, axis=0, tiled=True)]
    all_to_all x2, waiting for transfers between devices: 99.7 us -> 128 us  [exchange(): return lax.all_to_all(array, PB_PA, split_axis=0, concat_axis=0, tiled=True)]
    pallas_call x1, Pallas kernels: 33.8 us -> 29.6 us  [tail(): pl.pallas_call(functools.partial(tail_kernel, scale), out_shape=(jax.Shap...]
    pallas_call x1, Pallas kernels: 40.5 us -> 37.4 us  [far_forward(): pl.pallas_call(functools.partial(far_kernel, score_scale), out_shape=(jax...]
    ppermute x1, waiting for transfers between devices: 0.01 us -> 3.16 us  [weight_halves_sent(): first = lax.ppermute(jnp.where(odd, right, left), PB_PA, same)]
  transfers between devices with their start and end apart: 5 -> 5, of which waited for: 3 -> 3; matrix products, arithmetic and copies ran while one was open for 11% -> 11% of each run, Pallas kernels for 23% -> 21%
where the time goes in v8:
time: 306 us; the launch traced here: 305 us
  waiting for transfers between devices  131 us (43%)
  Pallas kernels  94.8 us (31%)
  starting transfers between devices  26.5 us (9%)
  matrix products  24.7 us (8%)
  between operations  14.3 us (5%)
  local copies, waits for them, and re-layouts  7.16 us (2%)
  other arithmetic  6.64 us (2%)
    all_to_all x2, waiting for transfers between devices, exchange(): return lax.all_to_all(array, PB_PA, split_axis=0, concat_axis=0, tiled=True)  128 us
    pallas_call x1, Pallas kernels, far_forward(): pl.pallas_call(functools.partial(far_kernel, score_scale), out_shape=(jax...  37.4 us
    pallas_call x1, Pallas kernels, tail(): pl.pallas_call(functools.partial(tail_kernel, scale), out_shape=(jax.Shap...  29.6 us
    pallas_call x1, Pallas kernels, layer_forward(): pl.pallas_call(layer_forward_kernel, out_shape=(jax.ShapeDtypeStruct((tok...  27.8 us
    all_to_all x2, starting transfers between devices, exchange(): return lax.all_to_all(array, PB_PA, split_axis=0, concat_axis=0, tiled=True)  20.1 us
    dot_general x2, matrix products, dot(): return jnp.dot(a, b, preferred_element_type=f32, **kw)  8.63 us
    dot_general x1, matrix products, local(): lax.dot_general(far_weight, arrived, product_dims, preferred_element_type...  6.63 us
  transfers between devices with their start and end apart: 5, of which 3 were waited for; matrix products, arithmetic and copies ran while one was open for 11% of the time, Pallas kernels for 21%

profile of v8, /device:TPU:1, one launch (start us, length us, event | category | flops | bytes accessed | tf_op | source)
XLA Modules:
  0.0 305.2 jit_solution(15117467289084059208)
XLA Ops:
  7.2 1.0 broadcast_select_fusion.2
  8.3 3.8 %collective-permute-start.1 = (bf16[28,1792]{1,0:T(8,128)(2,1)S(1)}, bf16[28,1792]{1,0:T(8,128)(2,1)S(1)}, u32[]{:S(2)}, u32[]{:S(2)}) collective-permute-start(bf16[28,1792]{1,0:T(8,128)(2,1)S(1)} %get-tuple-element.46), channel_id=1, source_target_pairs={{0,16},{1,0},{2,17},{3,1},{4,18},{5,2},{6,19},{7,3},{8,20},{9,4},{... | collective-permute-start | bytes 301064 | tf_op jit(solution)/shard_map/ppermute | solution.py:50
  12.1 2.5 collective-permute-start
  14.6 0.8 copy.25
  15.5 0.2 convert_reduce_fusion
  15.7 0.1 reduce_sum.23
  16.0 0.1 mul.59
  16.1 3.2 %collective-permute-done = bf16[28,1792]{1,0:T(8,128)(2,1)S(1)} collective-permute-done((bf16[28,1792]{1,0:T(8,128)(2,1)S(1)}, bf16[28,1792]{1,0:T(8,128)(2,1)S(1)}, u32[]{:S(2)}, u32[]{:S(2)}) %collective-permute-start) | collective-permute-done | bytes 100384 | tf_op jit(solution)/shard_map/ppermute | solution.py:49
  19.3 0.7 pad_maximum_fusion
  20.1 5.1 %convolution_bitcast_fusion = bf16[128,8,3584]{2,1,0:T(8,128)(2,1)} fusion(bf16[128,3584]{1,0:T(8,128)(2,1)S(1)} %copy-done, s32[128]{0:T(128)S(1)} %get-tuple-element.51, s32[128]{0:T(128)S(1)} %get-tuple-element.52, s32[128]{0:T(128)S(1)} %get-tuple-element.53, s32[128]{0:T(128)S(1)} %get-tuple-element.50), kind=kOutput, calls=%fused_computation.1 | convolution fusion | flops 940441600 | bytes 8259584 | tf_op jit(solution)/shard_map/dot_general | solution.py:763
  25.2 13.6 %all-to-all-start = ((bf16[128,8,3584]{2,1,0:T(8,128)(2,1)}), bf16[128,8,3584]{2,1,0:T(8,128)(2,1)}, u32[]{:S(2)}, u32[]{:S(2)}) async-start(bf16[128,8,3584]{2,1,0:T(8,128)(2,1)} %convolution_bitcast_fusion), calls=%async_computation | async-start | bytes 14680064 | tf_op jit(solution)/shard_map/all_to_all | solution.py:62
  38.8 3.4 %fusion.26 = (f32[128]{0:T(128)S(1)}, f32[128,512]{1,0:T(8,128)S(1)}) fusion(bf16[128,3584]{1,0:T(8,128)(2,1)S(1)} %copy-done, bf16[512,3584]{1,0:T(8,128)(2,1)} %passages_in.1), kind=kOutput, calls=%fused_computation.58 | convolution fusion | flops 469892992 | bytes 4850176 | tf_op jit(solution)/shard_map/dot_general | solution.py:29
  42.2 0.1 copy.28
  42.3 0.2 fusion.15
  42.5 0.1 copy.27
  42.6 0.6 log_add_fusion.near_mass
  43.2 0.9 copy.29.key_column
  44.1 90.2 %all-to-all-done = bf16[128,8,3584]{2,1,0:T(8,128)(2,1)} async-done(((bf16[128,8,3584]{2,1,0:T(8,128)(2,1)}), bf16[128,8,3584]{2,1,0:T(8,128)(2,1)}, u32[]{:S(2)}, u32[]{:S(2)}) %all-to-all-start) | async-done | bytes 7340064 | tf_op jit(solution)/shard_map/all_to_all | solution.py:62
  134.3 37.4 %far_forward.1 = (bf16[1024,3584]{1,0:T(8,128)(2,1)}, f32[1024,512]{1,0:T(8,128)}, bf16[256,1024]{1,0:T(8,128)(2,1)}, f32[128,1]{1,0:T(8,128)}, f32[1024,1]{1,0:T(8,128)}) custom-call(bf16[1024,3584]{1,0:T(8,128)(2,1)} %bitcast.6.arrived, bf16[512,3584]{1,0:T(8,128)(2,1)} %passages_in.1, f32[128,1]{1,0:T(8,128)} %log_add_fusion.near_mass, ...), custom_call_target="tpu_custom_call" | custom-call | tf_op jit(solution)/shard_map/far_forward/pallas_call | solution.py:411
  171.7 6.6 %all-to-all-start.1 = ((bf16[128,8,3584]{2,1,0:T(8,128)(2,1)}), bf16[128,8,3584]{2,1,0:T(8,128)(2,1)}, u32[]{:S(2)}, u32[]{:S(2)}) async-start(bf16[128,8,3584]{2,1,0:T(8,128)(2,1)} %bitcast.28), calls=%async_computation.1 | async-start | bytes 14680064 | tf_op jit(solution)/shard_map/all_to_all | solution.py:62
  178.3 0.6 reshape.59.norm
  179.0 5.2 %fusion.6 = f32[256,3584]{1,0:T(8,128)} fusion(bf16[512,3584]{1,0:T(8,128)(2,1)} %passages_in.1, bf16[128,512]{1,0:T(8,128)(2,1)S(1)} %fusion.10, bf16[128,512]{1,0:T(8,128)(2,1)S(1)} %get-tuple-element.42), kind=kOutput, calls=%fused_computation.15 | convolution fusion | flops 940048384 | bytes 7602176 | tf_op jit(solution)/shard_map/dot_general | solution.py:29
  184.2 1.2 reduce.1
  185.5 1.0 fusion.24
  186.5 6.6 %fusion = f32[512,3584]{1,0:T(8,128)S(1)} fusion(f32[1024,512]{1,0:T(8,128)S(1)} %copy-done.3, f32[1024]{0:T(1024)S(1)} %reduce.1, bf16[128,8,3584]{2,1,0:T(8,128)(2,1)} %all-to-all-done), kind=kOutput, calls=%fused_computation.6 | convolution fusion | flops 3759144960 | bytes 16781312 | tf_op jit(solution)/shard_map/dot_general | solution.py:792
  193.1 4.3 %add_multiply_fusion = f32[512,3584]{1,0:T(8,128)} fusion(f32[512,3584]{1,0:T(8,128)S(1)} %fusion, bf16[128,3584]{1,0:T(8,128)(2,1)S(1)} %copy-done, f32[128,512]{1,0:T(8,128)S(1)} %get-tuple-element.55, f32[128]{0:T(128)S(1)} %get-tuple-element.40, s32[128]{0:T(128)S(1)} %copy-done.5), kind=kOutput, calls=%fused_computation | convolution fusion | flops 473759744 | bytes 15860736 | tf_op jit(solution)/shard_map/dot_general | solution.py:793
  197.4 1.5 slice_subtract_fusion.near_in
  198.9 27.8 %layer_forward.1 = (bf16[512,3584]{1,0:T(8,128)(2,1)}, f32[512,16]{1,0:T(8,128)}, f32[512,16]{1,0:T(8,128)}, f32[512,1]{1,0:T(8,128)}) custom-call(bf16[512,3584]{1,0:T(8,128)(2,1)} %context.3, bf16[3584,1792]{1,0:T(8,128)(2,1)} %all-gather.2.cloned.1.call-done.half_weight, bf16[512,3584]{1,0:T(8,128)(2,1)} %residual.1, bf16[16,3584]{1,0:T(8,128)(2,1)} %bitcast.29, ...), custom_call_target="tpu_custom_call" | custom-call | flops 1000 | bytes 1000 | tf_op jit(solution)/shard_map/layer_forward/pallas_call | solution.py:163
  226.8 37.9 %all-to-all-done.1 = bf16[128,8,3584]{2,1,0:T(8,128)(2,1)} async-done(((bf16[128,8,3584]{2,1,0:T(8,128)(2,1)}), bf16[128,8,3584]{2,1,0:T(8,128)(2,1)}, u32[]{:S(2)}, u32[]{:S(2)}) %all-to-all-start.1) | async-done | bytes 7340064 | tf_op jit(solution)/shard_map/all_to_all | solution.py:62
  264.6 29.6 %tail.1 = (f32[128,3584]{1,0:T(8,128)}, f32[32,128]{1,0:T(8,128)}) custom-call(bf16[1024,3584]{1,0:T(8,128)(2,1)} %bitcast.11.returned, bf16[256,1024]{1,0:T(8,128)(2,1)} %get-tuple-element.31.mix_in, f32[128,3584]{1,0:T(8,128)} %slice_subtract_fusion.near_in, f32[1,3584]{1,0:T(1,128)} %reshape.59.norm, bf16[512,3584]{1,0:T(8,128)(2,1)} %get-tuple-element.33.hidden, ...), custom_call_target="tpu_custom_call" | custom-call | tf_op jit(solution)/shard_map/tail/pallas_call | solution.py:682
  294.2 1.3 fusion.25
  295.5 2.9 copy.32
  (26 shorter events, 0.5 us)
Async XLA Ops:
  7.2 12.9 %copy-start = (bf16[128,3584]{1,0:T(8,128)(2,1)S(1)}, bf16[128,3584]{1,0:T(8,128)(2,1)}, u32[]{:S(2)}) copy-start(bf16[128,3584]{1,0:T(8,128)(2,1)} %param.10) | copy-start | bytes 2752516
  7.2 191.8 %all-gather.2.cloned.1.call-start = ((), (), s32[]{:S(2)}) async-start(), calls=%async_computation.2 | async-start | bytes 13045760 | tf_op jit(solution)/shard_map/all_gather | solution.py:767
  8.3 7.8 %collective-permute-start.1 = (bf16[28,1792]{1,0:T(8,128)(2,1)S(1)}, bf16[28,1792]{1,0:T(8,128)(2,1)S(1)}, u32[]{:S(2)}, u32[]{:S(2)}) collective-permute-start(bf16[28,1792]{1,0:T(8,128)(2,1)S(1)} %get-tuple-element.46), channel_id=1, source_target_pairs={{0,16},{1,0},{2,17},{3,1},{4,18},{5,2},{6,19},{7,3},{8,20},{9,4},{... | collective-permute-start | bytes 301064 | tf_op jit(solution)/shard_map/ppermute | solution.py:50
  12.1 7.2 %collective-permute-start = (bf16[28,1792]{1,0:T(8,128)(2,1)S(1)}, bf16[28,1792]{1,0:T(8,128)(2,1)S(1)}, u32[]{:S(2)}, u32[]{:S(2)}) collective-permute-start(bf16[28,1792]{1,0:T(8,128)(2,1)S(1)} %get-tuple-element.47), channel_id=1, source_target_pairs={{0,0},{1,16},{2,1},{3,17},{4,2},{5,18},{6,3},{7,19},{8,4},{9,20},{... | collective-permute-start | bytes 301064 | tf_op jit(solution)/shard_map/ppermute | solution.py:49
  25.2 109.1 %all-to-all-start = ((bf16[128,8,3584]{2,1,0:T(8,128)(2,1)}), bf16[128,8,3584]{2,1,0:T(8,128)(2,1)}, u32[]{:S(2)}, u32[]{:S(2)}) async-start(bf16[128,8,3584]{2,1,0:T(8,128)(2,1)} %convolution_bitcast_fusion), calls=%async_computation | async-start | bytes 14680064 | tf_op jit(solution)/shard_map/all_to_all | solution.py:62
  171.7 6.6 %copy-start.4 = (bf16[3584]{0:T(1024)(128)(2,1)S(1)}, bf16[3584]{0:T(1024)(128)(2,1)}, u32[]{:S(2)}) copy-start(bf16[3584]{0:T(1024)(128)(2,1)} %param.19) | copy-start | bytes 21508
  171.7 7.2 %copy-start.5 = (s32[128]{0:T(128)S(1)}, s32[128]{0:T(128)}, u32[]{:S(2)}) copy-start(s32[128]{0:T(128)} %param.13) | copy-start | bytes 1540
  171.7 92.9 %all-to-all-start.1 = ((bf16[128,8,3584]{2,1,0:T(8,128)(2,1)}), bf16[128,8,3584]{2,1,0:T(8,128)(2,1)}, u32[]{:S(2)}, u32[]{:S(2)}) async-start(bf16[128,8,3584]{2,1,0:T(8,128)(2,1)} %bitcast.28), calls=%async_computation.1 | async-start | bytes 14680064 | tf_op jit(solution)/shard_map/all_to_all | solution.py:62
  179.0 7.4 %copy-start.3 = (f32[1024,512]{1,0:T(8,128)S(1)}, f32[1024,512]{1,0:T(8,128)}, u32[]{:S(2)}) copy-start(f32[1024,512]{1,0:T(8,128)} %get-tuple-element.28) | copy-start | bytes 6291460
  193.1 4.3 %copy-start.2 = (f32[256,3584]{1,0:T(8,128)S(1)}, f32[256,3584]{1,0:T(8,128)}, u32[]{:S(2)}) copy-start(f32[256,3584]{1,0:T(8,128)} %fusion.6) | copy-start | bytes 11010052
  264.6 33.8 %copy-start.1 = (bf16[128,3584]{1,0:T(8,128)(2,1)S(1)}, bf16[128,3584]{1,0:T(8,128)(2,1)}, u32[]{:S(2)}) copy-start(bf16[128,3584]{1,0:T(8,128)(2,1)} %param.10) | copy-start | bytes 2752516
Sparse Core Ops, SparseCore 0:
  20.2 161.1 all-gather.1
